TPU v7x, 32 devices: a whole 2x2x4 slice. The times are simulated.
32 devices in a mesh: ctx: 8 (over z, x), fsdp: 4 (over y, core).
Axes of the slice: x: 2, y: 2, z: 4, core: 2. Of those that a mesh axis runs over, the one named last changes fastest.
Arguments:
- tokens: bfloat16 [4, 1024, 2048], P('fsdp', 'ctx'), may hold values from -6 to 6
- ln1_gain: float32 [2048], P(('ctx', 'fsdp')), may hold values from 0.5 to 1.5
- ln1_bias: float32 [2048], P(('ctx', 'fsdp')), may hold values from -3 to 3
- w_qkv: float32 [2048, 6144], P(('ctx', 'fsdp')), may hold values from -0.125 to 0.125
- b_qv: float32 [4096], P(('ctx', 'fsdp')), may hold values from -3 to 3
- w_out: float32 [2048, 2048], P(('ctx', 'fsdp')), may hold values from -0.375 to 0.375
- b_out: float32 [2048], P(('ctx', 'fsdp')), may hold values from -3 to 3
- ln2_gain: float32 [2048], P(('ctx', 'fsdp')), may hold values from 0.5 to 1.5
- ln2_bias: float32 [2048], P(('ctx', 'fsdp')), may hold values from -3 to 3
- w_in: float32 [2048, 8192], P(('ctx', 'fsdp')), may hold values from -0.125 to 0.125
- b_in: float32 [8192], P(('ctx', 'fsdp')), may hold values from -3 to 3
- w_down: float32 [8192, 2048], P(('ctx', 'fsdp')), may hold values from -0.09375 to 0.09375
- b_down: float32 [2048], P(('ctx', 'fsdp')), may hold values from -3 to 3
- cotangent: bfloat16 [4, 1024, 2048], P('fsdp', 'ctx'), may hold values from -6 to 6
- block_seg: int32 [4, 8], P('fsdp'), may hold values from 0 to 1, as said below
- block_pos: int32 [4, 8], P('fsdp'), may hold values from 0 to 896, as said below
Outputs:
- output: bfloat16 [4, 1024, 2048], P('fsdp', 'ctx')
- grad_tokens: float32 [4, 1024, 2048], P('fsdp', 'ctx')
- grad_ln1_gain: float32 [2048], P(('ctx', 'fsdp'))
- grad_ln1_bias: float32 [2048], P(('ctx', 'fsdp'))
- grad_w_qkv: float32 [2048, 6144], P(('ctx', 'fsdp'))
- grad_b_qv: float32 [4096], P(('ctx', 'fsdp'))
- grad_w_out: float32 [2048, 2048], P(('ctx', 'fsdp'))
- grad_b_out: float32 [2048], P(('ctx', 'fsdp'))
- grad_ln2_gain: float32 [2048], P(('ctx', 'fsdp'))
- grad_ln2_bias: float32 [2048], P(('ctx', 'fsdp'))
- grad_w_in: float32 [2048, 8192], P(('ctx', 'fsdp'))
- grad_b_in: float32 [8192], P(('ctx', 'fsdp'))
- grad_w_down: float32 [8192, 2048], P(('ctx', 'fsdp'))
- grad_b_down: float32 [2048], P(('ctx', 'fsdp'))
Inputs may be any that keep to these rules, and one draw needn't show every extreme that they name: `block_seg`: in each group the stored blocks are the prompt's 512 // 128 blocks (segment 0, offsets 0, 128, 256, ...) and, for each continuation s, its 4 blocks (segment s, offsets 512, 640, ...), each once, in an order that varies; the first stored block is the prompt's first one and the last stored block is the prompt's last one. `block_pos`: offsets that go with block_seg as described there.
All inputs are finite; a program needn't handle non-finite values.
Results may differ from a plain program's by a relative error of at most 0.019.
Values may be sent and summed in bfloat16 or wider, within the bound.
No kernel may reach another device: no remote copies, remote signals or barrier semaphores. Data moves between devices by JAX's collectives and lax.ppermute only.
A program may use at most 384 MiB of HBM per device.

v0:
```python
import math

import jax
import jax.numpy as jnp
from jax import lax
from jax.sharding import PartitionSpec as P

D = 2048
H = 16
HD = 128
BLK = 128


EPSILON = 1e-05
NEG_FILL = -1e30


def norm_rows(values, norm_gain, norm_bias):
    center = values - jnp.mean(values, axis=-1, keepdims=True)
    spread = jnp.mean(center * center, axis=-1, keepdims=True)
    return center * lax.rsqrt(spread + EPSILON) * norm_gain + norm_bias


def to_half(values):
    return values.astype(jnp.bfloat16)


def to_full(values):
    return values.astype(jnp.float32)


def contract_rows(left_rows, right_rows):
    return lax.dot_general(
        left_rows, right_rows, (((0,), (0,)), ((), ())), preferred_element_type=jnp.float32
    )


def visibility(query_seg, query_pos, key_seg, key_pos):
    return ((key_seg[None, :] == 0) | (key_seg[None, :] == query_seg[:, None])) & (
        key_pos[None, :] <= query_pos[:, None]
    )


def score_values(query_rows, key_rows, query_pos, key_pos, slopes):
    raw_dot = jnp.einsum("qhd,khd->hqk", query_rows, key_rows, preferred_element_type=jnp.float32)
    distance = (query_pos[:, None] - key_pos[None, :]).astype(jnp.float32)
    return (
        raw_dot * (1.0 / math.sqrt(query_rows.shape[-1])) - slopes[:, None, None] * distance[None]
    )


def over_blocks(carried, row_total, step_rows, visit):

    def advance(partial_value, turn_index):
        return (visit(partial_value, turn_index * step_rows), None)

    finished, unused = lax.scan(
        advance, carried, jnp.arange(row_total // step_rows, dtype=jnp.int32)
    )
    return finished


def on_device(
    tokens,
    ln1_gain,
    ln1_bias,
    w_qkv,
    b_qv,
    w_out,
    b_out,
    ln2_gain,
    ln2_bias,
    w_in,
    b_in,
    w_down,
    b_down,
    cotangent,
    block_seg,
    block_pos,
):
    local_rows = tokens.shape[1]
    own_start = lax.axis_index("ctx") * local_rows
    offsets = jnp.arange(BLK, dtype=jnp.int32)
    seg_all = jnp.repeat(block_seg[0], BLK)
    pos_all = (block_pos[0][:, None] + offsets[None, :]).reshape(-1)
    own_seg = lax.dynamic_slice_in_dim(seg_all, own_start, local_rows)
    own_pos = lax.dynamic_slice_in_dim(pos_all, own_start, local_rows)
    slopes = jnp.exp2(-8.0 * (jnp.arange(H, dtype=jnp.float32) + 1.0) / H)
    scale_qk = 1.0 / math.sqrt(HD)
    attn_full = (
        lax.all_gather(to_half(ln1_gain), ("ctx", "fsdp"), axis=0, tiled=True),
        lax.all_gather(to_half(ln1_bias), ("ctx", "fsdp"), axis=0, tiled=True),
        lax.all_gather(to_half(w_qkv), ("ctx", "fsdp"), axis=0, tiled=True),
        lax.all_gather(to_half(b_qv), ("ctx", "fsdp"), axis=0, tiled=True),
        lax.all_gather(to_half(w_out), ("ctx", "fsdp"), axis=0, tiled=True),
        lax.all_gather(to_half(b_out), ("ctx", "fsdp"), axis=0, tiled=True),
    )
    gain_first, bias_first, qkv_matrix, qkv_bias, out_matrix, out_bias = attn_full
    input_rows = to_full(tokens[0])
    normed_half = to_half(norm_rows(input_rows, to_full(gain_first), to_full(bias_first)))
    mixed_rows = jnp.dot(normed_half, qkv_matrix, preferred_element_type=jnp.float32)
    bias_full = to_full(qkv_bias)
    query_half = to_half(mixed_rows[:, :D] + bias_full[:D])
    key_half = to_half(mixed_rows[:, D : 2 * D])
    value_half = to_half(mixed_rows[:, 2 * D :] + bias_full[D:])
    query_heads = query_half.reshape(local_rows, H, HD)
    key_heads = key_half.reshape(local_rows, H, HD)
    value_heads = value_half.reshape(local_rows, H, HD)
    start_state = (
        jnp.full((H, local_rows), NEG_FILL, jnp.float32),
        jnp.zeros((H, local_rows), jnp.float32),
        jnp.zeros((local_rows, H, HD), jnp.float32),
    )
    key_portion = lax.all_gather(key_half, "ctx", axis=0, tiled=True)
    value_portion = lax.all_gather(value_half, "ctx", axis=0, tiled=True)
    row_count = key_portion.shape[0]
    step_rows = math.gcd(row_count, 256)

    def visit(partial_value, row_begin):
        key_rows = lax.dynamic_slice_in_dim(key_portion, row_begin, step_rows).reshape(
            step_rows, H, HD
        )
        value_rows = lax.dynamic_slice_in_dim(value_portion, row_begin, step_rows).reshape(
            step_rows, H, HD
        )
        key_seg = lax.dynamic_slice_in_dim(seg_all, row_begin, step_rows)
        key_pos = lax.dynamic_slice_in_dim(pos_all, row_begin, step_rows)
        visible = visibility(own_seg, own_pos, key_seg, key_pos)

        def compute(inner_state):
            running_max, running_sum, running_acc = inner_state
            scores = jnp.where(
                visible[None],
                score_values(query_heads, key_rows, own_pos, key_pos, slopes),
                NEG_FILL,
            )
            new_max = jnp.maximum(running_max, jnp.max(scores, axis=-1))
            factor = jnp.exp(running_max - new_max)
            expon_rows = jnp.where(visible[None], jnp.exp(scores - new_max[..., None]), 0.0)
            running_sum = running_sum * factor + jnp.sum(expon_rows, axis=-1)
            running_acc = running_acc * factor.T[:, :, None] + jnp.einsum(
                "hqk,khd->qhd", to_half(expon_rows), value_rows, preferred_element_type=jnp.float32
            )
            return (new_max, running_sum, running_acc)

        return compute(partial_value)

    max_rows, sum_rows, acc_rows = over_blocks(start_state, row_count, step_rows, visit)
    attn_rows = acc_rows / sum_rows.T[:, :, None]
    lse_rows = max_rows + jnp.log(sum_rows)
    attn_half = to_half(attn_rows.reshape(local_rows, D))
    residual = (
        input_rows
        + jnp.dot(attn_half, out_matrix, preferred_element_type=jnp.float32)
        + to_full(out_bias)
    )
    ffn_full = (
        lax.all_gather(to_half(ln2_gain), ("ctx", "fsdp"), axis=0, tiled=True),
        lax.all_gather(to_half(ln2_bias), ("ctx", "fsdp"), axis=0, tiled=True),
        lax.all_gather(to_half(w_in), ("ctx", "fsdp"), axis=0, tiled=True),
        lax.all_gather(to_half(b_in), ("ctx", "fsdp"), axis=0, tiled=True),
        lax.all_gather(to_half(w_down), ("ctx", "fsdp"), axis=0, tiled=True),
        lax.all_gather(to_half(b_down), ("ctx", "fsdp"), axis=0, tiled=True),
    )
    gain_second, bias_second, in_matrix, in_bias, down_matrix, down_bias = ffn_full
    second_half = to_half(norm_rows(residual, to_full(gain_second), to_full(bias_second)))
    pre_act = jnp.dot(second_half, in_matrix, preferred_element_type=jnp.float32) + to_full(in_bias)
    act_half = to_half(jax.nn.gelu(pre_act, approximate=True))
    result = (
        residual
        + jnp.dot(act_half, down_matrix, preferred_element_type=jnp.float32)
        + to_full(down_bias)
    )
    output = to_half(result)[None]
    cot_half = cotangent[0]
    cot_rows = to_full(cot_half)
    grad_w_down = contract_rows(act_half, cot_half)
    grad_b_down = jnp.sum(cot_rows, axis=0)
    held_params = lax.optimization_barrier(
        (ln2_gain, ln2_bias, w_in, b_in, w_down, b_down, cot_rows)
    )
    ffn_again = (
        lax.all_gather(to_half(held_params[0]), ("ctx", "fsdp"), axis=0, tiled=True),
        lax.all_gather(to_half(held_params[1]), ("ctx", "fsdp"), axis=0, tiled=True),
        lax.all_gather(to_half(held_params[2]), ("ctx", "fsdp"), axis=0, tiled=True),
        lax.all_gather(to_half(held_params[3]), ("ctx", "fsdp"), axis=0, tiled=True),
        lax.all_gather(to_half(held_params[4]), ("ctx", "fsdp"), axis=0, tiled=True),
        lax.all_gather(to_half(held_params[5]), ("ctx", "fsdp"), axis=0, tiled=True),
    )
    gain_second, bias_second, in_matrix, in_bias, down_matrix, down_bias = ffn_again
    d_act = jnp.dot(cot_half, down_matrix.T, preferred_element_type=jnp.float32)
    unused_act, gelu_back = jax.vjp(lambda values: jax.nn.gelu(values, approximate=True), pre_act)
    d_pre_half = to_half(gelu_back(d_act)[0])
    grad_w_in = contract_rows(second_half, d_pre_half)
    grad_b_in = jnp.sum(to_full(d_pre_half), axis=0)
    d_second = jnp.dot(d_pre_half, in_matrix.T, preferred_element_type=jnp.float32)
    unused_second, second_back = jax.vjp(
        norm_rows, residual, to_full(gain_second), to_full(bias_second)
    )
    d_residual_norm, grad_ln2_gain, grad_ln2_bias = second_back(d_second)
    d_residual = cot_rows + d_residual_norm
    ffn_grads = (
        lax.psum_scatter(grad_ln2_gain, ("ctx", "fsdp"), scatter_dimension=0, tiled=True),
        lax.psum_scatter(grad_ln2_bias, ("ctx", "fsdp"), scatter_dimension=0, tiled=True),
        lax.psum_scatter(grad_w_in, ("ctx", "fsdp"), scatter_dimension=0, tiled=True),
        lax.psum_scatter(grad_b_in, ("ctx", "fsdp"), scatter_dimension=0, tiled=True),
        lax.psum_scatter(grad_w_down, ("ctx", "fsdp"), scatter_dimension=0, tiled=True),
        lax.psum_scatter(grad_b_down, ("ctx", "fsdp"), scatter_dimension=0, tiled=True),
    )
    held_attn = lax.optimization_barrier(
        (ln1_gain, ln1_bias, w_qkv, b_qv, w_out, b_out, d_residual)
    )
    attn_again = (
        lax.all_gather(to_half(held_attn[0]), ("ctx", "fsdp"), axis=0, tiled=True),
        lax.all_gather(to_half(held_attn[1]), ("ctx", "fsdp"), axis=0, tiled=True),
        lax.all_gather(to_half(held_attn[2]), ("ctx", "fsdp"), axis=0, tiled=True),
        lax.all_gather(to_half(held_attn[3]), ("ctx", "fsdp"), axis=0, tiled=True),
        lax.all_gather(to_half(held_attn[4]), ("ctx", "fsdp"), axis=0, tiled=True),
        lax.all_gather(to_half(held_attn[5]), ("ctx", "fsdp"), axis=0, tiled=True),
    )
    gain_first, bias_first, qkv_matrix, qkv_bias, out_matrix, out_bias = attn_again
    d_branch_half = to_half(d_residual)
    grad_w_out = contract_rows(attn_half, d_branch_half)
    grad_b_out = jnp.sum(to_full(d_branch_half), axis=0)
    d_attn_half = to_half(jnp.dot(d_branch_half, out_matrix.T, preferred_element_type=jnp.float32))
    d_attn_heads = d_attn_half.reshape(local_rows, H, HD)
    delta_rows = jnp.sum(to_full(d_attn_heads) * attn_rows, axis=-1).T
    lse_all, delta_all = (
        lax.all_gather(lse_rows, "ctx", axis=1, tiled=True),
        lax.all_gather(delta_rows, "ctx", axis=1, tiled=True),
    )
    query_key_portion = lax.all_gather(key_half, "ctx", axis=0, tiled=True)
    query_value_portion = lax.all_gather(value_half, "ctx", axis=0, tiled=True)
    row_count = query_key_portion.shape[0]
    query_step_rows = math.gcd(row_count, 256)

    def visit(partial_value, row_begin):
        key_rows = lax.dynamic_slice_in_dim(query_key_portion, row_begin, query_step_rows).reshape(
            query_step_rows, H, HD
        )
        value_rows = lax.dynamic_slice_in_dim(
            query_value_portion, row_begin, query_step_rows
        ).reshape(query_step_rows, H, HD)
        key_seg = lax.dynamic_slice_in_dim(seg_all, row_begin, query_step_rows)
        key_pos = lax.dynamic_slice_in_dim(pos_all, row_begin, query_step_rows)
        visible = visibility(own_seg, own_pos, key_seg, key_pos)

        def compute(inner_acc):
            scores = score_values(query_heads, key_rows, own_pos, key_pos, slopes)
            probs_soft = jnp.where(visible[None], jnp.exp(scores - lse_rows[..., None]), 0.0)
            d_prob = jnp.einsum(
                "qhd,khd->hqk", d_attn_heads, value_rows, preferred_element_type=jnp.float32
            )
            d_score = to_half(probs_soft * (d_prob - delta_rows[..., None]))
            return inner_acc + jnp.einsum(
                "hqk,khd->qhd", d_score, key_rows, preferred_element_type=jnp.float32
            )

        return compute(partial_value)

    d_query = over_blocks(
        jnp.zeros((local_rows, H, HD), jnp.float32), row_count, query_step_rows, visit
    )
    zero_heads = jnp.zeros((local_rows, H, HD), jnp.float32)
    query_portion_rows = lax.all_gather(query_half, "ctx", axis=0, tiled=True)
    grad_portion = lax.all_gather(d_attn_half, "ctx", axis=0, tiled=True)
    row_count = query_portion_rows.shape[0]
    key_step_rows = math.gcd(row_count, 256)

    def visit(partial_value, row_begin):
        query_rows = lax.dynamic_slice_in_dim(query_portion_rows, row_begin, key_step_rows).reshape(
            key_step_rows, H, HD
        )
        grad_rows = lax.dynamic_slice_in_dim(grad_portion, row_begin, key_step_rows).reshape(
            key_step_rows, H, HD
        )
        query_seg = lax.dynamic_slice_in_dim(seg_all, row_begin, key_step_rows)
        query_pos = lax.dynamic_slice_in_dim(pos_all, row_begin, key_step_rows)
        lse_block = lax.dynamic_slice_in_dim(lse_all, row_begin, key_step_rows, axis=1)
        delta_block = lax.dynamic_slice_in_dim(delta_all, row_begin, key_step_rows, axis=1)
        visible = visibility(query_seg, query_pos, own_seg, own_pos)

        def compute(inner_state):
            key_acc, value_acc = inner_state
            scores = score_values(query_rows, key_heads, query_pos, own_pos, slopes)
            probs_soft = jnp.where(visible[None], jnp.exp(scores - lse_block[..., None]), 0.0)
            value_acc = value_acc + jnp.einsum(
                "hqk,qhd->khd", to_half(probs_soft), grad_rows, preferred_element_type=jnp.float32
            )
            d_prob = jnp.einsum(
                "qhd,khd->hqk", grad_rows, value_heads, preferred_element_type=jnp.float32
            )
            d_score = to_half(probs_soft * (d_prob - delta_block[..., None]))
            key_acc = key_acc + jnp.einsum(
                "hqk,qhd->khd", d_score, query_rows, preferred_element_type=jnp.float32
            )
            return (key_acc, value_acc)

        return compute(partial_value)

    d_key, d_value = over_blocks((zero_heads, zero_heads), row_count, key_step_rows, visit)
    d_query_half = to_half((d_query * scale_qk).reshape(local_rows, D))
    d_key_half = to_half((d_key * scale_qk).reshape(local_rows, D))
    d_value_half = to_half(d_value.reshape(local_rows, D))
    d_mixed = jnp.concatenate([d_query_half, d_key_half, d_value_half], axis=1)
    grad_w_qkv = contract_rows(normed_half, d_mixed)
    grad_b_qv = jnp.concatenate(
        [jnp.sum(to_full(d_query_half), axis=0), jnp.sum(to_full(d_value_half), axis=0)]
    )
    d_normed = jnp.dot(d_mixed, qkv_matrix.T, preferred_element_type=jnp.float32)
    unused_first, first_back = jax.vjp(
        norm_rows, input_rows, to_full(gain_first), to_full(bias_first)
    )
    d_input_norm, grad_ln1_gain, grad_ln1_bias = first_back(d_normed)
    grad_input = d_residual + d_input_norm
    attn_grads = (
        lax.psum_scatter(grad_ln1_gain, ("ctx", "fsdp"), scatter_dimension=0, tiled=True),
        lax.psum_scatter(grad_ln1_bias, ("ctx", "fsdp"), scatter_dimension=0, tiled=True),
        lax.psum_scatter(grad_w_qkv, ("ctx", "fsdp"), scatter_dimension=0, tiled=True),
        lax.psum_scatter(grad_b_qv, ("ctx", "fsdp"), scatter_dimension=0, tiled=True),
        lax.psum_scatter(grad_w_out, ("ctx", "fsdp"), scatter_dimension=0, tiled=True),
        lax.psum_scatter(grad_b_out, ("ctx", "fsdp"), scatter_dimension=0, tiled=True),
    )
    return (
        output,
        grad_input[None],
        attn_grads[0],
        attn_grads[1],
        attn_grads[2],
        attn_grads[3],
        attn_grads[4],
        attn_grads[5],
        ffn_grads[0],
        ffn_grads[1],
        ffn_grads[2],
        ffn_grads[3],
        ffn_grads[4],
        ffn_grads[5],
    )


def solution(mesh):
    return jax.shard_map(
        on_device,
        mesh=mesh,
        in_specs=(
            P("fsdp", "ctx", None),
            P(("ctx", "fsdp")),
            P(("ctx", "fsdp")),
            P(("ctx", "fsdp"), None),
            P(("ctx", "fsdp")),
            P(("ctx", "fsdp"), None),
            P(("ctx", "fsdp")),
            P(("ctx", "fsdp")),
            P(("ctx", "fsdp")),
            P(("ctx", "fsdp"), None),
            P(("ctx", "fsdp")),
            P(("ctx", "fsdp"), None),
            P(("ctx", "fsdp")),
            P("fsdp", "ctx", None),
            P("fsdp", None),
            P("fsdp", None),
        ),
        out_specs=(
            P("fsdp", "ctx", None),
            P("fsdp", "ctx", None),
            P(("ctx", "fsdp")),
            P(("ctx", "fsdp")),
            P(("ctx", "fsdp"), None),
            P(("ctx", "fsdp")),
            P(("ctx", "fsdp"), None),
            P(("ctx", "fsdp")),
            P(("ctx", "fsdp")),
            P(("ctx", "fsdp")),
            P(("ctx", "fsdp"), None),
            P(("ctx", "fsdp")),
            P(("ctx", "fsdp"), None),
            P(("ctx", "fsdp")),
        ),
        check_vma=False,
    )
```

profile of v0, /device:TPU:8, one launch (start us, length us, event | category | flops | bytes accessed | tf_op | source)
XLA Modules:
  0.0 3776.2 jit_solution(13469337834883190823)
XLA Ops:
  15.0 41.9 %all-reduce.18 = (bf16[2048]{0:T(1024)(128)(2,1)S(1)}, bf16[2048]{0:T(1024)(128)(2,1)S(1)}, bf16[2048]{0:T(1024)(128)(2,1)S(1)}, bf16[2048]{0:T(1024)(128)(2,1)S...) all-reduce(bf16[2048]{0:T(1024)(128)(2,1)S(1)} %dynamic-update-slic, ...), channel_id=1, replica_groups=mesh['ctx'=8,'fsdp'=4] {'ctx','fsdp'}, use_global_device_ids=true, to_apply=%add.1 | all-reduce | flops 12288 | bytes 49152
  59.5 107.4 %all-gather.15.cloned.1.call-done = bf16[2048,6144]{1,0:T(8,128)(2,1)} async-done(((bf16[64,6144]{1,0:T(8,128)(2,1)}), bf16[2048,6144]{1,0:T(8,128)(2,1)}) %all-gather.15.cloned.1.call-update) | async-done | bytes 25165840 | tf_op jit(solution)/shard_map/all_gather | solution.py:93
  179.6 34.1 all-gather
  222.9 37.1 all-gather.1
  267.6 59.5 %all-gather.19.cloned.1.call-done = bf16[1024,2048]{1,0:T(8,128)(2,1)} async-done(((bf16[128,2048]{1,0:T(8,128)(2,1)}), bf16[1024,2048]{1,0:T(8,128)(2,1)}) %all-gather.19.cloned.1.call-update) | async-done | bytes 4194320 | tf_op jit(solution)/shard_map/all_gather | solution.py:115
  333.5 28.5 while.39
  363.3 43.6 %all-gather.21.cloned.1.call-done = bf16[2048,2048]{1,0:T(8,128)(2,1)} async-done(((bf16[64,2048]{1,0:T(8,128)(2,1)}), bf16[2048,2048]{1,0:T(8,128)(2,1)}) %all-gather.21.cloned.1.call-update) | async-done | bytes 8388624 | tf_op jit(solution)/shard_map/all_gather | solution.py:95
  412.0 189.7 %all-gather.23.cloned.1.call-done = bf16[2048,8192]{1,0:T(8,128)(2,1)} async-done(((bf16[64,8192]{1,0:T(8,128)(2,1)}), bf16[2048,8192]{1,0:T(8,128)(2,1)}) %all-gather.23.cloned.1.call-update) | async-done | bytes 33554448 | tf_op jit(solution)/shard_map/all_gather | solution.py:160
  618.9 179.1 %all-gather.27.cloned.1.call-done = bf16[8192,2048]{1,0:T(8,128)(2,1)} async-done(((bf16[256,2048]{1,0:T(8,128)(2,1)}), bf16[8192,2048]{1,0:T(8,128)(2,1)}) %all-gather.27.cloned.1.call-update) | async-done | bytes 33554448 | tf_op jit(solution)/shard_map/all_gather | solution.py:187
  818.2 175.6 %all-gather.29.cloned.1.call-done = bf16[2048,8192]{1,0:T(8,128)(2,1)} async-done(((bf16[64,8192]{1,0:T(8,128)(2,1)}), bf16[2048,8192]{1,0:T(8,128)(2,1)}) %all-gather.29.cloned.1.call-update) | async-done | bytes 33554448 | tf_op jit(solution)/shard_map/all_gather | solution.py:185
  1016.9 77.0 %all-gather.31.cloned.1.call-done = bf16[2048,2048]{1,0:T(8,128)(2,1)} async-done(((bf16[64,2048]{1,0:T(8,128)(2,1)}), bf16[2048,2048]{1,0:T(8,128)(2,1)}) %all-gather.31.cloned.1.call-update) | async-done | bytes 8388624 | tf_op jit(solution)/shard_map/all_gather | solution.py:218
  1109.4 28.0 all_gather.93
  1137.6 42.5 %all-reduce.17 = (bf16[2048]{0:T(1024)(128)(2,1)}, bf16[2048]{0:T(1024)(128)(2,1)S(1)}) all-reduce(bf16[2048]{0:T(1024)(128)(2,1)S(1)} %dynamic-update-slice.5, bf16[2048]{0:T(1024)(128)(2,1)S(1)} %dynamic-update-slice.7), channel_id=1, replica_groups=mesh['ctx'=8,'fsdp'=4] {'ctx','fsdp'}, use_global_device_ids=true, to_apply=%add.5 | all-reduce | flops 4096 | bytes 16384
  1182.1 28.9 all_gather.95
  1212.0 35.5 while.40
  1249.8 58.7 %while.41 = (s32[]{:T(128)}, f32[128,16,128]{0,2,1:T(8,128)}, f32[128,16,128]{0,2,1:T(8,128)}, s32[4]{0:T(128)S(1)}, bf16[1024,2048]{1,0:T(8,128)(2,1)}, /*index...) while((s32[]{:T(128)}, f32[128,16,128]{0,2,1:T(8,128)}, ...), condition=%wide.region_14.15_spmd.clone, body=%wide.region_13.14_spmd.clone.sunk | while | flops 542834816 | bytes 28747420 | solution.py:57
  1312.0 90.8 %all-gather.37.cloned.1.call-done = bf16[2048,6144]{1,0:T(8,128)(2,1)} async-done(((bf16[64,6144]{1,0:T(8,128)(2,1)}), bf16[2048,6144]{1,0:T(8,128)(2,1)}) %all-gather.37.cloned.1.call-update) | async-done | bytes 25165840 | tf_op jit(solution)/shard_map/all_gather | solution.py:216
  1478.4 29.0 fusion.66
  1508.1 90.5 %all-gather.25.cloned.1.call-done = bf16[8192,2048]{1,0:T(8,128)(2,1)} async-done(((bf16[256,2048]{1,0:T(8,128)(2,1)}), bf16[8192,2048]{1,0:T(8,128)(2,1)}) %all-gather.25.cloned.1.call-update) | async-done | bytes 33554448 | tf_op jit(solution)/shard_map/all_gather | solution.py:162
  1617.7 113.0 %all-reduce.21.cloned.1.call-done = (f32[2048]{0:T(1024)}, f32[2048]{0:T(1024)}, f32[4096]{0:T(1024)}, f32[2048]{0:T(1024)}, f32[2048]{0:T(1024)}, /*index=5*/f32[2048]{0:T(1024)}, f32[8192]{0:T(1024)}, f32[2048]{0:T(1024)}) async-done(((f32[2048]{0:T(1024)}, f32[2048]{0:T(1024)}, f32[4096]{0:T(1024)}, f32[2048]{0:T(1024)}, f32[2048]{0:T(1024)}, /*index=5*/f32[2048]{0:T(1024)}, f32[8192]{0:T(1024)}, ...) | async-done | bytes 98320
  1740.8 174.8 %reduce-scatter.7.cloned.1.call-done = f32[64,2048]{1,0:T(8,128)} async-done(((f32[2048,2048]{1,0:T(8,128)}), f32[64,2048]{1,0:T(8,128)}) %reduce-scatter.7.cloned.1.call-update) | async-done | bytes 524304 | tf_op jit(solution)/shard_map/reduce_scatter | solution.py:321
  1915.7 439.8 %reduce-scatter.5.cloned.1.call-done = f32[64,6144]{1,0:T(8,128)} async-done(((f32[2048,6144]{1,0:T(8,128)}), f32[64,6144]{1,0:T(8,128)}) %reduce-scatter.5.cloned.1.call-update) | async-done | bytes 1572880 | tf_op jit(solution)/shard_map/reduce_scatter | solution.py:319
  2355.4 705.0 %reduce-scatter.9.cloned.1.call-done = f32[64,8192]{1,0:T(8,128)} async-done(((f32[2048,8192]{1,0:T(8,128)}), f32[64,8192]{1,0:T(8,128)}) %reduce-scatter.9.cloned.1.call-update) | async-done | bytes 2097168 | tf_op jit(solution)/shard_map/reduce_scatter | solution.py:205
  3060.5 708.8 %reduce-scatter.11.cloned.1.call-done = f32[256,2048]{1,0:T(8,128)} async-done(((f32[8192,2048]{1,0:T(8,128)}), f32[256,2048]{1,0:T(8,128)}) %reduce-scatter.11.cloned.1.call-update) | async-done | bytes 2097168 | tf_op jit(solution)/shard_map/reduce_scatter | solution.py:207
  (397 shorter events, 356.5 us)
Async XLA Ops:
  7.2 159.7 %copy-start.4 = (bf16[1,128,2048]{2,1,0:T(8,128)(2,1)S(1)}, bf16[1,128,2048]{2,1,0:T(8,128)(2,1)}, u32[]{:S(2)}) copy-start(bf16[1,128,2048]{2,1,0:T(8,128)(2,1)} %param.22) | copy-start | bytes 1572868
  7.2 159.7 %all-gather.15.cloned.1.call-start = ((), (), s32[]{:S(2)}) async-start(), calls=%async_computation.4 | async-start | bytes 25952256 | tf_op jit(solution)/shard_map/all_gather | solution.py:93
  9.7 251.4 %all-gather.17.cloned.1.call-start = ((), (), s32[]{:S(2)}) async-start(), calls=%async_computation.5 | async-start | bytes 4718592 | tf_op jit(solution)/shard_map/all_gather | solution.py:114
  59.5 120.1 %copy-start.41 = (f32[128]{0:T(128)S(1)}, f32[128]{0:T(128)}, u32[]{:S(2)}) copy-start(f32[128]{0:T(128)} %param.26) | copy-start | bytes 1540
  179.6 147.5 %all-gather.19.cloned.1.call-start = ((), (), s32[]{:S(2)}) async-start(), calls=%async_computation.6 | async-start | bytes 4718592 | tf_op jit(solution)/shard_map/all_gather | solution.py:115
  216.5 190.4 %all-gather.21.cloned.1.call-start = ((), (), s32[]{:S(2)}) async-start(), calls=%async_computation.7 | async-start | bytes 8650752 | tf_op jit(solution)/shard_map/all_gather | solution.py:95
  217.3 384.4 %all-gather.23.cloned.1.call-start = ((), (), s32[]{:S(2)}) async-start(), calls=%async_computation.8 | async-start | bytes 34603008 | tf_op jit(solution)/shard_map/all_gather | solution.py:160
  218.5 579.5 %all-gather.27.cloned.1.call-start = ((), (), s32[]{:S(2)}) async-start(), calls=%async_computation.10 | async-start | bytes 34603008 | tf_op jit(solution)/shard_map/all_gather | solution.py:187
  221.4 772.5 %all-gather.29.cloned.1.call-start = ((), (), s32[]{:S(2)}) async-start(), calls=%async_computation.11 | async-start | bytes 34603008 | tf_op jit(solution)/shard_map/all_gather | solution.py:185
  222.5 871.3 %all-gather.31.cloned.1.call-start = ((), (), s32[]{:S(2)}) async-start(), calls=%async_computation.12 | async-start | bytes 8650752 | tf_op jit(solution)/shard_map/all_gather | solution.py:218
  260.1 341.7 %copy-start.27 = (f32[2048]{0:T(1024)}, f32[2048]{0:T(1024)S(1)}, u32[]{:S(2)}) copy-start(f32[2048]{0:T(1024)S(1)} %convert_element_type.217) | copy-start | bytes 24580
  260.1 341.6 %copy-start.29 = (f32[2048]{0:T(1024)}, f32[2048]{0:T(1024)S(1)}, u32[]{:S(2)}) copy-start(f32[2048]{0:T(1024)S(1)} %convert_element_type.215) | copy-start | bytes 24580
  411.7 600.0 %copy-start.2 = (f32[128,2048]{1,0:T(8,128)}, f32[128,2048]{1,0:T(8,128)S(1)}, u32[]{:S(2)}) copy-start(f32[128,2048]{1,0:T(8,128)S(1)} %get-tuple-element.670) | copy-start | bytes 3145732
  818.2 193.5 %copy-start.11 = (bf16[128,8192]{1,0:T(8,128)(2,1)}, bf16[128,8192]{1,0:T(8,128)(2,1)S(1)}, u32[]{:S(2)}) copy-start(bf16[128,8192]{1,0:T(8,128)(2,1)S(1)} %get-tuple-element.674) | copy-start | bytes 6291460
  1016.1 233.7 %all-gather.33.cloned.1.call-start = ((), (), s32[]{:S(2)}) async-start(), calls=%async_computation.13 | async-start | bytes 4718592 | tf_op jit(solution)/shard_map/all_gather | solution.py:265
  1016.8 232.9 %all-gather.35.cloned.1.call-start = ((), (), s32[]{:S(2)}) async-start(), calls=%async_computation.14 | async-start | bytes 4718592 | tf_op jit(solution)/shard_map/all_gather | solution.py:266
  1101.0 301.9 %all-gather.37.cloned.1.call-start = ((), (), s32[]{:S(2)}) async-start(), calls=%async_computation.15 | async-start | bytes 25952256 | tf_op jit(solution)/shard_map/all_gather | solution.py:216
  1103.7 494.9 %all-gather.25.cloned.1.call-start = ((), (), s32[]{:S(2)}) async-start(), calls=%async_computation.9 | async-start | bytes 34603008 | tf_op jit(solution)/shard_map/all_gather | solution.py:162
  1104.9 625.9 %all-reduce.21.cloned.1.call-start = ((), (), s32[]{:S(2)}) async-start(), calls=%async_computation.20 | async-start | bytes 196608
  1249.8 153.1 %copy-start.32 = (f32[128]{0:T(128)S(1)}, f32[128]{0:T(128)}, u32[]{:S(2)}) copy-start(f32[128]{0:T(128)} %copy-done.31) | copy-start | bytes 1540
  1420.1 495.5 %reduce-scatter.7.cloned.1.call-start = ((), (), s32[]{:S(2)}) async-start(), calls=%async_computation.17 | async-start | bytes 17301504 | tf_op jit(solution)/shard_map/reduce_scatter | solution.py:321
  1428.6 926.9 %reduce-scatter.5.cloned.1.call-start = ((), (), s32[]{:S(2)}) async-start(), calls=%async_computation.16 | async-start | bytes 51904512 | tf_op jit(solution)/shard_map/reduce_scatter | solution.py:319
  1451.3 1609.2 %reduce-scatter.9.cloned.1.call-start = ((), (), s32[]{:S(2)}) async-start(), calls=%async_computation.18 | async-start | bytes 69206016 | tf_op jit(solution)/shard_map/reduce_scatter | solution.py:205
  1477.4 2291.8 %reduce-scatter.11.cloned.1.call-start = ((), (), s32[]{:S(2)}) async-start(), calls=%async_computation.19 | async-start | bytes 69206016 | tf_op jit(solution)/shard_map/reduce_scatter | solution.py:207
  (46 other events, 1179.0 us)
Sparse Core Ops, SparseCore 0:
  11.5 155.3 all-gather.14
  179.7 72.9 all-gather.16
  255.3 71.6 all-gather.18
  330.4 76.4 all-gather.20
  410.2 191.4 all-gather.22
  605.0 192.9 all-gather.26
  800.9 192.9 all-gather.28
  1016.2 77.5 all-gather.30
  1096.0 73.2 all-gather.32
  1171.8 75.7 all-gather.34
  1250.5 152.2 all-gather.36
  1405.6 192.9 all-gather.24
  1605.0 125.6 all-reduce.20
  1733.6 182.0 reduce-scatter.6
  1923.6 431.7 reduce-scatter.4
  2358.4 702.0 reduce-scatter.8
  3063.4 705.8 reduce-scatter.10
where the time goes:
time: 3790 us; the launch traced here: 3780 us
  waiting for transfers between devices  3160 us (83%)
  matrix products  257 us (7%)
  blocking collectives  213 us (6%)
  local copies, waits for them, and re-layouts  84 us (2%)
  other arithmetic  42.4 us (1%)
    reduce_scatter x1, waiting for transfers between devices, on_device(): lax.psum_scatter(grad_w_down, ('ctx', 'fsdp'), scatter_dimension=0, tiled...  709 us
    reduce_scatter x1, waiting for transfers between devices, on_device(): lax.psum_scatter(grad_w_in, ('ctx', 'fsdp'), scatter_dimension=0, tiled=T...  705 us
    reduce_scatter x1, waiting for transfers between devices, on_device(): lax.psum_scatter(grad_w_qkv, ('ctx', 'fsdp'), scatter_dimension=0, tiled=...  440 us
    all_gather x1, waiting for transfers between devices, on_device(): lax.all_gather(to_half(w_in), ('ctx', 'fsdp'), axis=0, tiled=True)  190 us
    all_gather x1, waiting for transfers between devices, on_device(): lax.all_gather(to_half(held_params[4]), ('ctx', 'fsdp'), axis=0, tiled=True)  179 us
    all_gather x1, waiting for transfers between devices, on_device(): lax.all_gather(to_half(held_params[2]), ('ctx', 'fsdp'), axis=0, tiled=True)  176 us
    reduce_scatter x1, waiting for transfers between devices, on_device(): lax.psum_scatter(grad_w_out, ('ctx', 'fsdp'), scatter_dimension=0, tiled=...  175 us
    unnamed x18, waiting for transfers between devices  114 us
  transfers between devices with their start and end apart: 17, of which 14 were waited for; matrix products, arithmetic and copies ran while one was open for 9% of the time, Pallas kernels for 0%

commit v1 on v0

v1 whole, which is shorter than its diff:
```python
import math

import jax
import jax.numpy as jnp
from jax import lax
from jax.sharding import Mesh
from jax.sharding import PartitionSpec as P

HD = 128
BLK = 128
EPSILON = 1e-05
NEG_FILL = -1e30

EVERY = ("tp", "sp", "fs")
TOKENS = ("sp", "fs")
SNAKE = (0, 2, 4, 6, 7, 5, 3, 1)


def half(values):
    return values.astype(jnp.bfloat16)


def full(values):
    return values.astype(jnp.float32)


def dot(left, right, left_dim, right_dim, out=jnp.float32):
    return lax.dot_general(
        left, right, (((left_dim,), (right_dim,)), ((), ())), preferred_element_type=jnp.float32
    ).astype(out)


def normalize(values):
    center = values - jnp.mean(values, axis=-1, keepdims=True)
    spread = jnp.mean(center * center, axis=-1, keepdims=True)
    scale = lax.rsqrt(spread + EPSILON)
    return center * scale, scale


def normalize_back(normed, scale, grad):
    return scale * (
        grad
        - jnp.mean(grad, axis=-1, keepdims=True)
        - normed * jnp.mean(grad * normed, axis=-1, keepdims=True)
    )


class Ring:
    def __init__(self, size):
        self.size = size
        order = SNAKE if size == len(SNAKE) else tuple(range(size))
        place = [order.index(i) for i in range(size)]
        self.order = order
        self.up = [(order[i], order[(i + 1) % size]) for i in range(size)]
        self.down = [(b, a) for a, b in self.up]
        self.place = jnp.asarray(place, jnp.int32)[lax.axis_index("tp")]

    def index(self, shift):
        return jnp.asarray(self.order, jnp.int32)[(self.place + shift) % self.size]

    def send_up(self, values):
        return lax.ppermute(values, "tp", self.up)

    def send_down(self, values):
        return lax.ppermute(values, "tp", self.down)

    def gather(self, rows):
        n = rows.shape[0]
        out = jnp.zeros((self.size * n,) + rows.shape[1:], rows.dtype)

        def put(out, chunk, shift, begin=0):
            return lax.dynamic_update_slice_in_dim(out, chunk, self.index(shift) * n + begin, 0)

        out = put(out, rows, 0)
        from_below = from_above = rows
        for hop in range(1, (self.size + 1) // 2):
            from_below, from_above = self.send_up(from_below), self.send_down(from_above)
            out = put(out, from_below, -hop)
            out = put(out, from_above, hop)
        if self.size % 2 == 0:
            low = self.send_up(from_below[: n // 2])
            high = self.send_down(from_above[n // 2 :])
            out = put(out, low, self.size // 2)
            out = put(out, high, self.size // 2, n // 2)
        return out

    def reduce_scatter(self, partial):
        n = partial.shape[0] // self.size
        middle = self.size // 2

        def own(shift):
            return lax.dynamic_slice_in_dim(partial, self.index(shift) * n, n)

        far = own(middle)
        low, high = self.send_up(far[: n // 2]), self.send_down(far[n // 2 :])
        part = own(middle - 1)
        upward = jnp.concatenate([half(full(part[: n // 2]) + full(low)), part[n // 2 :]])
        part = own(1 - middle)
        downward = jnp.concatenate([part[: n // 2], half(full(part[n // 2 :]) + full(high))])
        for hop in range(middle - 2, -1, -1):
            upward, downward = self.send_up(upward), self.send_down(downward)
            if hop:
                upward = half(full(upward) + full(own(hop)))
                downward = half(full(downward) + full(own(-hop)))
        return full(own(0)) + full(upward) + full(downward)


def columns_in(rows, groups, tp):
    n, width = rows.shape
    part = width // groups // tp
    rows = lax.all_to_all(
        rows.reshape(n, groups, tp, part), "tp", split_axis=2, concat_axis=0, tiled=False
    )
    rows = lax.all_gather(rows.reshape(tp, n, groups * part), TOKENS, axis=1, tiled=True)
    return rows.reshape(-1, groups * part)


def columns_out(grad, groups, tp):
    part = grad.shape[1] // groups
    grad = grad.reshape(tp, -1, groups * part)
    grad = lax.psum_scatter(half(grad), TOKENS, scatter_dimension=1, tiled=True)
    n = grad.shape[1]
    grad = lax.all_to_all(
        grad.reshape(tp, n, groups, part), "tp", split_axis=0, concat_axis=2, tiled=False
    )
    return full(grad.reshape(n, groups * tp * part))


def on_device(
    tokens,
    ln1_gain,
    ln1_bias,
    w_qkv,
    b_qv,
    w_out,
    b_out,
    ln2_gain,
    ln2_bias,
    w_in,
    b_in,
    w_down,
    b_down,
    cotangent,
    block_seg,
    block_pos,
):
    tp = lax.axis_size("tp")
    sp = lax.axis_size("sp")
    fs = lax.axis_size("fs")
    devices = tp * sp * fs
    my_tp = lax.axis_index("tp")
    my_sp = lax.axis_index("sp")
    ring = Ring(tp)
    local_rows, width = tokens.shape[1:]
    heads = width // HD
    my_heads = heads // tp
    head_cols = my_heads * HD
    group_rows = tp * local_rows

    offsets = jnp.arange(BLK, dtype=jnp.int32)
    seg_all = jnp.repeat(block_seg[0], BLK).reshape(tp, sp, local_rows)
    pos_all = (block_pos[0][:, None] + offsets[None, :]).reshape(tp, sp, local_rows)
    query_seg = lax.dynamic_index_in_dim(seg_all, my_sp, 1, keepdims=False).reshape(-1)
    query_pos = lax.dynamic_index_in_dim(pos_all, my_sp, 1, keepdims=False).reshape(-1)
    key_seg = seg_all.transpose(1, 0, 2).reshape(-1)
    key_pos = pos_all.transpose(1, 0, 2).reshape(-1)

    small = [ln1_gain, ln1_bias, b_out, ln2_gain, ln2_bias, b_down, b_qv, b_in]
    sizes = [v.shape[0] for v in small]
    gathered = lax.all_gather(jnp.concatenate(small), EVERY, axis=0, tiled=True)
    gathered = full(half(gathered)).reshape(devices, -1)
    cuts = [sum(sizes[:i]) for i in range(len(sizes) + 1)]
    gain1, bias1, out_bias, gain2, bias2, down_bias, qv_bias, in_bias = (
        gathered[:, cuts[i] : cuts[i + 1]].reshape(-1) for i in range(len(sizes))
    )
    qv_bias = lax.dynamic_slice_in_dim(qv_bias.reshape(2, width), my_tp * head_cols, head_cols, 1)
    in_bias = lax.dynamic_slice_in_dim(in_bias, my_tp * (in_bias.shape[0] // tp), in_bias.shape[0] // tp)

    qkv_slice = columns_in(half(w_qkv), 3, tp)
    out_slice = lax.all_gather(half(w_out), TOKENS, axis=0, tiled=True)
    group_tokens = ring.gather(tokens[0])
    in_slice = columns_in(half(w_in), 1, tp)
    down_slice = lax.all_gather(half(w_down), TOKENS, axis=0, tiled=True)
    group_cot = ring.gather(cotangent[0])

    group_normed, unused_scale = normalize(full(group_tokens))
    normed_half = half(group_normed * gain1 + bias1)
    mixed = dot(normed_half, qkv_slice, 1, 0)
    query = half(mixed[:, :head_cols] + qv_bias[0])
    key = half(mixed[:, head_cols : 2 * head_cols])
    value = half(mixed[:, 2 * head_cols :] + qv_bias[1])

    def by_head(rows):
        return rows.reshape(-1, my_heads, HD)

    query_heads = by_head(query)
    key_heads, value_heads = by_head(key), by_head(value)
    if sp > 1:
        key_heads = lax.all_gather(key_heads, "sp", axis=0, tiled=True)
        value_heads = lax.all_gather(value_heads, "sp", axis=0, tiled=True)
    head_ids = my_tp * my_heads + jnp.arange(my_heads, dtype=jnp.int32)
    slopes = jnp.exp2(-8.0 * (head_ids.astype(jnp.float32) + 1.0) / heads)
    scale_qk = 1.0 / math.sqrt(HD)
    visible = ((key_seg[None, :] == 0) | (key_seg[None, :] == query_seg[:, None])) & (
        key_pos[None, :] <= query_pos[:, None]
    )
    distance = (query_pos[:, None] - key_pos[None, :]).astype(jnp.float32)
    scores = jnp.einsum("qhd,khd->hqk", query_heads, key_heads, preferred_element_type=jnp.float32)
    scores = scores * scale_qk - slopes[:, None, None] * distance[None]
    scores = jnp.where(visible[None], scores, NEG_FILL)
    top = jnp.max(scores, axis=-1, keepdims=True)
    expon = jnp.exp(scores - top)
    probs = expon / jnp.sum(expon, axis=-1, keepdims=True)
    probs_half = half(probs)
    attended = jnp.einsum(
        "hqk,khd->qhd", probs_half, value_heads, preferred_element_type=jnp.float32
    )
    attended = half(attended.reshape(group_rows, head_cols))
    branch = ring.reduce_scatter(dot(attended, out_slice, 1, 0, jnp.bfloat16))
    residual = full(tokens[0]) + branch + out_bias

    own_normed2, scale2 = normalize(residual)
    second = ring.gather(half(own_normed2 * gain2 + bias2))
    pre_act = dot(second, in_slice, 1, 0) + in_bias
    d_act = dot(group_cot, down_slice, 1, 1)
    act, gelu_back = jax.vjp(lambda v: jax.nn.gelu(v, approximate=True), pre_act)
    act = half(act)
    d_pre_full = gelu_back(d_act)[0]
    d_pre = half(d_pre_full)
    d_second = ring.reduce_scatter(dot(d_pre, in_slice, 1, 1, jnp.bfloat16))
    ffn = ring.reduce_scatter(dot(act, down_slice, 1, 0, jnp.bfloat16))
    output = half(residual + ffn + down_bias)
    grad_down_slice = dot(act, group_cot, 0, 0, jnp.bfloat16)
    grad_in_slice = dot(second, d_pre, 0, 0, jnp.bfloat16)
    grad_w_down = full(lax.psum_scatter(grad_down_slice, TOKENS, scatter_dimension=0, tiled=True))
    grad_w_in = columns_out(grad_in_slice, 1, tp)
    grad_b_in = jnp.sum(full(d_pre), axis=0)

    own_cot = full(cotangent[0])
    d_residual = own_cot + normalize_back(own_normed2, scale2, d_second * gain2)
    d_branch_own = half(d_residual)
    d_branch = ring.gather(d_branch_own)

    grad_out_slice = dot(attended, d_branch, 0, 0, jnp.bfloat16)
    grad_w_out = full(lax.psum_scatter(grad_out_slice, TOKENS, scatter_dimension=0, tiled=True))
    d_attended = by_head(dot(d_branch, out_slice, 1, 1, jnp.bfloat16))
    d_prob = jnp.einsum(
        "qhd,khd->hqk", d_attended, value_heads, preferred_element_type=jnp.float32
    )
    delta = jnp.sum(probs * d_prob, axis=-1, keepdims=True)
    d_score = half(probs * (d_prob - delta))
    d_query = jnp.einsum("hqk,khd->qhd", d_score, key_heads, preferred_element_type=jnp.float32)
    d_key = jnp.einsum("hqk,qhd->khd", d_score, query_heads, preferred_element_type=jnp.float32)
    d_value = jnp.einsum(
        "hqk,qhd->khd", probs_half, d_attended, preferred_element_type=jnp.float32
    )
    if sp > 1:
        d_key = lax.psum_scatter(d_key, "sp", scatter_dimension=0, tiled=True)
        d_value = lax.psum_scatter(d_value, "sp", scatter_dimension=0, tiled=True)
    d_query = half((d_query * scale_qk).reshape(group_rows, head_cols))
    d_key = half((d_key * scale_qk).reshape(group_rows, head_cols))
    d_value = half(d_value.reshape(group_rows, head_cols))
    d_mixed = jnp.concatenate([d_query, d_key, d_value], axis=1)
    d_normed_partial = dot(d_mixed, qkv_slice, 1, 1)
    d_normed = ring.reduce_scatter(half(d_normed_partial))
    grad_w_qkv = columns_out(dot(normed_half, d_mixed, 0, 0, jnp.bfloat16), 3, tp)

    own_normed1, scale1 = normalize(full(tokens[0]))
    grad_tokens = d_residual + normalize_back(own_normed1, scale1, d_normed * gain1)

    def placed(values, whole):
        start = my_tp * values.shape[-1]
        blank = jnp.zeros(values.shape[:-1] + (whole,), jnp.float32)
        return lax.dynamic_update_slice_in_dim(blank, values, start, values.ndim - 1)

    grad_b_qv = placed(
        jnp.stack([jnp.sum(full(d_query), axis=0), jnp.sum(full(d_value), axis=0)]), width
    )
    partials = [
        jnp.sum(d_normed_partial * group_normed, axis=0),
        jnp.sum(d_normed_partial, axis=0),
        jnp.sum(full(d_branch_own), axis=0),
        jnp.sum(d_second * own_normed2, axis=0),
        jnp.sum(d_second, axis=0),
        jnp.sum(own_cot, axis=0),
        grad_b_qv.reshape(-1),
        placed(grad_b_in, tp * grad_b_in.shape[0]),
    ]
    stacked = jnp.concatenate([v.reshape(devices, -1) for v in partials], axis=1)
    summed = lax.psum_scatter(stacked, EVERY, scatter_dimension=0, tiled=True).reshape(-1)
    g_gain1, g_bias1, g_b_out, g_gain2, g_bias2, g_b_down, g_b_qv, g_b_in = (
        summed[cuts[i] : cuts[i + 1]] for i in range(len(sizes))
    )
    return (
        output[None],
        grad_tokens[None],
        g_gain1,
        g_bias1,
        grad_w_qkv,
        g_b_qv,
        grad_w_out,
        g_b_out,
        g_gain2,
        g_bias2,
        grad_w_in,
        g_b_in,
        grad_w_down,
        g_b_down,
    )


def solution(mesh):
    ctx, fs = mesh.shape["ctx"], mesh.shape["fsdp"]
    tp = math.gcd(ctx, len(SNAKE))
    inner = Mesh(mesh.devices.reshape(tp, ctx // tp, fs), EVERY)
    rows = P("fs", ("tp", "sp"), None)
    vector, matrix, blocks = P(EVERY), P(EVERY, None), P("fs", None)
    return jax.shard_map(
        on_device,
        mesh=inner,
        in_specs=(
            rows,
            vector,
            vector,
            matrix,
            vector,
            matrix,
            vector,
            vector,
            vector,
            matrix,
            vector,
            matrix,
            vector,
            rows,
            blocks,
            blocks,
        ),
        out_specs=(
            rows,
            rows,
            vector,
            vector,
            matrix,
            vector,
            matrix,
            vector,
            vector,
            vector,
            matrix,
            vector,
            matrix,
            vector,
        ),
        check_vma=False,
    )
```

time: 3790 us -> 757 us (0.20)
  waiting for transfers between devices: 3160 us -> 329 us
  matrix products: 257 us -> 101 us
  blocking collectives: 213 us -> 73.4 us
  starting transfers between devices: 1.17 us -> 87.2 us
    reduce_scatter x4, waiting for transfers between devices: 2030 us -> 94.4 us  [the longest x1 45.5 us: on_device(): lax.psum_scatter(grad_down_slice, TOKENS, scatter_dimension=0, tiled=True)]
    all_gather x12 -> x4, waiting for transfers between devices: 1010 us -> 0.05 us  [the longest x2 0.02 us: columns_in(): lax.all_gather(rows.reshape(tp, n, groups * part), TOKENS, axis=1, tiled=...]
    ppermute x0 -> x64, waiting for transfers between devices: none -> 196 us  [the longest x32 142 us: send_up(): return lax.ppermute(values, 'tp', self.up)]
    dot_general x40 -> x17, matrix products: 257 us -> 92.6 us  [the longest x12 80.5 us: dot(): lax.dot_general(left, right, (((left_dim,), (right_dim,)), ((), ())), pre...]
    unnamed x2 -> x0, blocking collectives: 84.5 us -> none
    all_gather x4 -> x1, blocking collectives: 128 us -> 48.1 us  [on_device(): gathered = lax.all_gather(jnp.concatenate(small), EVERY, axis=0, tiled=True)]
    unnamed x18 -> x10, waiting for transfers between devices: 114 us -> 39 us
    ppermute x0 -> x64, starting transfers between devices: none -> 70.2 us  [the longest x32 36.9 us: send_down(): return lax.ppermute(values, 'tp', self.down)]
  transfers between devices with their start and end apart: 17 -> 76, of which waited for: 14 -> 47; matrix products, arithmetic and copies ran while one was open for 9% -> 26% of each run, Pallas kernels for 0% -> 0%
where the time goes in v1:
time: 757 us; the launch traced here: 744 us
  waiting for transfers between devices  329 us (43%)
  matrix products  101 us (13%)
  starting transfers between devices  87.2 us (12%)
  blocking collectives  73.4 us (10%)
  local copies, waits for them, and re-layouts  71.4 us (9%)
  other arithmetic  55 us (7%)
  between operations  27 us (4%)
    ppermute x32, waiting for transfers between devices, send_up(): return lax.ppermute(values, 'tp', self.up)  142 us
    dot_general x12, matrix products, dot(): lax.dot_general(left, right, (((left_dim,), (right_dim,)), ((), ())), pre...  80.5 us
    ppermute x32, waiting for transfers between devices, send_down(): return lax.ppermute(values, 'tp', self.down)  53.8 us
    all_gather x1, blocking collectives, on_device(): gathered = lax.all_gather(jnp.concatenate(small), EVERY, axis=0, tiled=True)  48.1 us
    reduce_scatter x1, waiting for transfers between devices, on_device(): lax.psum_scatter(grad_down_slice, TOKENS, scatter_dimension=0, tiled=True)  45.5 us
    unnamed x10, waiting for transfers between devices  39 us
    ppermute x32, starting transfers between devices, send_down(): return lax.ppermute(values, 'tp', self.down)  36.9 us
    reduce_scatter x2, waiting for transfers between devices, columns_out(): grad = lax.psum_scatter(half(grad), TOKENS, scatter_dimension=1, tiled=True)  35.7 us
  transfers between devices with their start and end apart: 76, of which 47 were waited for; matrix products, arithmetic and copies ran while one was open for 26% of the time, Pallas kernels for 0%

profile of v1, /device:TPU:8, one launch (start us, length us, event | category | flops | bytes accessed | tf_op | source)
XLA Modules:
  0.0 744.0 jit_solution(16944290966287903664)
XLA Ops:
  9.1 25.3 %all_to_all.48 = bf16[1,64,3,8,256]{4,1,2,0,3:T(8,128)(2,1)S(1)} all-to-all(bf16[1,64,3,8,256]{4,1,2,0,3:T(8,128)(2,1)S(1)} %copy.145), channel_id=1, replica_groups=mesh['ctx'=8,'fsdp'=4] {'ctx'}, dimensions={3} | all-to-all | bytes 1572864 | tf_op jit(solution)/shard_map/all_to_all | solution.py:111
  48.3 48.1 %all-gather.1 = bf16[32,1,768]{2,1,0:T(2,128)(2,1)S(1)} all-gather(bf16[1,1,768]{2,1,0:T(2,128)(2,1)S(1)} %reshape.496), channel_id=1, replica_groups=mesh['ctx'=8,'fsdp'=4] {'ctx','fsdp'}, dimensions={0}, use_global_device_ids=true | all-gather | bytes 50688 | tf_op jit(solution)/shard_map/all_gather | solution.py:170
  125.5 8.3 %collective-permute-done.2 = bf16[128,2048]{1,0:T(8,128)(2,1)S(1)} collective-permute-done((bf16[128,2048]{1,0:T(8,128)(2,1)}, bf16[128,2048]{1,0:T(8,128)(2,1)S(1)}, u32[]{:S(2)}, u32[]{:S(2)}) %collective-permute-start.2) | collective-permute-done | bytes 524320 | tf_op jit(solution)/shard_map/ppermute | solution.py:62
  138.4 9.1 %collective-permute-done.4 = bf16[128,2048]{1,0:T(8,128)(2,1)S(1)} collective-permute-done((bf16[128,2048]{1,0:T(8,128)(2,1)S(1)}, bf16[128,2048]{1,0:T(8,128)(2,1)S(1)}, u32[]{:S(2)}, u32[]{:S(2)}) %collective-permute-start.4) | collective-permute-done | bytes 524320 | tf_op jit(solution)/shard_map/ppermute | solution.py:62
  172.3 8.1 %fusion.65 = (f32[2,1024]{1,0:T(2,128)S(1)}, f32[2,1024,1024]{1,2,0:T(8,128)}) fusion(f32[1024,1024]{0,1:T(8,128)} %subtract_convert_fusion, f32[2]{0:T(128)S(1)} %copy-done.44, pred[1024,1024]{0,1:T(8,128)(4,1)S(1)} %compare_and_fusion, bf16[1024,2,128]{0,2,1:T(8,128)(2,1)S(1)} %bitcast.167, bf16[1024,2,128]{0,2,1:T(8,128)(2,1)S(1)} %bitcast.169), kind=kOutput, calls=%fused_computation.212 | convolution fusion | flops 549454848 | bytes 14688264 | tf_op jit(solution)/shard_map/sub | solution.py:212
  207.8 8.9 %collective-permute-done.13 = bf16[128,2048]{1,0:T(8,128)(2,1)} collective-permute-done((bf16[128,2048]{1,0:T(8,128)(2,1)}, bf16[128,2048]{1,0:T(8,128)(2,1)}, u32[]{:S(2)}, u32[]{:S(2)}) %collective-permute-start.13) | collective-permute-done | bytes 524320 | tf_op jit(solution)/shard_map/ppermute | solution.py:65
  232.0 9.1 %collective-permute-done.10 = bf16[128,2048]{1,0:T(8,128)(2,1)S(1)} collective-permute-done((bf16[128,2048]{1,0:T(8,128)(2,1)S(1)}, bf16[128,2048]{1,0:T(8,128)(2,1)S(1)}, u32[]{:S(2)}, u32[]{:S(2)}) %collective-permute-start.10) | collective-permute-done | bytes 524320 | tf_op jit(solution)/shard_map/ppermute | solution.py:62
  255.6 8.0 %collective-permute-done.11 = bf16[128,2048]{1,0:T(8,128)(2,1)S(1)} collective-permute-done((bf16[128,2048]{1,0:T(8,128)(2,1)S(1)}, bf16[128,2048]{1,0:T(8,128)(2,1)S(1)}, u32[]{:S(2)}, u32[]{:S(2)}) %collective-permute-start.11) | collective-permute-done | bytes 524320 | tf_op jit(solution)/shard_map/ppermute | solution.py:62
  320.2 8.2 %fusion.67 = f32[1024,1024]{1,0:T(8,128)} fusion(bf16[1024,2048]{1,0:T(8,128)(2,1)} %constant_dynamic-update-slice_fusion.12, bf16[2048,1024]{1,0:T(8,128)(2,1)S(1)} %bitcast.156), kind=kOutput, calls=%fused_computation.214 | convolution fusion | flops 4294967296 | bytes 12582912 | tf_op jit(solution)/shard_map/dot_general | solution.py:28
  328.5 11.7 %convert_reduce_fusion.1 = (f32[1024]{0:T(1024)S(1)}, bf16[1024,1024]{1,0:T(8,128)(2,1)S(1)}) fusion(f32[1024,1024]{1,0:T(8,128)} %fusion.67, f32[1024]{0:T(1024)S(1)} %dynamic_slice.348, bf16[1024,2048]{1,0:T(8,128)(2,1)} %constant_dynamic-update-slice_fusion.13, bf16[1024,2048]{1,0:T(8,128)(2,1)} %all-gather.11.cloned.1.call-done), kind=kOutput, calls=%fused_computation.25 | convolution fusion | flops 4319083520 | bytes 14688256 | tf_op jit(solution)/shard_map/dot_general | solution.py:28
  365.5 8.9 %collective-permute-done.45 = bf16[128,2048]{1,0:T(8,128)(2,1)S(1)} collective-permute-done((bf16[128,2048]{1,0:T(8,128)(2,1)S(1)}, bf16[128,2048]{1,0:T(8,128)(2,1)S(1)}, u32[]{:S(2)}, u32[]{:S(2)}) %collective-permute-start.45) | collective-permute-done | bytes 524320 | tf_op jit(solution)/shard_map/ppermute | solution.py:65
  376.8 8.8 %collective-permute-done.29 = bf16[128,2048]{1,0:T(8,128)(2,1)S(1)} collective-permute-done((bf16[128,2048]{1,0:T(8,128)(2,1)S(1)}, bf16[128,2048]{1,0:T(8,128)(2,1)S(1)}, u32[]{:S(2)}, u32[]{:S(2)}) %collective-permute-start.29) | collective-permute-done | bytes 524320 | tf_op jit(solution)/shard_map/ppermute | solution.py:65
  430.0 8.4 %convolution_convert_fusion.2 = bf16[2048,1024]{1,0:T(8,128)(2,1)} fusion(bf16[1024,2048]{1,0:T(8,128)(2,1)} %constant_dynamic-update-slice_fusion.12, bf16[1024,1024]{1,0:T(8,128)(2,1)S(1)} %copy-done.47), kind=kOutput, calls=%fused_computation.37 | convolution fusion | flops 4297064448 | bytes 10485760 | tf_op jit(solution)/shard_map/dot_general | solution.py:28
  442.6 8.6 %collective-permute-done.50 = bf16[128,2048]{1,0:T(8,128)(2,1)S(1)} collective-permute-done((bf16[128,2048]{1,0:T(8,128)(2,1)S(1)}, bf16[128,2048]{1,0:T(8,128)(2,1)S(1)}, u32[]{:S(2)}, u32[]{:S(2)}) %collective-permute-start.50) | collective-permute-done | bytes 524320 | tf_op jit(solution)/shard_map/ppermute | solution.py:62
  453.8 9.4 %collective-permute-done.52 = bf16[128,2048]{1,0:T(8,128)(2,1)S(1)} collective-permute-done((bf16[128,2048]{1,0:T(8,128)(2,1)S(1)}, bf16[128,2048]{1,0:T(8,128)(2,1)S(1)}, u32[]{:S(2)}, u32[]{:S(2)}) %collective-permute-start.52) | collective-permute-done | bytes 524320 | tf_op jit(solution)/shard_map/ppermute | solution.py:62
  483.6 7.9 %fusion.59 = (f32[2048]{0:T(1024)S(1)}, f32[2048]{0:T(1024)S(1)}, bf16[1024,2048]{1,0:T(8,128)(2,1)}) fusion(f32[1024]{0:T(1024)S(1)} %copy-done.30, f32[1024]{0:T(1024)S(1)} %broadcast_multiply_fusion, bf16[1024,2048]{1,0:T(8,128)(2,1)} %constant_dynamic-update-slice_fusion.28, bf16[2048,768]{1,0:T(8,128)(2,1)S(1)} %bitcast.193, ...), kind=kOutput, calls=%fused_computation.208 | convolution fusion | flops 3240620032 | bytes 13131776 | tf_op jit(solution)/shard_map/dot_general | solution.py:28
  492.8 8.4 %convolution_convert_fusion.5 = bf16[2048,768]{1,0:T(8,128)(2,1)} fusion(bf16[1024,256]{0,1:T(8,128)(2,1)S(1)} %bitcast.195, bf16[1024,256]{0,1:T(8,128)(2,1)S(1)} %bitcast.178, bf16[1024,256]{0,1:T(8,128)(2,1)S(1)} %bitcast.182, bf16[1024,2048]{1,0:T(8,128)(2,1)} %constant_dynamic-update-slice_fusion.28, f32[2048]{0:T(1024)S(1)} %copy-done.27, ...), kind=kOutput, calls=%fused_computation.40 | convolution fusion | flops 3240099840 | bytes 8937472 | tf_op jit(solution)/shard_map/dot_general | solution.py:28
  505.8 10.8 %convolution_convert_fusion.1 = bf16[1024,2048]{1,0:T(8,128)(2,1)} fusion(bf16[1024,2048]{1,0:T(8,128)(2,1)} %constant_dynamic-update-slice_fusion.13, f32[1024,1024]{1,0:T(8,128)} %fusion.67, f32[1024]{0:T(1024)S(1)} %dynamic_slice.348), kind=kOutput, calls=%fused_computation.36 | convolution fusion | flops 4307550208 | bytes 12587008 | tf_op jit(solution)/shard_map/dot_general | solution.py:28
  536.5 13.0 %collective-permute-done.61 = bf16[128,2048]{1,0:T(8,128)(2,1)S(1)} collective-permute-done((bf16[128,2048]{1,0:T(8,128)(2,1)S(1)}, bf16[128,2048]{1,0:T(8,128)(2,1)S(1)}, u32[]{:S(2)}, u32[]{:S(2)}) %collective-permute-start.61) | collective-permute-done | bytes 524320 | tf_op jit(solution)/shard_map/ppermute | solution.py:65
  554.1 17.2 %collective-permute-done.58 = bf16[128,2048]{1,0:T(8,128)(2,1)S(1)} collective-permute-done((bf16[128,2048]{1,0:T(8,128)(2,1)S(1)}, bf16[128,2048]{1,0:T(8,128)(2,1)S(1)}, u32[]{:S(2)}, u32[]{:S(2)}) %collective-permute-start.58) | collective-permute-done | bytes 524320 | tf_op jit(solution)/shard_map/ppermute | solution.py:62
  576.4 38.9 %all-reduce.3.cloned.1.call-done = f32[32,768]{1,0:T(8,128)} async-done(((f32[32,768]{1,0:T(8,128)}), f32[32,768]{1,0:T(8,128)}) %all-reduce.3.cloned.1.call-update) | async-done | bytes 98320
  619.3 35.7 %reduce-scatter.5.cloned.1.call-done = bf16[8,64,768]{2,1,0:T(8,128)(2,1)} async-done(((bf16[8,256,768]{2,1,0:T(8,128)(2,1)}), bf16[8,64,768]{2,1,0:T(8,128)(2,1)}) %reduce-scatter.5.cloned.1.call-update) | async-done | bytes 786448 | tf_op jit(solution)/shard_map/reduce_scatter | solution.py:121
  669.7 13.3 %reduce-scatter.7.cloned.1.call-done = bf16[64,2048]{1,0:T(8,128)(2,1)} async-done(((bf16[256,2048]{1,0:T(8,128)(2,1)}), bf16[64,2048]{1,0:T(8,128)(2,1)}) %reduce-scatter.7.cloned.1.call-update) | async-done | bytes 262160 | tf_op jit(solution)/shard_map/reduce_scatter | solution.py:245
  684.8 45.5 %reduce-scatter.11.cloned.1.call-done = bf16[256,2048]{1,0:T(8,128)(2,1)} async-done(((bf16[1024,2048]{1,0:T(8,128)(2,1)}), bf16[256,2048]{1,0:T(8,128)(2,1)}) %reduce-scatter.11.cloned.1.call-update) | async-done | bytes 1048592 | tf_op jit(solution)/shard_map/reduce_scatter | solution.py:235
  (412 shorter events, 337.6 us)
Async XLA Ops:
  7.2 157.5 %all-gather.7.cloned.1.call-start = ((), (), s32[]{:S(2)}) async-start(), calls=%async_computation.8 | async-start | bytes 3932160 | tf_op jit(solution)/shard_map/all_gather | solution.py:114
  36.8 80.4 %collective-permute-start = (bf16[128,2048]{1,0:T(8,128)(2,1)S(1)}, bf16[128,2048]{1,0:T(8,128)(2,1)}, u32[]{:S(2)}, u32[]{:S(2)}) collective-permute-start(bf16[128,2048]{1,0:T(8,128)(2,1)S(1)} %bitcast.150), channel_id=1, source_target_pairs={{0,8},{8,16},{16,24},{24,28},{28,20},{20,12},{12,4},{4,0},{1,9},{9... | collective-permute-start | bytes 1572872 | tf_op jit(solution)/shard_map/ppermute | solution.py:62
  37.3 83.0 %collective-permute-start.1 = (bf16[128,2048]{1,0:T(8,128)(2,1)S(1)}, bf16[128,2048]{1,0:T(8,128)(2,1)S(1)}, u32[]{:S(2)}, u32[]{:S(2)}) collective-permute-start(bf16[128,2048]{1,0:T(8,128)(2,1)S(1)} %bitcast.151), channel_id=1, source_target_pairs={{8,0},{16,8},{24,16},{28,24},{20,28},{12,20},{4,12},{0,4},{9,1},{1... | collective-permute-start | bytes 1572872 | tf_op jit(solution)/shard_map/ppermute | solution.py:65
  42.8 113.4 %all-to-all-start.1 = ((bf16[1,64,1,8,1024]{4,1,2,0,3:T(8,128)(2,1)}), bf16[1,64,1,8,1024]{4,1,2,0,3:T(8,128)(2,1)S(1)}, u32[]{:S(2)}, u32[]{:S(2)}) async-start(bf16[1,64,1,8,1024]{4,1,2,0,3:T(8,128)(2,1)} %copy.150), calls=%async_computation.1 | async-start | bytes 2097152 | tf_op jit(solution)/shard_map/all_to_all | solution.py:111
  47.3 137.3 %all-gather.9.cloned.1.call-start = ((), (), s32[]{:S(2)}) async-start(), calls=%async_computation.9 | async-start | bytes 1310720 | tf_op jit(solution)/shard_map/all_gather | solution.py:180
  48.1 245.0 %all-gather.13.cloned.1.call-start = ((), (), s32[]{:S(2)}) async-start(), calls=%async_computation.15 | async-start | bytes 5242880 | tf_op jit(solution)/shard_map/all_gather | solution.py:114
  157.8 170.7 %all-gather.11.cloned.1.call-start = ((), (), s32[]{:S(2)}) async-start(), calls=%async_computation.10 | async-start | bytes 5242880 | tf_op jit(solution)/shard_map/all_gather | solution.py:183
  204.4 25.5 %collective-permute-start.32 = (bf16[128,2048]{1,0:T(8,128)(2,1)S(1)}, bf16[128,2048]{1,0:T(8,128)(2,1)}, u32[]{:S(2)}, u32[]{:S(2)}) collective-permute-start(bf16[128,2048]{1,0:T(8,128)(2,1)S(1)} %bitcast.164), channel_id=1, source_target_pairs={{0,8},{8,16},{16,24},{24,28},{28,20},{20,12},{12,4},{4,0},{1,9},{9... | collective-permute-start | bytes 1572872 | tf_op jit(solution)/shard_map/ppermute | solution.py:62
  205.5 25.3 %collective-permute-start.33 = (bf16[128,2048]{1,0:T(8,128)(2,1)S(1)}, bf16[128,2048]{1,0:T(8,128)(2,1)}, u32[]{:S(2)}, u32[]{:S(2)}) collective-permute-start(bf16[128,2048]{1,0:T(8,128)(2,1)S(1)} %bitcast.165), channel_id=1, source_target_pairs={{8,0},{16,8},{24,16},{28,24},{20,28},{12,20},{4,12},{0,4},{9,1},{1... | collective-permute-start | bytes 1572872 | tf_op jit(solution)/shard_map/ppermute | solution.py:65
  207.6 323.6 %reduce-scatter.9.cloned.1.call-start = ((), (), s32[]{:S(2)}) async-start(), calls=%async_computation.13 | async-start | bytes 5242880 | tf_op jit(solution)/shard_map/reduce_scatter | solution.py:121
  229.9 22.4 %collective-permute-start.34 = (bf16[128,2048]{1,0:T(8,128)(2,1)}, bf16[128,2048]{1,0:T(8,128)(2,1)S(1)}, u32[]{:S(2)}, u32[]{:S(2)}) collective-permute-start(bf16[128,2048]{1,0:T(8,128)(2,1)} %collective-permute-done.32), channel_id=1, source_target_pairs={{0,8},{8,16},{16,24},{24,28},{28,20},{20,12},{12,4},{4,0},{1,9},{9... | collective-permute-start | bytes 1572872 | tf_op jit(solution)/shard_map/ppermute | solution.py:62
  230.8 22.4 %collective-permute-start.35 = (bf16[128,2048]{1,0:T(8,128)(2,1)}, bf16[128,2048]{1,0:T(8,128)(2,1)S(1)}, u32[]{:S(2)}, u32[]{:S(2)}) collective-permute-start(bf16[128,2048]{1,0:T(8,128)(2,1)} %collective-permute-done.33), channel_id=1, source_target_pairs={{8,0},{16,8},{24,16},{28,24},{20,28},{12,20},{4,12},{0,4},{9,1},{1... | collective-permute-start | bytes 1572872 | tf_op jit(solution)/shard_map/ppermute | solution.py:65
  252.3 22.5 %collective-permute-start.36 = (bf16[128,2048]{1,0:T(8,128)(2,1)S(1)}, bf16[128,2048]{1,0:T(8,128)(2,1)S(1)}, u32[]{:S(2)}, u32[]{:S(2)}) collective-permute-start(bf16[128,2048]{1,0:T(8,128)(2,1)S(1)} %collective-permute-done.34), channel_id=1, source_target_pairs={{0,8},{8,16},{16,24},{24,28},{28,20},{20,12},{12,4},{4,0},{1,9},{9... | collective-permute-start | bytes 1572872 | tf_op jit(solution)/shard_map/ppermute | solution.py:62
  253.2 22.5 %collective-permute-start.37 = (bf16[128,2048]{1,0:T(8,128)(2,1)S(1)}, bf16[128,2048]{1,0:T(8,128)(2,1)S(1)}, u32[]{:S(2)}, u32[]{:S(2)}) collective-permute-start(bf16[128,2048]{1,0:T(8,128)(2,1)S(1)} %collective-permute-done.35), channel_id=1, source_target_pairs={{8,0},{16,8},{24,16},{28,24},{20,28},{12,20},{4,12},{0,4},{9,1},{1... | collective-permute-start | bytes 1572872 | tf_op jit(solution)/shard_map/ppermute | solution.py:65
  363.3 22.3 %collective-permute-start.29 = (bf16[128,2048]{1,0:T(8,128)(2,1)S(1)}, bf16[128,2048]{1,0:T(8,128)(2,1)S(1)}, u32[]{:S(2)}, u32[]{:S(2)}) collective-permute-start(bf16[128,2048]{1,0:T(8,128)(2,1)S(1)} %pad_maximum_fusion.6), channel_id=1, source_target_pairs={{8,0},{16,8},{24,16},{28,24},{20,28},{12,20},{4,12},{0,4},{9,1},{1... | collective-permute-start | bytes 1572872 | tf_op jit(solution)/shard_map/ppermute | solution.py:65
  375.5 21.4 %collective-permute-start.46 = (bf16[128,2048]{1,0:T(8,128)(2,1)S(1)}, bf16[128,2048]{1,0:T(8,128)(2,1)S(1)}, u32[]{:S(2)}, u32[]{:S(2)}) collective-permute-start(bf16[128,2048]{1,0:T(8,128)(2,1)S(1)} %get-tuple-element.46), channel_id=1, source_target_pairs={{8,0},{16,8},{24,16},{28,24},{20,28},{12,20},{4,12},{0,4},{9,1},{1... | collective-permute-start | bytes 1572872 | tf_op jit(solution)/shard_map/ppermute | solution.py:65
  438.4 176.8 %all-reduce.3.cloned.1.call-start = ((), (), s32[]{:S(2)}) async-start(), calls=%async_computation.16 | async-start | bytes 196608
  492.4 162.6 %reduce-scatter.5.cloned.1.call-start = ((), (), s32[]{:S(2)}) async-start(), calls=%async_computation.11 | async-start | bytes 3932160 | tf_op jit(solution)/shard_map/reduce_scatter | solution.py:121
  501.3 181.7 %reduce-scatter.7.cloned.1.call-start = ((), (), s32[]{:S(2)}) async-start(), calls=%async_computation.12 | async-start | bytes 1310720 | tf_op jit(solution)/shard_map/reduce_scatter | solution.py:245
  505.8 224.5 %reduce-scatter.11.cloned.1.call-start = ((), (), s32[]{:S(2)}) async-start(), calls=%async_computation.14 | async-start | bytes 5242880 | tf_op jit(solution)/shard_map/reduce_scatter | solution.py:235
  531.1 127.5 %all-to-all-start.3 = ((bf16[8,64,1,1,1024]{4,1,3,2,0:T(8,128)(2,1)}), bf16[8,64,1,1,1024]{4,1,3,2,0:T(8,128)(2,1)S(1)}, u32[]{:S(2)}, u32[]{:S(2)}) async-start(bf16[8,64,1,1,1024]{4,1,3,2,0:T(8,128)(2,1)} %bitcast.173), calls=%async_computation.6 | async-start | bytes 2097152 | tf_op jit(solution)/shard_map/all_to_all | solution.py:123
  574.0 90.8 %collective-permute-start.59 = (bf16[128,2048]{1,0:T(8,128)(2,1)}, bf16[128,2048]{1,0:T(8,128)(2,1)}, u32[]{:S(2)}, u32[]{:S(2)}) collective-permute-start(bf16[128,2048]{1,0:T(8,128)(2,1)} %get-tuple-element.33), channel_id=1, source_target_pairs={{0,8},{8,16},{16,24},{24,28},{28,20},{20,12},{12,4},{4,0},{1,9},{9... | collective-permute-start | bytes 1572872 | tf_op jit(solution)/shard_map/ppermute | solution.py:62
  576.4 88.4 %collective-permute-start.63 = (bf16[128,2048]{1,0:T(8,128)(2,1)}, bf16[128,2048]{1,0:T(8,128)(2,1)}, u32[]{:S(2)}, u32[]{:S(2)}) collective-permute-start(bf16[128,2048]{1,0:T(8,128)(2,1)} %get-tuple-element.34), channel_id=1, source_target_pairs={{8,0},{16,8},{24,16},{28,24},{20,28},{12,20},{4,12},{0,4},{9,1},{1... | collective-permute-start | bytes 1572872 | tf_op jit(solution)/shard_map/ppermute | solution.py:65
  658.6 76.2 %all-to-all-start.2 = ((bf16[8,64,3,1,256]{4,1,3,2,0:T(8,128)(2,1)}), bf16[8,64,3,1,256]{4,1,3,2,0:T(8,128)(2,1)S(1)}, u32[]{:S(2)}, u32[]{:S(2)}) async-start(bf16[8,64,3,1,256]{4,1,3,2,0:T(8,128)(2,1)} %copy.158), calls=%async_computation.3 | async-start | bytes 1572864 | tf_op jit(solution)/shard_map/all_to_all | solution.py:123
  (102 other events, 1478.3 us)
Sparse Core Ops, SparseCore 0:
  36.9 28.0 all-gather.6
  67.1 16.9 all-gather.8
  157.9 31.8 all-gather.12
  207.7 32.6 all-gather.10
  438.6 42.4 reduce-scatter.8
  492.5 122.7 all-reduce.2
  617.9 37.0 reduce-scatter.4
  658.1 24.8 reduce-scatter.6
  685.7 44.5 reduce-scatter.10

commit v2 on v1

v2 whole, which is shorter than its diff:
```python
import functools
import math

import jax
import jax.numpy as jnp
from jax import lax
from jax.experimental import pallas as pl
from jax.experimental.pallas import tpu as pltpu
from jax.sharding import Mesh
from jax.sharding import PartitionSpec as P

HD = 128
BLK = 128
EPSILON = 1e-05
NEG_FILL = -1e30

EVERY = ("tp", "sp", "fs")
TOKENS = ("sp", "fs")
SNAKE = (0, 2, 4, 6, 7, 5, 3, 1)
PLACES = len(SNAKE)
SHIFTS = (0, -1, 1, -2, 2, -3, 3, 4)
PARTS = ((0, 1), (1, 3), (3, 5), (5, 7), (7, 8))


def half(values):
    return values.astype(jnp.bfloat16)


def full(values):
    return values.astype(jnp.float32)


def dot(left, right, left_dim, right_dim, out=jnp.float32):
    return lax.dot_general(
        left, right, (((left_dim,), (right_dim,)), ((), ())), preferred_element_type=jnp.float32
    ).astype(out)


def fence(*values):
    return lax.optimization_barrier(values)


def normalize(values):
    center = values - jnp.mean(values, axis=-1, keepdims=True)
    spread = jnp.mean(center * center, axis=-1, keepdims=True)
    scale = lax.rsqrt(spread + EPSILON)
    return center * scale, scale


def normalize_back(normed, scale, grad):
    return scale * (
        grad
        - jnp.mean(grad, axis=-1, keepdims=True)
        - normed * jnp.mean(grad * normed, axis=-1, keepdims=True)
    )


def hop(upward, downward):
    up = [(SNAKE[i], SNAKE[(i + 1) % PLACES]) for i in range(PLACES)]
    down = [(b, a) for a, b in up]
    return lax.ppermute(upward, "tp", up), lax.ppermute(downward, "tp", down)


def last_hop(below, above):
    n = below.shape[0] // 2
    return hop(below[:n], above[n:])


def first_sum(part, low, high):
    below, above = jnp.split(part, 2)
    n = below.shape[0] // 2
    upward = jnp.concatenate([half(full(above[:n]) + full(low)), above[n:]])
    downward = jnp.concatenate([below[:n], half(full(below[n:]) + full(high))])
    return upward, downward


def next_sum(part, upward, downward):
    below, above = jnp.split(part, 2)
    return half(full(above) + full(upward)), half(full(below) + full(downward))


def last_sum(part, upward, downward):
    return full(part) + full(upward) + full(downward)


def join(pair):
    return jnp.concatenate(pair)


def put(buffer, part, index, local_rows):
    return lax.dynamic_update_slice_in_dim(buffer, part, PARTS[index][0] * local_rows, 0)


def bits_of(names):
    return [
        (name, 1 << bit, lax.axis_size(name))
        for name in reversed(names)
        for bit in range(lax.axis_size(name).bit_length() - 1)
    ]


def swap(values, name, bit, size):
    return lax.ppermute(values, name, [(i, i ^ bit) for i in range(size)])


def gather_small(values):
    values = values[None]
    for name, bit, size in bits_of(EVERY):
        other = swap(values, name, bit, size)
        first = (lax.axis_index(name) & bit) == 0
        values = jnp.concatenate([jnp.where(first, values, other), jnp.where(first, other, values)])
    return values


def sum_small(values):
    for name, bit, size in bits_of(EVERY):
        values = values.reshape(-1, 2, values.shape[-1])
        low, high = values[:, 0], values[:, 1]
        first = (lax.axis_index(name) & bit) == 0
        other = swap(jnp.where(first, high, low), name, bit, size)
        values = jnp.where(first, low, high) + other
    return values[0]


def by_place(rows, groups):
    n, width = rows.shape
    part = width // groups // PLACES
    rows = half(rows).reshape(n, groups, PLACES, part).transpose(2, 0, 1, 3)
    return rows.reshape(PLACES, n, groups * part)


def exchange(pieces):
    return lax.all_to_all(pieces, "tp", split_axis=0, concat_axis=0, tiled=True)


def rows_product(lefts, rights, tile, name):
    count, out_rows, out_cols = len(lefts), lefts[0].shape[1], rights[0].shape[1]

    def body(*refs):
        total = None
        for left, right in zip(refs[:count], refs[count : 2 * count], strict=True):
            term = lax.dot_general(
                left[...],
                right[...],
                (((0,), (0,)), ((), ())),
                preferred_element_type=jnp.float32,
            )
            total = term if total is None else total + term
        refs[2 * count][...] = half(total)

    return pl.pallas_call(
        body,
        grid=(out_rows // tile,),
        in_specs=[pl.BlockSpec((v.shape[0], tile), lambda i: (0, i)) for v in lefts]
        + [pl.BlockSpec(v.shape, lambda i: (0, 0)) for v in rights],
        out_specs=pl.BlockSpec((tile, out_cols), lambda i: (i, 0)),
        out_shape=jax.ShapeDtypeStruct((out_rows, out_cols), jnp.bfloat16),
        compiler_params=pltpu.CompilerParams(vmem_limit_bytes=40 << 20),
        cost_estimate=pl.CostEstimate(flops=1 << 20, bytes_accessed=1 << 20, transcendentals=0),
        name=name,
    )(*lefts, *rights)


def score_rows(keys, queries, slope, first_block, query_pos, query_seg, key_pos, key_seg):
    scores = dot(keys, queries, 1, 1)
    count = queries.shape[0] // BLK
    lane = lax.broadcasted_iota(jnp.int32, (1, queries.shape[0]), 1)
    down = lax.broadcasted_iota(jnp.int32, (BLK, queries.shape[0]), 0)
    ahead = down - lax.rem(lane, BLK)
    slant = slope * full(down)
    tiles = []
    for j in range(keys.shape[0] // BLK):
        limit = jnp.zeros((1, queries.shape[0]), jnp.int32)
        for i in range(count):
            block = first_block * count + i
            seen = (key_seg[j] == 0) | (key_seg[j] == query_seg[block])
            here = jnp.where(seen, query_pos[block] - key_pos[j], -BLK)
            limit = jnp.where(lane >= i * BLK, here, limit)
        tile = scores[j * BLK : (j + 1) * BLK] * (1.0 / math.sqrt(HD))
        tile = tile + (slant + slope * full(key_pos[j]))
        tiles.append(jnp.where(ahead <= limit, tile, NEG_FILL))
    return jnp.concatenate(tiles)


def attend_body(
    query_pos, query_seg, key_pos, key_seg, slopes, query, key, value, attended, level, value_t
):
    @pl.when(pl.program_id(1) == 0)
    def turn():
        value_t[...] = half(full(value[...]).T)

    scores = score_rows(
        key[...],
        query[...],
        slopes[pl.program_id(0)],
        pl.program_id(1),
        query_pos,
        query_seg,
        key_pos,
        key_seg,
    )
    top = jnp.max(scores, axis=0, keepdims=True)
    expon = jnp.exp(scores - top)
    total = jnp.sum(expon, axis=0, keepdims=True)
    probs = half(expon * (1.0 / total))
    attended[...] = half(dot(value_t[...], probs, 1, 0).T)
    level[...] = (top + jnp.log(total))[None]


def attend_back_body(
    my_heads,
    split,
    query_pos,
    query_seg,
    key_pos,
    key_seg,
    slopes,
    query,
    key,
    value,
    grad,
    level,
    *rest,
):
    d_query, d_keys = (rest[0], rest[1]) if split else (rest[0], rest[0])
    key_t, key_acc, value_acc = rest[-3:]
    head, block = pl.program_id(0), pl.program_id(1)
    rows = query.shape[0]
    scale = 1.0 / math.sqrt(HD)

    def columns(place):
        return pl.ds(pl.multiple_of((place * my_heads + head) * HD, HD), HD)

    @pl.when(block == 0)
    def begin():
        key_t[...] = half(full(key[...]).T)
        key_acc[...] = jnp.zeros_like(key_acc)
        value_acc[...] = jnp.zeros_like(value_acc)

    scores = score_rows(
        key[...], query[...], slopes[head], block, query_pos, query_seg, key_pos, key_seg
    )
    probs = jnp.exp(scores - level[0])
    d_probs = dot(value[...], grad[...], 1, 1)
    delta = jnp.sum(probs * d_probs, axis=0, keepdims=True)
    d_scores = half(probs * (d_probs - delta))
    turned = (dot(key_t[...], d_scores, 1, 0) * scale).T
    d_query[pl.ds(pl.multiple_of(block * rows, rows), rows), columns(0)] = half(turned)
    key_acc[...] += dot(d_scores, query[...], 1, 0)
    value_acc[...] += dot(half(probs), grad[...], 1, 0)

    @pl.when(block == pl.num_programs(1) - 1)
    def end():
        shift = 0 if split else 1
        d_keys[:, columns(shift)] = half(key_acc[...] * scale)
        d_keys[:, columns(shift + 1)] = half(value_acc[...])


def attention(blocks, slopes, query, keys, first, grad=None, level=None):
    my_heads = slopes.shape[0]
    rows, total = query.shape[0], keys.shape[0]
    step = 256 if total <= 1024 else BLK
    columns = my_heads * HD
    scalars = pl.BlockSpec(memory_space=pltpu.SMEM)
    of_query = pl.BlockSpec((step, HD), lambda h, i: (i, h))
    of_level = pl.BlockSpec((1, 1, step), lambda h, i: (h, 0, i))
    in_specs = [scalars] * 5 + [
        of_query,
        pl.BlockSpec((total, HD), lambda h, i: (0, first + h)),
        pl.BlockSpec((total, HD), lambda h, i: (0, first + my_heads + h)),
    ]
    settings = {
        "grid": (my_heads, rows // step),
        "compiler_params": pltpu.CompilerParams(vmem_limit_bytes=48 << 20),
        "cost_estimate": pl.CostEstimate(
            flops=(4 if grad is None else 10) * rows * total * columns,
            bytes_accessed=32 << 20,
            transcendentals=my_heads * rows * total,
        ),
    }
    if grad is None:
        return pl.pallas_call(
            attend_body,
            in_specs=in_specs,
            out_specs=[of_query, of_level],
            out_shape=[
                jax.ShapeDtypeStruct((rows, columns), jnp.bfloat16),
                jax.ShapeDtypeStruct((my_heads, 1, rows), jnp.float32),
            ],
            scratch_shapes=[pltpu.VMEM((HD, total), jnp.bfloat16)],
            name="attend",
            **settings,
        )(*blocks, slopes, query, keys, keys)
    split = query is not keys
    shapes = [(rows, columns), (total, 2 * columns)] if split else [(rows, 3 * columns)]
    return pl.pallas_call(
        functools.partial(attend_back_body, my_heads, split),
        in_specs=in_specs + [of_query, of_level],
        out_specs=[pl.BlockSpec(shape, lambda h, i: (0, 0)) for shape in shapes],
        out_shape=[jax.ShapeDtypeStruct(shape, jnp.bfloat16) for shape in shapes],
        scratch_shapes=[
            pltpu.VMEM((HD, total), jnp.bfloat16),
            pltpu.VMEM((total, HD), jnp.float32),
            pltpu.VMEM((total, HD), jnp.float32),
        ],
        name="attend_back",
        **settings,
    )(*blocks, slopes, query, keys, keys, grad, level)


def products(parts, matrix, name):
    count, tile = len(parts), 512

    def body(*refs):
        for part, out in zip(refs[:count], refs[count + 1 :], strict=True):
            out[...] = dot(part[...], refs[count][...], 1, 1, jnp.bfloat16)

    return pl.pallas_call(
        body,
        grid=(matrix.shape[0] // tile,),
        in_specs=[pl.BlockSpec(v.shape, lambda i: (0, 0)) for v in parts]
        + [pl.BlockSpec((tile, matrix.shape[1]), lambda i: (i, 0))],
        out_specs=[pl.BlockSpec((v.shape[0], tile), lambda i: (0, i)) for v in parts],
        out_shape=[
            jax.ShapeDtypeStruct((v.shape[0], matrix.shape[0]), jnp.bfloat16) for v in parts
        ],
        compiler_params=pltpu.CompilerParams(vmem_limit_bytes=40 << 20),
        cost_estimate=pl.CostEstimate(flops=1 << 20, bytes_accessed=1 << 20, transcendentals=0),
        name=name,
    )(*parts, matrix)


def gather_rows(rows):
    rows = lax.all_gather(rows, TOKENS, axis=1, tiled=True)
    return rows.reshape(-1, rows.shape[2])


def from_places(grad, groups):
    places, n, width = grad.shape
    grad = grad.reshape(places, n, groups, width // groups).transpose(1, 2, 0, 3)
    return full(grad.reshape(n, places * width))


def on_device(
    tokens,
    ln1_gain,
    ln1_bias,
    w_qkv,
    b_qv,
    w_out,
    b_out,
    ln2_gain,
    ln2_bias,
    w_in,
    b_in,
    w_down,
    b_down,
    cotangent,
    block_seg,
    block_pos,
):
    sp = lax.axis_size("sp")
    fs = lax.axis_size("fs")
    devices = PLACES * sp * fs
    my_tp = lax.axis_index("tp")
    my_sp = lax.axis_index("sp")
    local_rows, width = tokens.shape[1:]
    heads = width // HD
    my_heads = heads // PLACES
    head_cols = my_heads * HD
    hidden = w_in.shape[1] // PLACES
    group_rows = PLACES * local_rows

    def buffer(columns):
        return jnp.zeros((group_rows, columns), jnp.bfloat16)

    def by_part(rows):
        return [rows[a * local_rows : b * local_rows] for a, b in PARTS]

    order = [[SNAKE[(SNAKE.index(i) + s) % PLACES] for s in SHIFTS] for i in range(PLACES)]
    sources = jnp.asarray(order, jnp.int32)[my_tp]
    picked = (sources[:, None] == jnp.arange(PLACES, dtype=jnp.int32)[None, :]).astype(jnp.int32)

    def in_order(blocks):
        blocks = jnp.sum(picked[:, :, None, None] * blocks.reshape(1, PLACES, sp, -1), axis=1)
        mine = lax.dynamic_index_in_dim(blocks, my_sp, 1, keepdims=False).reshape(-1)
        return mine, blocks.transpose(1, 0, 2).reshape(-1)

    query_seg, key_seg = in_order(block_seg[0])
    query_pos, key_pos = in_order(block_pos[0])
    blocks = (query_pos, query_seg, key_pos, key_seg)
    head_ids = my_tp * my_heads + jnp.arange(my_heads, dtype=jnp.int32)
    slopes = jnp.exp2(-8.0 * (head_ids.astype(jnp.float32) + 1.0) / heads)

    small = [ln1_gain, ln1_bias, b_out, ln2_gain, ln2_bias, b_down, b_qv, b_in]
    sizes = [v.shape[0] for v in small]
    cuts = [sum(sizes[:i]) for i in range(len(sizes) + 1)]
    own, own_cot = tokens[0], cotangent[0]

    low1, high1 = hop(own, own)
    down_slice = lax.all_gather(half(w_down), TOKENS, axis=0, tiled=True)
    small_own, qkv_pieces = fence(half(jnp.concatenate(small)), by_place(w_qkv, 3))
    qkv_pieces = exchange(qkv_pieces)
    gathered = gather_small(small_own)
    low2, high2 = hop(low1, high1)
    in_pieces = by_place(w_in, 1)
    (
        low1,
        high1,
        low2,
        high2,
        qkv_pieces,
        in_pieces,
        gathered,
        down_slice,
        w_out,
        own_cot,
    ) = fence(
        low1,
        high1,
        low2,
        high2,
        qkv_pieces,
        in_pieces,
        gathered,
        down_slice,
        w_out,
        own_cot,
    )
    gathered = full(gathered)
    gain1, bias1, out_bias, gain2, bias2, down_bias, qv_bias, in_bias = (
        gathered[:, cuts[i] : cuts[i + 1]].reshape(-1) for i in range(len(sizes))
    )
    qv_bias = lax.dynamic_slice_in_dim(qv_bias.reshape(2, width), my_tp * head_cols, head_cols, 1)
    in_bias = lax.dynamic_slice_in_dim(in_bias, my_tp * hidden, hidden)

    def norm1(rows):
        return half(normalize(full(rows))[0] * gain1 + bias1)

    in_pieces = exchange(in_pieces)
    qkv_slice = gather_rows(qkv_pieces)
    out_slice = lax.all_gather(half(w_out), TOKENS, axis=0, tiled=True)
    token_parts = [own, join((low1, high1)), join((low2, high2))]
    low3, high3 = hop(low2, high2)
    normed = [norm1(part) for part in token_parts]
    low3, high3, own_cot, *normed = fence(low3, high3, own_cot, *normed)
    low4, high4 = last_hop(low3, high3)
    token_parts.append(join((low3, high3)))
    normed.append(norm1(token_parts[3]))
    low4, high4, own_cot, in_pieces, qkv_slice, *normed = fence(
        low4, high4, own_cot, in_pieces, qkv_slice, *normed
    )

    cot_low1, cot_high1 = hop(own_cot, own_cot)
    token_parts.append(join((low4, high4)))
    normed.append(norm1(token_parts[4]))
    blank = jnp.zeros((head_cols,), jnp.float32)
    qkv_bias = jnp.concatenate([qv_bias[0], blank, qv_bias[1]])
    mixed = jnp.concatenate([half(dot(part, qkv_slice, 1, 0) + qkv_bias) for part in normed])
    mixed, cot_low1, cot_high1, out_slice = fence(mixed, cot_low1, cot_high1, out_slice)
    in_slice = gather_rows(in_pieces)
    cot_low2, cot_high2 = hop(cot_low1, cot_high1)
    keys = mixed
    if sp > 1:
        keys = lax.all_gather(mixed[:, head_cols:], "sp", axis=0, tiled=True)
    first_key = my_heads if sp == 1 else 0
    attended, level = attention(blocks, slopes, mixed, keys, first_key)
    attended, cot_low2, cot_high2 = fence(attended, cot_low2, cot_high2)

    attended_parts = by_part(attended)
    branch_parts = [dot(attended_parts[i], out_slice, 1, 0, jnp.bfloat16) for i in range(5)]
    branch_low, branch_high = hop(*jnp.split(branch_parts[4], 2))
    cot_low3, cot_high3 = hop(cot_low2, cot_high2)
    branch_low, branch_high, cot_low3, cot_high3, *branch_parts = fence(
        branch_low, branch_high, cot_low3, cot_high3, *branch_parts
    )
    up, down = hop(*first_sum(branch_parts[3], branch_low, branch_high))
    cot_low4, cot_high4 = last_hop(cot_low3, cot_high3)
    up, down, cot_low4, cot_high4, in_slice = fence(up, down, cot_low4, cot_high4, in_slice)
    up, down = hop(*next_sum(branch_parts[2], up, down))
    cot_parts = [own_cot, join((cot_low1, cot_high1)), join((cot_low2, cot_high2))]
    cot_parts += [join((cot_low3, cot_high3)), join((cot_low4, cot_high4))]
    up, down, *cot_parts = fence(up, down, *cot_parts)
    up, down = fence(*hop(*next_sum(branch_parts[1], up, down)))
    residual = full(own) + last_sum(branch_parts[0], up, down) + out_bias

    own_normed2, scale2 = normalize(residual)
    second = half(own_normed2 * gain2 + bias2)
    second_parts, act_parts, d_pre_parts, d_second_parts, ffn_parts = [second], [], [], [], []
    low, high = second, second
    for index in range(5):
        if index < 3:
            new_low, new_high = hop(low, high)
        elif index == 3:
            new_low, new_high = last_hop(low, high)
        if index:
            second_parts.append(join((low, high)))
        pre_act = dot(second_parts[index], in_slice, 1, 0) + in_bias
        act, gelu_back = jax.vjp(lambda v: jax.nn.gelu(v, approximate=True), pre_act)
        act_parts.append(half(act))
        d_pre = half(gelu_back(dot(cot_parts[index], down_slice, 1, 1))[0])
        d_pre_parts.append(d_pre)
        d_second_parts.append(dot(d_pre, in_slice, 1, 1, jnp.bfloat16))
        made = [act_parts, d_pre_parts, d_second_parts]
        if index < 3:
            ffn_parts.append(dot(act_parts[index], down_slice, 1, 0, jnp.bfloat16))
            made.append(ffn_parts)
        if index < 4:
            low, high, *held = fence(new_low, new_high, *[parts[index] for parts in made])
            for parts, value in zip(made, held, strict=True):
                parts[index] = value

    low, high = hop(*jnp.split(d_second_parts[4], 2))
    ffn_parts += [dot(act, down_slice, 1, 0, jnp.bfloat16) for act in act_parts[3:]]
    low, high, d_pre_parts[4], act_parts[4], *ffn_parts = fence(
        low, high, d_pre_parts[4], act_parts[4], *ffn_parts
    )
    up, down = hop(*first_sum(d_second_parts[3], low, high))
    out_up, out_down = hop(*jnp.split(ffn_parts[4], 2))
    grad_in = rows_product(second_parts, d_pre_parts, 512, "grad_in")
    grad_in = grad_in.reshape(PLACES, -1, hidden)
    up, down, out_up, out_down, grad_in = fence(up, down, out_up, out_down, grad_in)
    grad_in = lax.psum_scatter(grad_in, TOKENS, scatter_dimension=1, tiled=True)
    up, down = hop(*next_sum(d_second_parts[2], up, down))
    out_up, out_down = hop(*first_sum(ffn_parts[3], out_up, out_down))
    up, down, out_up, out_down, act_parts[4] = fence(up, down, out_up, out_down, act_parts[4])
    up, down = hop(*next_sum(d_second_parts[1], up, down))
    out_up, out_down = hop(*next_sum(ffn_parts[2], out_up, out_down))
    grad_down = rows_product(act_parts, cot_parts, 256, "grad_down")
    grad_b_in = sum(jnp.sum(full(part), axis=0) for part in d_pre_parts)
    up, down, out_up, out_down, grad_down, grad_b_in = fence(
        up, down, out_up, out_down, grad_down, grad_b_in
    )
    grad_down = lax.psum_scatter(grad_down, TOKENS, scatter_dimension=0, tiled=True)
    d_second = last_sum(d_second_parts[0], up, down)

    d_residual = full(own_cot) + normalize_back(own_normed2, scale2, d_second * gain2)
    d_branch = half(d_residual)
    low, high = hop(d_branch, d_branch)
    out_up, out_down = hop(*next_sum(ffn_parts[1], out_up, out_down))
    low, high, out_up, out_down = fence(low, high, out_up, out_down)
    d_branch_parts, d_attended = [d_branch], [dot(d_branch, out_slice, 1, 1, jnp.bfloat16)]
    for index in range(1, 5):
        d_branch_parts.append(join((low, high)))
        d_attended.append(dot(d_branch_parts[index], out_slice, 1, 1, jnp.bfloat16))
        if index < 3:
            low, high = hop(low, high)
            low, high, grad_in, d_attended[index] = fence(low, high, grad_in, d_attended[index])
        elif index == 3:
            low, high = last_hop(low, high)
            low, high, grad_in, d_attended[index] = fence(low, high, grad_in, d_attended[index])
            grad_in = exchange(grad_in)

    d_attended = jnp.concatenate(d_attended)
    grads = attention(blocks, slopes, mixed, keys, first_key, d_attended, level)
    if sp == 1:
        (d_mixed,) = grads
    else:
        d_keys = half(lax.psum_scatter(full(grads[1]), "sp", scatter_dimension=0, tiled=True))
        d_mixed = jnp.concatenate([grads[0], d_keys], axis=1)
    d_mixed, d_branch_parts[4], grad_down = fence(d_mixed, d_branch_parts[4], grad_down)

    mixed_parts = by_part(d_mixed)
    far = dot(mixed_parts[4], qkv_slice, 1, 1, jnp.bfloat16)
    low, high = hop(*jnp.split(far, 2))
    near = dot(mixed_parts[3], qkv_slice, 1, 1, jnp.bfloat16)
    grad_qkv = rows_product(normed, mixed_parts, 512, "grad_qkv")
    grad_qkv = grad_qkv.reshape(PLACES, -1, 3 * head_cols)
    low, high, grad_qkv, near, grad_in = fence(low, high, grad_qkv, near, grad_in)
    grad_qkv = lax.psum_scatter(grad_qkv, TOKENS, scatter_dimension=1, tiled=True)
    up, down = hop(*first_sum(near, low, high))
    d_normed = products(mixed_parts[:3], qkv_slice, "d_normed")
    up, down, attended_parts[4], *d_normed = fence(up, down, attended_parts[4], *d_normed)
    up, down = hop(*next_sum(d_normed[2], up, down))
    grad_out = rows_product(attended_parts, d_branch_parts, 128, "grad_out")
    up, down, grad_out = fence(up, down, grad_out)
    grad_qkv, grad_out = fence(grad_qkv, grad_out)
    grad_out = lax.psum_scatter(grad_out, TOKENS, scatter_dimension=0, tiled=True)
    up, down = hop(*next_sum(d_normed[1], up, down))
    up, down, grad_qkv, grad_in, grad_down, out_up, out_down = fence(
        up, down, grad_qkv, grad_in, grad_down, out_up, out_down
    )
    grad_qkv = exchange(grad_qkv)
    d_normed_own = last_sum(d_normed[0], up, down)
    own_normed1, scale1 = normalize(full(own))
    grad_tokens = d_residual + normalize_back(own_normed1, scale1, d_normed_own * gain1)
    grad_w_in = from_places(grad_in, 1)
    grad_w_down = full(grad_down)
    output = half(residual + last_sum(ffn_parts[0], out_up, out_down) + down_bias)

    def placed(values, whole):
        start = my_tp * values.shape[-1]
        blank = jnp.zeros(values.shape[:-1] + (whole,), jnp.float32)
        return lax.dynamic_update_slice_in_dim(blank, values, start, values.ndim - 1)

    mixed_sum = jnp.sum(full(d_mixed), axis=0)
    grad_b_qv = placed(
        jnp.stack([mixed_sum[:head_cols], mixed_sum[2 * head_cols :]]), width
    )
    partials = [
        jnp.sum(d_normed_own * own_normed1, axis=0),
        jnp.sum(d_normed_own, axis=0),
        jnp.sum(full(d_branch), axis=0),
        jnp.sum(d_second * own_normed2, axis=0),
        jnp.sum(d_second, axis=0),
        jnp.sum(full(own_cot), axis=0),
        grad_b_qv.reshape(-1),
        placed(grad_b_in, PLACES * hidden),
    ]
    stacked = jnp.concatenate([v.reshape(devices, -1) for v in partials], axis=1)
    summed = sum_small(stacked)
    grad_w_out = full(grad_out)
    grad_w_qkv = from_places(grad_qkv, 3)
    g_gain1, g_bias1, g_b_out, g_gain2, g_bias2, g_b_down, g_b_qv, g_b_in = (
        summed[cuts[i] : cuts[i + 1]] for i in range(len(sizes))
    )
    return (
        output[None],
        grad_tokens[None],
        g_gain1,
        g_bias1,
        grad_w_qkv,
        g_b_qv,
        grad_w_out,
        g_b_out,
        g_gain2,
        g_bias2,
        grad_w_in,
        g_b_in,
        grad_w_down,
        g_b_down,
    )


def solution(mesh):
    ctx, fs = mesh.shape["ctx"], mesh.shape["fsdp"]
    inner = Mesh(mesh.devices.reshape(PLACES, ctx // PLACES, fs), EVERY)
    rows = P("fs", ("tp", "sp"), None)
    vector, matrix, blocks = P(EVERY), P(EVERY, None), P("fs", None)
    kinds = (
        rows,
        vector,
        vector,
        matrix,
        vector,
        matrix,
        vector,
        vector,
        vector,
        matrix,
        vector,
        matrix,
        vector,
    )
    return jax.shard_map(
        on_device,
        mesh=inner,
        in_specs=kinds + (rows, blocks, blocks),
        out_specs=(rows,) + kinds,
        check_vma=False,
    )
```

time: 757 us -> 556 us (0.73)
  waiting for transfers between devices: 329 us -> 179 us
  blocking collectives: 73.4 us -> 0 us
  matrix products: 101 us -> 52.1 us
  Pallas kernels: 0 us -> 45.5 us
  starting transfers between devices: 87.2 us -> 122 us
  other arithmetic: 55 us -> 65.9 us
  between operations: 27 us -> 16.7 us
    reduce_scatter x4, waiting for transfers between devices: 94.4 us -> 0.03 us  [the longest x1 0.02 us: on_device(): lax.psum_scatter(grad_qkv, TOKENS, scatter_dimension=1, tiled=True)]
    all_gather x1 -> x0, blocking collectives: 48.1 us -> none  [on_device(): gathered = lax.all_gather(jnp.concatenate(small), EVERY, axis=0, tiled=True)]
    pallas_call x0 -> x7, Pallas kernels: none -> 45.5 us  [the longest x4 21 us: rows_product(): pl.pallas_call(body, grid=(out_rows // tile,), in_specs=[pl.BlockSpec((v....]
    unnamed x10 -> x8, waiting for transfers between devices: 39 us -> 0.14 us
    dynamic_update_slice x35 -> x0, local copies, waits for them, and re-layouts: 29.3 us -> none  [put(): lax.dynamic_update_slice_in_dim(out, chunk, self.index(shift) * n + begin...]
    dot_general x12 -> x37, matrix products: 80.5 us -> 52.1 us  [dot(): lax.dot_general(left, right, (((left_dim,), (right_dim,)), ((), ())), pre...]
    ppermute x64 -> x74, starting transfers between devices: 70.2 us -> 96.8 us  [the longest x64 81 us: hop(): return (lax.ppermute(upward, 'tp', up), lax.ppermute(downward, 'tp', down))]
    all_to_all x1 -> x0, blocking collectives: 25.3 us -> none  [columns_in(): lax.all_to_all(rows.reshape(n, groups, tp, part), 'tp', split_axis=2, con...]
  transfers between devices with their start and end apart: 76 -> 86, of which waited for: 47 -> 42; matrix products, arithmetic and copies ran while one was open for 26% -> 27% of each run, Pallas kernels for 0% -> 8%
where the time goes in v2:
time: 556 us; the launch traced here: 550 us
  waiting for transfers between devices  179 us (32%)
  starting transfers between devices  122 us (22%)
  local copies, waits for them, and re-layouts  68.1 us (12%)
  other arithmetic  65.9 us (12%)
  matrix products  52.1 us (9%)
  Pallas kernels  45.5 us (8%)
  between operations  16.7 us (3%)
    ppermute x64, waiting for transfers between devices, hop(): return (lax.ppermute(upward, 'tp', up), lax.ppermute(downward, 'tp', down))  155 us
    ppermute x64, starting transfers between devices, hop(): return (lax.ppermute(upward, 'tp', up), lax.ppermute(downward, 'tp', down))  81 us
    dot_general x37, matrix products, dot(): lax.dot_general(left, right, (((left_dim,), (right_dim,)), ((), ())), pre...  52.1 us
    unnamed x277, local copies, waits for them, and re-layouts  29.9 us
    convert_element_type x21, other arithmetic, half(): return values.astype(jnp.bfloat16)  27 us
    all_to_all x4, starting transfers between devices, exchange(): return lax.all_to_all(pieces, 'tp', split_axis=0, concat_axis=0, tiled=True)  25.3 us
    ppermute x10, waiting for transfers between devices, swap(): return lax.ppermute(values, name, [(i, i ^ bit) for i in range(size)])  24 us
    pallas_call x4, Pallas kernels, rows_product(): pl.pallas_call(body, grid=(out_rows // tile,), in_specs=[pl.BlockSpec((v....  21 us
  transfers between devices with their start and end apart: 86, of which 42 were waited for; matrix products, arithmetic and copies ran while one was open for 27% of the time, Pallas kernels for 8%

profile of v2, /device:TPU:8, one launch (start us, length us, event | category | flops | bytes accessed | tf_op | source)
XLA Modules:
  0.0 550.2 jit_solution(8635755260435041014)
XLA Ops:
  17.7 6.3 %all-to-all-start = ((bf16[8,64,768]{2,1,0:T(8,128)(2,1)}), bf16[8,64,768]{2,1,0:T(8,128)(2,1)}, u32[]{:S(2)}, u32[]{:S(2)}) async-start(bf16[8,64,768]{2,1,0:T(8,128)(2,1)} %reshape.409), calls=%async_computation | async-start | bytes 1572864 | tf_op jit(solution)/shard_map/all_to_all | solution.py:133
  37.7 5.7 %collective-permute-done.7 = bf16[8,768]{1,0:T(8,128)(2,1)S(1)} collective-permute-done((bf16[8,768]{1,0:T(8,128)(2,1)S(1)}, bf16[8,768]{1,0:T(8,128)(2,1)S(1)}, u32[]{:S(2)}, u32[]{:S(2)}) %collective-permute-start.7) | collective-permute-done | bytes 12320 | tf_op jit(solution)/shard_map/ppermute | solution.py:103
  48.9 8.7 %collective-permute-done.8 = bf16[16,768]{1,0:T(8,128)(2,1)S(1)} collective-permute-done((bf16[16,768]{1,0:T(8,128)(2,1)S(1)}, bf16[16,768]{1,0:T(8,128)(2,1)S(1)}, u32[]{:S(2)}, u32[]{:S(2)}) %collective-permute-start.8) | collective-permute-done | bytes 24608 | tf_op jit(solution)/shard_map/ppermute | solution.py:103
  66.4 6.0 %all-to-all-start.1 = ((bf16[8,64,1024]{2,1,0:T(8,128)(2,1)}), bf16[8,64,1024]{2,1,0:T(8,128)(2,1)}, u32[]{:S(2)}, u32[]{:S(2)}) async-start(bf16[8,64,1024]{2,1,0:T(8,128)(2,1)} %copy.104), calls=%async_computation.1 | async-start | bytes 2097152 | tf_op jit(solution)/shard_map/all_to_all | solution.py:133
  83.6 19.0 %collective-permute-done.12 = bf16[64,2048]{1,0:T(8,128)(2,1)S(1)} collective-permute-done((bf16[64,2048]{1,0:T(8,128)(2,1)S(1)}, bf16[64,2048]{1,0:T(8,128)(2,1)S(1)}, u32[]{:S(2)}, u32[]{:S(2)}) %collective-permute-start.12) | collective-permute-done | bytes 262176 | tf_op jit(solution)/shard_map/ppermute | solution.py:61
  122.5 9.4 %attend.1 = (bf16[1024,256]{1,0:T(8,128)(2,1)S(1)}, f32[2,1,1024]{2,1,0:T(1,128)S(1)}) custom-call(s32[8]{0:T(128)S(1)} %get-tuple-element.325.query_pos.key_pos, s32[8]{0:T(128)S(1)} %get-tuple-element.324.query_seg.key_seg, s32[8]{0:T(128)S(1)} %get-tuple-element.325.query_pos.key_pos, s32[8]{0:T(128)S(1)} %get-tuple-element.324.query_seg.key_seg, ...), custom_call_target="tpu_custom_call" | custom-call | flops 1073741824 | bytes 33554432 | tf_op jit(solution)/shard_map/attend/pallas_call | solution.py:282
  141.6 7.5 %collective-permute-done.19 = bf16[128,2048]{1,0:T(8,128)(2,1)S(1)} collective-permute-done((bf16[128,2048]{1,0:T(8,128)(2,1)}, bf16[128,2048]{1,0:T(8,128)(2,1)S(1)}, u32[]{:S(2)}, u32[]{:S(2)}) %collective-permute-start.19) | collective-permute-done | bytes 524320 | tf_op jit(solution)/shard_map/ppermute | solution.py:61
  158.2 6.6 %copy.106 = bf16[8,256,1024]{2,1,0:T(8,128)(2,1)} copy(bf16[8,256,1024]{2,0,1:T(8,128)(2,1)} %all-gather.11.cloned.1.call-done) | data formatting | bytes 8388608 | tf_op jit(solution)/shard_map/all_gather | solution.py:334
  183.2 12.7 %collective-permute-start.27 = (bf16[128,2048]{1,0:T(8,128)(2,1)}, bf16[128,2048]{1,0:T(8,128)(2,1)}, u32[]{:S(2)}, u32[]{:S(2)}) collective-permute-start(bf16[128,2048]{1,0:T(8,128)(2,1)} %get-tuple-element.367), channel_id=1, source_target_pairs={{0,8},{8,16},{16,24},{24,28},{28,20},{20,12},{12,4},{4,0},{1,9},{9... | collective-permute-start | bytes 1572872 | tf_op jit(solution)/shard_map/ppermute | solution.py:61
  196.2 8.4 %collective-permute-done.27 = bf16[128,2048]{1,0:T(8,128)(2,1)} collective-permute-done((bf16[128,2048]{1,0:T(8,128)(2,1)}, bf16[128,2048]{1,0:T(8,128)(2,1)}, u32[]{:S(2)}, u32[]{:S(2)}) %collective-permute-start.27) | collective-permute-done | bytes 524320 | tf_op jit(solution)/shard_map/ppermute | solution.py:61
  216.9 5.3 collective-permute-done.30
  277.5 6.5 %grad_in.1 = bf16[2048,1024]{1,0:T(8,128)(2,1)S(1)} custom-call(bf16[128,2048]{1,0:T(8,128)(2,1)S(1)} %add_convert_fusion.13.refs_0_, bf16[256,2048]{1,0:T(8,128)(2,1)S(1)} %constant_dynamic-update-slice_fusion.refs_1_, bf16[256,2048]{1,0:T(8,128)(2,1)S(1)} %constant_dynamic-update-slice_fusion.2.refs_2_, ...), custom_call_target="tpu_custom_call" | custom-call | flops 1048576 | bytes 1048576 | tf_op jit(solution)/shard_map/grad_in/pallas_call | solution.py:151
  286.0 5.8 %collective-permute-done.42 = bf16[64,2048]{1,0:T(8,128)(2,1)S(1)} collective-permute-done((bf16[64,2048]{1,0:T(8,128)(2,1)S(1)}, bf16[64,2048]{1,0:T(8,128)(2,1)S(1)}, u32[]{:S(2)}, u32[]{:S(2)}) %collective-permute-start.42) | collective-permute-done | bytes 262176 | tf_op jit(solution)/shard_map/ppermute | solution.py:61
  301.3 7.3 %collective-permute-done.45 = bf16[128,2048]{1,0:T(8,128)(2,1)S(1)} collective-permute-done((bf16[128,2048]{1,0:T(8,128)(2,1)S(1)}, bf16[128,2048]{1,0:T(8,128)(2,1)S(1)}, u32[]{:S(2)}, u32[]{:S(2)}) %collective-permute-start.45) | collective-permute-done | bytes 524320 | tf_op jit(solution)/shard_map/ppermute | solution.py:61
  311.0 8.9 %collective-permute-done.43 = bf16[128,2048]{1,0:T(8,128)(2,1)S(1)} collective-permute-done((bf16[128,2048]{1,0:T(8,128)(2,1)S(1)}, bf16[128,2048]{1,0:T(8,128)(2,1)S(1)}, u32[]{:S(2)}, u32[]{:S(2)}) %collective-permute-start.43) | collective-permute-done | bytes 524320 | tf_op jit(solution)/shard_map/ppermute | solution.py:61
  330.8 6.5 %grad_down.1 = bf16[1024,2048]{1,0:T(8,128)(2,1)S(1)} custom-call(bf16[128,1024]{1,0:T(8,128)(2,1)S(1)} %copy-done.57, bf16[256,1024]{1,0:T(8,128)(2,1)S(1)} %copy-done.61, bf16[256,1024]{1,0:T(8,128)(2,1)S(1)} %copy-done.63, bf16[256,1024]{1,0:T(8,128)(2,1)S(1)} %copy-done.65, bf16[128,1024]{1,0:T(8,128)(2,1)S(1)} %copy-done.59, ...), custom_call_target="tpu_custom_call" | custom-call | flops 1048576 | bytes 1048576 | tf_op jit(solution)/shard_map/grad_down/pallas_call | solution.py:151
  339.3 6.3 %collective-permute-done.48 = bf16[128,2048]{1,0:T(8,128)(2,1)} collective-permute-done((bf16[128,2048]{1,0:T(8,128)(2,1)}, bf16[128,2048]{1,0:T(8,128)(2,1)}, u32[]{:S(2)}, u32[]{:S(2)}) %collective-permute-start.48) | collective-permute-done | bytes 524320 | tf_op jit(solution)/shard_map/ppermute | solution.py:61
  366.3 9.1 %collective-permute-done.54 = bf16[128,2048]{1,0:T(8,128)(2,1)S(1)} collective-permute-done((bf16[128,2048]{1,0:T(8,128)(2,1)S(1)}, bf16[128,2048]{1,0:T(8,128)(2,1)S(1)}, u32[]{:S(2)}, u32[]{:S(2)}) %collective-permute-start.54) | collective-permute-done | bytes 524320 | tf_op jit(solution)/shard_map/ppermute | solution.py:61
  380.2 8.3 %collective-permute-done.55 = bf16[128,2048]{1,0:T(8,128)(2,1)S(1)} collective-permute-done((bf16[128,2048]{1,0:T(8,128)(2,1)S(1)}, bf16[128,2048]{1,0:T(8,128)(2,1)S(1)}, u32[]{:S(2)}, u32[]{:S(2)}) %collective-permute-start.55) | collective-permute-done | bytes 524320 | tf_op jit(solution)/shard_map/ppermute | solution.py:61
  394.7 14.4 %collective-permute-done.57 = bf16[128,2048]{1,0:T(8,128)(2,1)S(1)} collective-permute-done((bf16[128,2048]{1,0:T(8,128)(2,1)}, bf16[128,2048]{1,0:T(8,128)(2,1)S(1)}, u32[]{:S(2)}, u32[]{:S(2)}) %collective-permute-start.57) | collective-permute-done | bytes 524320 | tf_op jit(solution)/shard_map/ppermute | solution.py:61
  430.2 11.6 %attend_back.1 = bf16[1024,768]{1,0:T(8,128)(2,1)S(1)} custom-call(s32[8]{0:T(128)S(1)} %get-tuple-element.325.query_pos.key_pos, s32[8]{0:T(128)S(1)} %get-tuple-element.324.query_seg.key_seg, s32[8]{0:T(128)S(1)} %get-tuple-element.325.query_pos.key_pos, s32[8]{0:T(128)S(1)} %get-tuple-element.324.query_seg.key_seg, f32[2]{0:T(128)S(1)} %multiply_exponential_fusion.slopes, ...), custom_call_target="tpu_custom_call" | custom-call | flops 2684354560 | bytes 33554432 | tf_op jit(solution)/shard_map/attend_back/pallas_call | solution.py:296
  447.7 5.2 grad_qkv.1
  495.3 6.8 %collective-permute-done.68 = bf16[128,2048]{1,0:T(8,128)(2,1)S(1)} collective-permute-done((bf16[128,2048]{1,0:T(8,128)(2,1)}, bf16[128,2048]{1,0:T(8,128)(2,1)S(1)}, u32[]{:S(2)}, u32[]{:S(2)}) %collective-permute-start.68) | collective-permute-done | bytes 524320 | tf_op jit(solution)/shard_map/ppermute | solution.py:61
  504.0 8.3 %all-to-all-start.3 = ((bf16[8,64,768]{2,1,0:T(8,128)(2,1)}), bf16[8,64,768]{2,1,0:T(8,128)(2,1)S(1)}, u32[]{:S(2)}, u32[]{:S(2)}) async-start(bf16[8,64,768]{2,1,0:T(8,128)(2,1)} %reduce-scatter.9.cloned.1.call-done), calls=%async_computation.6 | async-start | bytes 1572864 | tf_op jit(solution)/shard_map/all_to_all | solution.py:133
  (654 shorter events, 332.9 us)
Async XLA Ops:
  7.3 52.3 %all-gather.5.cloned.1.call-start = ((), (), s32[]{:S(2)}) async-start(), calls=%async_computation.8 | async-start | bytes 5242880 | tf_op jit(solution)/shard_map/all_gather | solution.py:401
  17.2 20.5 %collective-permute-start.1 = (bf16[128,2048]{1,0:T(8,128)(2,1)S(1)}, bf16[128,2048]{1,0:T(8,128)(2,1)S(1)}, u32[]{:S(2)}, u32[]{:S(2)}) collective-permute-start(bf16[128,2048]{1,0:T(8,128)(2,1)S(1)} %bitcast.208), channel_id=1, source_target_pairs={{8,0},{16,8},{24,16},{28,24},{20,28},{12,20},{4,12},{0,4},{9,1},{1... | collective-permute-start | bytes 1572872 | tf_op jit(solution)/shard_map/ppermute | solution.py:61
  17.7 41.9 %all-to-all-start = ((bf16[8,64,768]{2,1,0:T(8,128)(2,1)}), bf16[8,64,768]{2,1,0:T(8,128)(2,1)}, u32[]{:S(2)}, u32[]{:S(2)}) async-start(bf16[8,64,768]{2,1,0:T(8,128)(2,1)} %reshape.409), calls=%async_computation | async-start | bytes 1572864 | tf_op jit(solution)/shard_map/all_to_all | solution.py:133
  23.9 78.7 %all-gather.7.cloned.1.call-start = ((), (), s32[]{:S(2)}) async-start(), calls=%async_computation.9 | async-start | bytes 3932160 | tf_op jit(solution)/shard_map/all_gather | solution.py:334
  33.3 24.3 %collective-permute-start.2 = (bf16[128,2048]{1,0:T(8,128)(2,1)S(1)}, bf16[128,2048]{1,0:T(8,128)(2,1)S(1)}, u32[]{:S(2)}, u32[]{:S(2)}) collective-permute-start(bf16[128,2048]{1,0:T(8,128)(2,1)S(1)} %collective-permute-done), channel_id=1, source_target_pairs={{0,8},{8,16},{16,24},{24,28},{28,20},{20,12},{12,4},{4,0},{1,9},{9... | collective-permute-start | bytes 1572872 | tf_op jit(solution)/shard_map/ppermute | solution.py:61
  37.7 21.8 %collective-permute-start.3 = (bf16[128,2048]{1,0:T(8,128)(2,1)S(1)}, bf16[128,2048]{1,0:T(8,128)(2,1)S(1)}, u32[]{:S(2)}, u32[]{:S(2)}) collective-permute-start(bf16[128,2048]{1,0:T(8,128)(2,1)S(1)} %collective-permute-done.1), channel_id=1, source_target_pairs={{8,0},{16,8},{24,16},{28,24},{20,28},{12,20},{4,12},{0,4},{9,1},{1... | collective-permute-start | bytes 1572872 | tf_op jit(solution)/shard_map/ppermute | solution.py:61
  66.4 36.2 %all-to-all-start.1 = ((bf16[8,64,1024]{2,1,0:T(8,128)(2,1)}), bf16[8,64,1024]{2,1,0:T(8,128)(2,1)}, u32[]{:S(2)}, u32[]{:S(2)}) async-start(bf16[8,64,1024]{2,1,0:T(8,128)(2,1)} %copy.104), calls=%async_computation.1 | async-start | bytes 2097152 | tf_op jit(solution)/shard_map/all_to_all | solution.py:133
  72.5 45.6 %all-gather.9.cloned.1.call-start = ((), (), s32[]{:S(2)}) async-start(), calls=%async_computation.10 | async-start | bytes 1310720 | tf_op jit(solution)/shard_map/all_gather | solution.py:442
  74.8 83.4 %all-gather.11.cloned.1.call-start = ((), (), s32[]{:S(2)}) async-start(), calls=%async_computation.11 | async-start | bytes 5242880 | tf_op jit(solution)/shard_map/all_gather | solution.py:334
  79.4 23.2 %collective-permute-start.12 = (bf16[64,2048]{1,0:T(8,128)(2,1)S(1)}, bf16[64,2048]{1,0:T(8,128)(2,1)S(1)}, u32[]{:S(2)}, u32[]{:S(2)}) collective-permute-start(bf16[64,2048]{1,0:T(8,128)(2,1)S(1)} %slice.235), channel_id=1, source_target_pairs={{8,0},{16,8},{24,16},{28,24},{20,28},{12,20},{4,12},{0,4},{9,1},{1... | collective-permute-start | bytes 786440 | tf_op jit(solution)/shard_map/ppermute | solution.py:61
  79.8 22.8 %collective-permute-start.11 = (bf16[64,2048]{1,0:T(8,128)(2,1)S(1)}, bf16[64,2048]{1,0:T(8,128)(2,1)S(1)}, u32[]{:S(2)}, u32[]{:S(2)}) collective-permute-start(bf16[64,2048]{1,0:T(8,128)(2,1)S(1)} %slice.234), channel_id=1, source_target_pairs={{0,8},{8,16},{16,24},{24,28},{28,20},{20,12},{12,4},{4,0},{1,9},{9... | collective-permute-start | bytes 786440 | tf_op jit(solution)/shard_map/ppermute | solution.py:61
  110.6 278.8 %reduce-scatter.5.cloned.1.call-start = ((), (), s32[]{:S(2)}) async-start(), calls=%async_computation.12 | async-start | bytes 5242880 | tf_op jit(solution)/shard_map/reduce_scatter | solution.py:523
  183.2 21.4 %collective-permute-start.27 = (bf16[128,2048]{1,0:T(8,128)(2,1)}, bf16[128,2048]{1,0:T(8,128)(2,1)}, u32[]{:S(2)}, u32[]{:S(2)}) collective-permute-start(bf16[128,2048]{1,0:T(8,128)(2,1)} %get-tuple-element.367), channel_id=1, source_target_pairs={{0,8},{8,16},{16,24},{24,28},{28,20},{20,12},{12,4},{4,0},{1,9},{9... | collective-permute-start | bytes 1572872 | tf_op jit(solution)/shard_map/ppermute | solution.py:61
  293.6 149.3 %reduce-scatter.7.cloned.1.call-start = ((), (), s32[]{:S(2)}) async-start(), calls=%async_computation.13 | async-start | bytes 5242880 | tf_op jit(solution)/shard_map/reduce_scatter | solution.py:534
  298.8 21.0 %collective-permute-start.43 = (bf16[128,2048]{1,0:T(8,128)(2,1)S(1)}, bf16[128,2048]{1,0:T(8,128)(2,1)S(1)}, u32[]{:S(2)}, u32[]{:S(2)}) collective-permute-start(bf16[128,2048]{1,0:T(8,128)(2,1)S(1)} %get-tuple-element.355), channel_id=1, source_target_pairs={{0,8},{8,16},{16,24},{24,28},{28,20},{20,12},{12,4},{4,0},{1,9},{9... | collective-permute-start | bytes 1572872 | tf_op jit(solution)/shard_map/ppermute | solution.py:61
  299.1 23.1 %collective-permute-start.46 = (bf16[128,2048]{1,0:T(8,128)(2,1)S(1)}, bf16[128,2048]{1,0:T(8,128)(2,1)S(1)}, u32[]{:S(2)}, u32[]{:S(2)}) collective-permute-start(bf16[128,2048]{1,0:T(8,128)(2,1)S(1)} %pad_maximum_fusion.13), channel_id=1, source_target_pairs={{8,0},{16,8},{24,16},{28,24},{20,28},{12,20},{4,12},{0,4},{9,1},{1... | collective-permute-start | bytes 1572872 | tf_op jit(solution)/shard_map/ppermute | solution.py:61
  389.3 19.7 %collective-permute-start.57 = (bf16[128,2048]{1,0:T(8,128)(2,1)}, bf16[128,2048]{1,0:T(8,128)(2,1)S(1)}, u32[]{:S(2)}, u32[]{:S(2)}) collective-permute-start(bf16[128,2048]{1,0:T(8,128)(2,1)} %copy-done.98), channel_id=1, source_target_pairs={{0,8},{8,16},{16,24},{24,28},{28,20},{20,12},{12,4},{4,0},{1,9},{9... | collective-permute-start | bytes 1572872 | tf_op jit(solution)/shard_map/ppermute | solution.py:61
  391.1 19.9 %collective-permute-start.58 = (bf16[128,2048]{1,0:T(8,128)(2,1)}, bf16[128,2048]{1,0:T(8,128)(2,1)S(1)}, u32[]{:S(2)}, u32[]{:S(2)}) collective-permute-start(bf16[128,2048]{1,0:T(8,128)(2,1)} %collective-permute-done.56), channel_id=1, source_target_pairs={{8,0},{16,8},{24,16},{28,24},{20,28},{12,20},{4,12},{0,4},{9,1},{1... | collective-permute-start | bytes 1572872 | tf_op jit(solution)/shard_map/ppermute | solution.py:61
  420.4 35.3 %all-to-all-start.2 = ((bf16[8,64,1024]{2,1,0:T(8,128)(2,1)}), bf16[8,64,1024]{2,1,0:T(8,128)(2,1)}, u32[]{:S(2)}, u32[]{:S(2)}) async-start(bf16[8,64,1024]{2,1,0:T(8,128)(2,1)} %reduce-scatter.5.cloned.1.call-done), calls=%async_computation.4 | async-start | bytes 2097152 | tf_op jit(solution)/shard_map/all_to_all | solution.py:133
  425.1 70.2 %reduce-scatter.9.cloned.1.call-start = ((), (), s32[]{:S(2)}) async-start(), calls=%async_computation.14 | async-start | bytes 3932160 | tf_op jit(solution)/shard_map/reduce_scatter | solution.py:570
  455.7 85.7 %reduce-scatter.11.cloned.1.call-start = ((), (), s32[]{:S(2)}) async-start(), calls=%async_computation.15 | async-start | bytes 1310720 | tf_op jit(solution)/shard_map/reduce_scatter | solution.py:578
  470.5 19.2 %collective-permute-start.66 = (bf16[128,2048]{1,0:T(8,128)(2,1)}, bf16[128,2048]{1,0:T(8,128)(2,1)}, u32[]{:S(2)}, u32[]{:S(2)}) collective-permute-start(bf16[128,2048]{1,0:T(8,128)(2,1)} %get-tuple-element.338), channel_id=1, source_target_pairs={{8,0},{16,8},{24,16},{28,24},{20,28},{12,20},{4,12},{0,4},{9,1},{1... | collective-permute-start | bytes 1572872 | tf_op jit(solution)/shard_map/ppermute | solution.py:61
  471.0 18.8 %collective-permute-start.65 = (bf16[128,2048]{1,0:T(8,128)(2,1)}, bf16[128,2048]{1,0:T(8,128)(2,1)}, u32[]{:S(2)}, u32[]{:S(2)}) collective-permute-start(bf16[128,2048]{1,0:T(8,128)(2,1)} %get-tuple-element.339), channel_id=1, source_target_pairs={{0,8},{8,16},{16,24},{24,28},{28,20},{20,12},{12,4},{4,0},{1,9},{9... | collective-permute-start | bytes 1572872 | tf_op jit(solution)/shard_map/ppermute | solution.py:61
  504.0 33.9 %all-to-all-start.3 = ((bf16[8,64,768]{2,1,0:T(8,128)(2,1)}), bf16[8,64,768]{2,1,0:T(8,128)(2,1)S(1)}, u32[]{:S(2)}, u32[]{:S(2)}) async-start(bf16[8,64,768]{2,1,0:T(8,128)(2,1)} %reduce-scatter.9.cloned.1.call-done), calls=%async_computation.6 | async-start | bytes 1572864 | tf_op jit(solution)/shard_map/all_to_all | solution.py:133
  (190 other events, 1600.3 us)
Sparse Core Ops, SparseCore 0:
  10.3 35.6 all-gather.4
  59.7 27.8 all-gather.6
  89.1 16.7 all-gather.8
  110.7 32.5 all-gather.10
  293.7 42.8 reduce-scatter.4
  348.3 42.8 reduce-scatter.6
  455.8 37.8 reduce-scatter.8
  496.5 25.3 reduce-scatter.10

commit v3 on v2

--- a/solution.py
+++ b/solution.py
@@ -103,23 +103,18 @@
     return lax.ppermute(values, name, [(i, i ^ bit) for i in range(size)])
 
 
-def gather_small(values):
-    values = values[None]
-    for name, bit, size in bits_of(EVERY):
+def gather_small(values, bits):
+    for name, bit, size in bits:
         other = swap(values, name, bit, size)
         first = (lax.axis_index(name) & bit) == 0
         values = jnp.concatenate([jnp.where(first, values, other), jnp.where(first, other, values)])
     return values
 
 
-def sum_small(values):
-    for name, bit, size in bits_of(EVERY):
-        values = values.reshape(-1, 2, values.shape[-1])
-        low, high = values[:, 0], values[:, 1]
-        first = (lax.axis_index(name) & bit) == 0
-        other = swap(jnp.where(first, high, low), name, bit, size)
-        values = jnp.where(first, low, high) + other
-    return values[0]
+def sum_small(values, names):
+    for name, bit, size in bits_of(names):
+        values = values + swap(values, name, bit, size)
+    return values
 
 
 def by_place(rows, groups):
@@ -131,6 +126,18 @@
 
 def exchange(pieces):
     return lax.all_to_all(pieces, "tp", split_axis=0, concat_axis=0, tiled=True)
+
+
+def in_hbm(*arrays):
+    return [pltpu.with_memory_space_constraint(v, pltpu.HBM) for v in arrays]
+
+
+def settings(name, megabytes=40):
+    return {
+        "compiler_params": pltpu.CompilerParams(vmem_limit_bytes=megabytes << 20),
+        "cost_estimate": pl.CostEstimate(flops=1 << 20, bytes_accessed=1 << 20, transcendentals=0),
+        "name": name,
+    }
 
 
 def rows_product(lefts, rights, tile, name):
@@ -154,51 +161,42 @@
         in_specs=[pl.BlockSpec((v.shape[0], tile), lambda i: (0, i)) for v in lefts]
         + [pl.BlockSpec(v.shape, lambda i: (0, 0)) for v in rights],
         out_specs=pl.BlockSpec((tile, out_cols), lambda i: (i, 0)),
-        out_shape=jax.ShapeDtypeStruct((out_rows, out_cols), jnp.bfloat16),
-        compiler_params=pltpu.CompilerParams(vmem_limit_bytes=40 << 20),
-        cost_estimate=pl.CostEstimate(flops=1 << 20, bytes_accessed=1 << 20, transcendentals=0),
-        name=name,
+        out_shape=pltpu.HBM((out_rows, out_cols), jnp.bfloat16),
+        **settings(name),
     )(*lefts, *rights)
 
 
-def score_rows(keys, queries, slope, first_block, query_pos, query_seg, key_pos, key_seg):
+def score_rows(table, keys, queries, heads, query_blocks):
     scores = dot(keys, queries, 1, 1)
-    count = queries.shape[0] // BLK
+    count, key_blocks = queries.shape[0] // BLK, keys.shape[0] // BLK
     lane = lax.broadcasted_iota(jnp.int32, (1, queries.shape[0]), 1)
     down = lax.broadcasted_iota(jnp.int32, (BLK, queries.shape[0]), 0)
     ahead = down - lax.rem(lane, BLK)
+    head = table[2 * query_blocks + 2 * key_blocks] + pl.program_id(0)
+    slope = jnp.exp2(full(jnp.full(down.shape, head + 1, jnp.int32)) * (-8.0 / heads))
     slant = slope * full(down)
     tiles = []
-    for j in range(keys.shape[0] // BLK):
+    for j in range(key_blocks):
+        key_pos = table[2 * query_blocks + j]
+        key_seg = table[2 * query_blocks + key_blocks + j]
         limit = jnp.zeros((1, queries.shape[0]), jnp.int32)
         for i in range(count):
-            block = first_block * count + i
-            seen = (key_seg[j] == 0) | (key_seg[j] == query_seg[block])
-            here = jnp.where(seen, query_pos[block] - key_pos[j], -BLK)
+            block = pl.program_id(1) * count + i
+            seen = (key_seg == 0) | (key_seg == table[query_blocks + block])
+            here = jnp.where(seen, table[block] - key_pos, -BLK)
             limit = jnp.where(lane >= i * BLK, here, limit)
         tile = scores[j * BLK : (j + 1) * BLK] * (1.0 / math.sqrt(HD))
-        tile = tile + (slant + slope * full(key_pos[j]))
+        tile = tile + (slant + slope * full(key_pos))
         tiles.append(jnp.where(ahead <= limit, tile, NEG_FILL))
     return jnp.concatenate(tiles)
 
 
-def attend_body(
-    query_pos, query_seg, key_pos, key_seg, slopes, query, key, value, attended, level, value_t
-):
+def attend_body(heads, query_blocks, table, query, key, value, attended, level, value_t):
     @pl.when(pl.program_id(1) == 0)
     def turn():
         value_t[...] = half(full(value[...]).T)
 
-    scores = score_rows(
-        key[...],
-        query[...],
-        slopes[pl.program_id(0)],
-        pl.program_id(1),
-        query_pos,
-        query_seg,
-        key_pos,
-        key_seg,
-    )
+    scores = score_rows(table, key[...], query[...], heads, query_blocks)
     top = jnp.max(scores, axis=0, keepdims=True)
     expon = jnp.exp(scores - top)
     total = jnp.sum(expon, axis=0, keepdims=True)
@@ -208,22 +206,20 @@
 
 
 def attend_back_body(
+    heads,
+    query_blocks,
     my_heads,
     split,
-    query_pos,
-    query_seg,
-    key_pos,
-    key_seg,
-    slopes,
+    table,
     query,
     key,
     value,
-    grad,
     level,
     *rest,
 ):
+    rest, grad_parts = rest[len(PARTS) :], rest[: len(PARTS)]
     d_query, d_keys = (rest[0], rest[1]) if split else (rest[0], rest[0])
-    key_t, key_acc, value_acc = rest[-3:]
+    grads, key_t, key_acc, value_acc = rest[-4:]
     head, block = pl.program_id(0), pl.program_id(1)
     rows = query.shape[0]
     scale = 1.0 / math.sqrt(HD)
@@ -233,21 +229,24 @@
 
     @pl.when(block == 0)
     def begin():
+        begin_row = 0
+        for part in grad_parts:
+            grads[begin_row : begin_row + part.shape[0], :] = part[...]
+            begin_row += part.shape[0]
         key_t[...] = half(full(key[...]).T)
         key_acc[...] = jnp.zeros_like(key_acc)
         value_acc[...] = jnp.zeros_like(value_acc)
 
-    scores = score_rows(
-        key[...], query[...], slopes[head], block, query_pos, query_seg, key_pos, key_seg
-    )
+    scores = score_rows(table, key[...], query[...], heads, query_blocks)
     probs = jnp.exp(scores - level[0])
-    d_probs = dot(value[...], grad[...], 1, 1)
+    grad = grads[pl.ds(pl.multiple_of(block * rows, rows), rows), :]
+    d_probs = dot(value[...], grad, 1, 1)
     delta = jnp.sum(probs * d_probs, axis=0, keepdims=True)
     d_scores = half(probs * (d_probs - delta))
     turned = (dot(key_t[...], d_scores, 1, 0) * scale).T
     d_query[pl.ds(pl.multiple_of(block * rows, rows), rows), columns(0)] = half(turned)
     key_acc[...] += dot(d_scores, query[...], 1, 0)
-    value_acc[...] += dot(half(probs), grad[...], 1, 0)
+    value_acc[...] += dot(half(probs), grad, 1, 0)
 
     @pl.when(block == pl.num_programs(1) - 1)
     def end():
@@ -256,20 +255,20 @@
         d_keys[:, columns(shift + 1)] = half(value_acc[...])
 
 
-def attention(blocks, slopes, query, keys, first, grad=None, level=None):
-    my_heads = slopes.shape[0]
+def attention(table, heads, my_heads, query, keys, first, grad=None, level=None):
     rows, total = query.shape[0], keys.shape[0]
     step = 256 if total <= 1024 else BLK
     columns = my_heads * HD
     scalars = pl.BlockSpec(memory_space=pltpu.SMEM)
     of_query = pl.BlockSpec((step, HD), lambda h, i: (i, h))
     of_level = pl.BlockSpec((1, 1, step), lambda h, i: (h, 0, i))
-    in_specs = [scalars] * 5 + [
+    in_specs = [
+        scalars,
         of_query,
         pl.BlockSpec((total, HD), lambda h, i: (0, first + h)),
         pl.BlockSpec((total, HD), lambda h, i: (0, first + my_heads + h)),
     ]
-    settings = {
+    common = {
         "grid": (my_heads, rows // step),
         "compiler_params": pltpu.CompilerParams(vmem_limit_bytes=48 << 20),
         "cost_estimate": pl.CostEstimate(
@@ -280,7 +279,7 @@
     }
     if grad is None:
         return pl.pallas_call(
-            attend_body,
+            functools.partial(attend_body, heads, rows // BLK),
             in_specs=in_specs,
             out_specs=[of_query, of_level],
             out_shape=[
@@ -289,23 +288,26 @@
             ],
             scratch_shapes=[pltpu.VMEM((HD, total), jnp.bfloat16)],
             name="attend",
-            **settings,
-        )(*blocks, slopes, query, keys, keys)
+            **common,
+        )(table, *in_hbm(query, keys, keys))
     split = query is not keys
     shapes = [(rows, columns), (total, 2 * columns)] if split else [(rows, 3 * columns)]
     return pl.pallas_call(
-        functools.partial(attend_back_body, my_heads, split),
-        in_specs=in_specs + [of_query, of_level],
+        functools.partial(attend_back_body, heads, rows // BLK, my_heads, split),
+        in_specs=in_specs
+        + [of_level]
+        + [pl.BlockSpec((part.shape[0], HD), lambda h, i: (0, h)) for part in grad],
         out_specs=[pl.BlockSpec(shape, lambda h, i: (0, 0)) for shape in shapes],
         out_shape=[jax.ShapeDtypeStruct(shape, jnp.bfloat16) for shape in shapes],
         scratch_shapes=[
+            pltpu.VMEM((rows, HD), jnp.bfloat16),
             pltpu.VMEM((HD, total), jnp.bfloat16),
             pltpu.VMEM((total, HD), jnp.float32),
             pltpu.VMEM((total, HD), jnp.float32),
         ],
         name="attend_back",
-        **settings,
-    )(*blocks, slopes, query, keys, keys, grad, level)
+        **common,
+    )(table, *in_hbm(query, keys, keys, level, *grad))
 
 
 def products(parts, matrix, name):
@@ -324,9 +326,7 @@
         out_shape=[
             jax.ShapeDtypeStruct((v.shape[0], matrix.shape[0]), jnp.bfloat16) for v in parts
         ],
-        compiler_params=pltpu.CompilerParams(vmem_limit_bytes=40 << 20),
-        cost_estimate=pl.CostEstimate(flops=1 << 20, bytes_accessed=1 << 20, transcendentals=0),
-        name=name,
+        **settings(name),
     )(*parts, matrix)
 
 
@@ -335,10 +335,178 @@
     return rows.reshape(-1, rows.shape[2])
 
 
-def from_places(grad, groups):
+def from_places(grad, groups, name):
     places, n, width = grad.shape
-    grad = grad.reshape(places, n, groups, width // groups).transpose(1, 2, 0, 3)
-    return full(grad.reshape(n, places * width))
+    part = width // groups
+
+    def body(grad_ref, out_ref):
+        for group in range(groups):
+            for place in range(places):
+                begin = (group * places + place) * part
+                out_ref[:, begin : begin + part] = full(
+                    grad_ref[place, :, group * part : (group + 1) * part]
+                )
+
+    return pl.pallas_call(
+        body,
+        out_shape=jax.ShapeDtypeStruct((n, places * width), jnp.float32),
+        **settings(name),
+    )(grad)
+
+
+def norm_back(sums, rows, gain, direct, name, branch):
+    n, width = rows.shape
+    step = 32
+
+    def body(part, upward, downward, rows_ref, gain_ref, direct_ref, grad_ref, *rest):
+        @pl.when(pl.program_id(0) == 0)
+        def begin():
+            for ref in rest[-3 if branch else -2 :]:
+                ref[...] = jnp.zeros_like(ref)
+
+        grad = full(part[...]) + full(upward[...]) + full(downward[...])
+        normed, scale = normalize(full(rows_ref[...]))
+        out = full(direct_ref[...]) + normalize_back(normed, scale, grad * gain_ref[...])
+        grad_ref[...] = out
+        if branch:
+            rounded = half(out)
+            rest[0][...] = rounded
+            rest[-3][...] += jnp.sum(full(rounded), axis=0, keepdims=True)
+        rest[-2][...] += jnp.sum(grad * normed, axis=0, keepdims=True)
+        rest[-1][...] += jnp.sum(grad, axis=0, keepdims=True)
+
+    tile = pl.BlockSpec((step, width), lambda i: (i, 0))
+    line = pl.BlockSpec((1, width), lambda i: (0, 0))
+    lines = 3 if branch else 2
+    return pl.pallas_call(
+        body,
+        grid=(n // step,),
+        in_specs=[tile] * 4 + [line, tile],
+        out_specs=[tile] * (2 if branch else 1) + [line] * lines,
+        out_shape=[jax.ShapeDtypeStruct((n, width), jnp.float32)]
+        + [jax.ShapeDtypeStruct((n, width), jnp.bfloat16)] * branch
+        + [jax.ShapeDtypeStruct((1, width), jnp.float32)] * lines,
+        **settings(name),
+    )(*sums, rows, gain.reshape(1, -1), direct)
+
+
+def converted(values, name):
+    def body(values_ref, out_ref):
+        out_ref[...] = full(values_ref[...])
+
+    return pl.pallas_call(
+        body, out_shape=jax.ShapeDtypeStruct(values.shape, jnp.float32), **settings(name)
+    )(values)
+
+
+def total(sums, rows, bias, name):
+    def body(part, upward, downward, rows_ref, bias_ref, out_ref):
+        out = full(part[...]) + full(upward[...]) + full(downward[...])
+        out_ref[...] = half(rows_ref[...] + out + bias_ref[...])
+
+    return pl.pallas_call(
+        body, out_shape=jax.ShapeDtypeStruct(rows.shape, jnp.bfloat16), **settings(name)
+    )(*sums, rows, bias.reshape(1, -1))
+
+
+def rows_by_place(vectors, name):
+    widths = [v.shape[1] // PLACES for v in vectors]
+
+    def body(*refs):
+        begin = 0
+        for ref, width in zip(refs[:-1], widths, strict=True):
+            for place in range(PLACES):
+                refs[-1][place : place + 1, begin : begin + width] = ref[
+                    :, place * width : (place + 1) * width
+                ]
+            begin += width
+
+    return pl.pallas_call(
+        body,
+        out_shape=jax.ShapeDtypeStruct((PLACES, sum(widths)), jnp.float32),
+        **settings(name),
+    )(*vectors)
+
+
+def with_rows(pieces, rows, name):
+    places, n, width = pieces.shape
+    more = -(-rows.shape[1] // width)
+    padded = -(-more // 16) * 16
+
+    def body(pieces_ref, rows_ref, out_ref):
+        out_ref[:, :n, :] = pieces_ref[...]
+        out_ref[:, n:, :] = jnp.zeros((places, padded, width), jnp.bfloat16)
+        for place in range(places):
+            lines = [
+                rows_ref[place : place + 1, i * width : (i + 1) * width] for i in range(more)
+            ]
+            lines.append(jnp.zeros((padded - more, width), jnp.float32))
+            out_ref[place, n:, :] = half(jnp.concatenate(lines))
+
+    return pl.pallas_call(
+        body,
+        out_shape=jax.ShapeDtypeStruct((places, n + padded, width), jnp.bfloat16),
+        **settings(name),
+    )(pieces, rows)
+
+
+def from_places_and_rows(received, groups, n, count, name):
+    places, padded, width = received.shape
+    part = width // groups
+    more = count // width
+
+    def body(received_ref, out_ref, sum_ref):
+        for group in range(groups):
+            for place in range(places):
+                begin = (group * places + place) * part
+                out_ref[:, begin : begin + part] = full(
+                    received_ref[place, :n, group * part : (group + 1) * part]
+                )
+        lines = jnp.sum(full(received_ref[:, n:, :]), axis=0)
+        for i in range(more):
+            sum_ref[:, i * width : (i + 1) * width] = lines[i : i + 1]
+
+    return pl.pallas_call(
+        body,
+        out_shape=[
+            jax.ShapeDtypeStruct((n, places * width), jnp.float32),
+            jax.ShapeDtypeStruct((1, count), jnp.float32),
+        ],
+        **settings(name),
+    )(received)
+
+
+def norm_sums(grads, rows, mixed, name):
+    width, count, step = rows[0].shape[1], len(rows), 64
+    columns = mixed[0].shape[1]
+
+    def body(*refs):
+        gain = jnp.zeros((1, width), jnp.float32)
+        bias = jnp.zeros((1, width), jnp.float32)
+        for grad_ref, rows_ref in zip(refs[:count], refs[count : 2 * count], strict=True):
+
+            def add(i, carried, grad_ref=grad_ref, rows_ref=rows_ref):
+                here = pl.ds(pl.multiple_of(i * step, step), step)
+                grad = full(grad_ref[here, :])
+                normed = normalize(full(rows_ref[here, :]))[0]
+                return (
+                    carried[0] + jnp.sum(grad * normed, axis=0, keepdims=True),
+                    carried[1] + jnp.sum(grad, axis=0, keepdims=True),
+                )
+
+            gain, bias = lax.fori_loop(0, rows_ref.shape[0] // step, add, (gain, bias))
+        refs[-3][...] = gain
+        refs[-2][...] = bias
+        refs[-1][...] = sum(
+            jnp.sum(full(ref[...]), axis=0, keepdims=True) for ref in refs[2 * count : 3 * count]
+        )
+
+    return pl.pallas_call(
+        body,
+        out_shape=[jax.ShapeDtypeStruct((1, width), jnp.float32)] * 2
+        + [jax.ShapeDtypeStruct((1, columns), jnp.float32)],
+        **settings(name),
+    )(*grads, *rows, *mixed)
 
 
 def on_device(
@@ -388,9 +556,8 @@
 
     query_seg, key_seg = in_order(block_seg[0])
     query_pos, key_pos = in_order(block_pos[0])
-    blocks = (query_pos, query_seg, key_pos, key_seg)
-    head_ids = my_tp * my_heads + jnp.arange(my_heads, dtype=jnp.int32)
-    slopes = jnp.exp2(-8.0 * (head_ids.astype(jnp.float32) + 1.0) / heads)
+    first_head = jnp.full((1,), my_tp * my_heads, jnp.int32)
+    table = jnp.concatenate([query_pos, query_seg, key_pos, key_seg, first_head])
 
     small = [ln1_gain, ln1_bias, b_out, ln2_gain, ln2_bias, b_down, b_qv, b_in]
     sizes = [v.shape[0] for v in small]
@@ -401,7 +568,7 @@
     down_slice = lax.all_gather(half(w_down), TOKENS, axis=0, tiled=True)
     small_own, qkv_pieces = fence(half(jnp.concatenate(small)), by_place(w_qkv, 3))
     qkv_pieces = exchange(qkv_pieces)
-    gathered = gather_small(small_own)
+    gathered = gather_small(small_own[None], bits_of(EVERY))
     low2, high2 = hop(low1, high1)
     in_pieces = by_place(w_in, 1)
     (
@@ -447,24 +614,25 @@
     low4, high4 = last_hop(low3, high3)
     token_parts.append(join((low3, high3)))
     normed.append(norm1(token_parts[3]))
-    low4, high4, own_cot, in_pieces, qkv_slice, *normed = fence(
-        low4, high4, own_cot, in_pieces, qkv_slice, *normed
-    )
+    blank = jnp.zeros((head_cols,), jnp.float32)
+    qkv_bias = jnp.concatenate([qv_bias[0], blank, qv_bias[1]])
+    mixed = [half(dot(part, qkv_slice, 1, 0) + qkv_bias) for part in normed]
+    low4, high4, own_cot, qkv_slice, *mixed = fence(low4, high4, own_cot, qkv_slice, *mixed)
 
     cot_low1, cot_high1 = hop(own_cot, own_cot)
     token_parts.append(join((low4, high4)))
     normed.append(norm1(token_parts[4]))
-    blank = jnp.zeros((head_cols,), jnp.float32)
-    qkv_bias = jnp.concatenate([qv_bias[0], blank, qv_bias[1]])
-    mixed = jnp.concatenate([half(dot(part, qkv_slice, 1, 0) + qkv_bias) for part in normed])
-    mixed, cot_low1, cot_high1, out_slice = fence(mixed, cot_low1, cot_high1, out_slice)
+    mixed = jnp.concatenate([*mixed, half(dot(normed[4], qkv_slice, 1, 0) + qkv_bias)])
+    mixed, cot_low1, cot_high1, in_pieces, out_slice = fence(
+        mixed, cot_low1, cot_high1, in_pieces, out_slice
+    )
     in_slice = gather_rows(in_pieces)
     cot_low2, cot_high2 = hop(cot_low1, cot_high1)
     keys = mixed
     if sp > 1:
         keys = lax.all_gather(mixed[:, head_cols:], "sp", axis=0, tiled=True)
     first_key = my_heads if sp == 1 else 0
-    attended, level = attention(blocks, slopes, mixed, keys, first_key)
+    attended, level = attention(table, heads, my_heads, mixed, keys, first_key)
     attended, cot_low2, cot_high2 = fence(attended, cot_low2, cot_high2)
 
     attended_parts = by_part(attended)
@@ -528,14 +696,17 @@
     out_up, out_down = hop(*next_sum(ffn_parts[2], out_up, out_down))
     grad_down = rows_product(act_parts, cot_parts, 256, "grad_down")
     grad_b_in = sum(jnp.sum(full(part), axis=0) for part in d_pre_parts)
+    blank = jnp.zeros((PLACES * hidden,), jnp.float32)
+    grad_b_in = lax.dynamic_update_slice_in_dim(blank, grad_b_in, my_tp * hidden, 0)
+    g_b_down = jnp.sum(full(own_cot), axis=0)
     up, down, out_up, out_down, grad_down, grad_b_in = fence(
         up, down, out_up, out_down, grad_down, grad_b_in
     )
     grad_down = lax.psum_scatter(grad_down, TOKENS, scatter_dimension=0, tiled=True)
-    d_second = last_sum(d_second_parts[0], up, down)
-
-    d_residual = full(own_cot) + normalize_back(own_normed2, scale2, d_second * gain2)
-    d_branch = half(d_residual)
+
+    d_residual, d_branch, g_b_out, g_gain2, g_bias2 = norm_back(
+        (d_second_parts[0], up, down), residual, gain2, own_cot, "norm2_back", True
+    )
     low, high = hop(d_branch, d_branch)
     out_up, out_down = hop(*next_sum(ffn_parts[1], out_up, out_down))
     low, high, out_up, out_down = fence(low, high, out_up, out_down)
@@ -551,8 +722,7 @@
             low, high, grad_in, d_attended[index] = fence(low, high, grad_in, d_attended[index])
             grad_in = exchange(grad_in)
 
-    d_attended = jnp.concatenate(d_attended)
-    grads = attention(blocks, slopes, mixed, keys, first_key, d_attended, level)
+    grads = attention(table, heads, my_heads, mixed, keys, first_key, d_attended, level)
     if sp == 1:
         (d_mixed,) = grads
     else:
@@ -563,56 +733,46 @@
     mixed_parts = by_part(d_mixed)
     far = dot(mixed_parts[4], qkv_slice, 1, 1, jnp.bfloat16)
     low, high = hop(*jnp.split(far, 2))
-    near = dot(mixed_parts[3], qkv_slice, 1, 1, jnp.bfloat16)
+    (near,) = products(mixed_parts[3:4], qkv_slice, "d_normed_near")
     grad_qkv = rows_product(normed, mixed_parts, 512, "grad_qkv")
     grad_qkv = grad_qkv.reshape(PLACES, -1, 3 * head_cols)
-    low, high, grad_qkv, near, grad_in = fence(low, high, grad_qkv, near, grad_in)
+    low, high, near, grad_qkv, mixed_parts[0] = fence(low, high, near, grad_qkv, mixed_parts[0])
     grad_qkv = lax.psum_scatter(grad_qkv, TOKENS, scatter_dimension=1, tiled=True)
     up, down = hop(*first_sum(near, low, high))
-    d_normed = products(mixed_parts[:3], qkv_slice, "d_normed")
-    up, down, attended_parts[4], *d_normed = fence(up, down, attended_parts[4], *d_normed)
+    d_normed = [*products(mixed_parts[:3], qkv_slice, "d_normed"), near, far]
+    g_gain1, g_bias1, mixed_sum = norm_sums(d_normed, token_parts, mixed_parts, "norm1_sums")
+    up, down, grad_in, g_gain1, g_bias1, mixed_sum, *d_normed[:3] = fence(
+        up, down, grad_in, g_gain1, g_bias1, mixed_sum, *d_normed[:3]
+    )
     up, down = hop(*next_sum(d_normed[2], up, down))
     grad_out = rows_product(attended_parts, d_branch_parts, 128, "grad_out")
-    up, down, grad_out = fence(up, down, grad_out)
-    grad_qkv, grad_out = fence(grad_qkv, grad_out)
+    grad_w_in = from_places(grad_in, 1, "in_back")
+    grad_b_qv = jnp.zeros((2, width), jnp.float32)
+    for i in range(2):
+        piece = mixed_sum[:, 2 * i * head_cols : (2 * i + 1) * head_cols]
+        grad_b_qv = lax.dynamic_update_slice(grad_b_qv, piece, (i, my_tp * head_cols))
+    whole = [g_gain1, g_bias1, g_b_out, g_gain2, g_bias2, g_b_down, grad_b_qv, grad_b_in]
+    summed = rows_by_place([v.reshape(1, -1) for v in whole], "sums_by_place")
+    summed = sum_small(summed, TOKENS)
+    own_rows = grad_qkv.shape[1]
+    grad_qkv = with_rows(grad_qkv, summed, "qkv_with_sums")
+    up, down, grad_out, grad_w_in, grad_qkv = fence(up, down, grad_out, grad_w_in, grad_qkv)
+    up, down = hop(*next_sum(d_normed[1], up, down))
+    grad_qkv = exchange(grad_qkv)
+    grad_w_down = converted(grad_down, "down_back")
+    output = total((ffn_parts[0], out_up, out_down), residual, down_bias, "output")
+    up, down, grad_w_down, output, grad_qkv = fence(up, down, grad_w_down, output, grad_qkv)
     grad_out = lax.psum_scatter(grad_out, TOKENS, scatter_dimension=0, tiled=True)
-    up, down = hop(*next_sum(d_normed[1], up, down))
-    up, down, grad_qkv, grad_in, grad_down, out_up, out_down = fence(
-        up, down, grad_qkv, grad_in, grad_down, out_up, out_down
-    )
-    grad_qkv = exchange(grad_qkv)
-    d_normed_own = last_sum(d_normed[0], up, down)
-    own_normed1, scale1 = normalize(full(own))
-    grad_tokens = d_residual + normalize_back(own_normed1, scale1, d_normed_own * gain1)
-    grad_w_in = from_places(grad_in, 1)
-    grad_w_down = full(grad_down)
-    output = half(residual + last_sum(ffn_parts[0], out_up, out_down) + down_bias)
-
-    def placed(values, whole):
-        start = my_tp * values.shape[-1]
-        blank = jnp.zeros(values.shape[:-1] + (whole,), jnp.float32)
-        return lax.dynamic_update_slice_in_dim(blank, values, start, values.ndim - 1)
-
-    mixed_sum = jnp.sum(full(d_mixed), axis=0)
-    grad_b_qv = placed(
-        jnp.stack([mixed_sum[:head_cols], mixed_sum[2 * head_cols :]]), width
-    )
-    partials = [
-        jnp.sum(d_normed_own * own_normed1, axis=0),
-        jnp.sum(d_normed_own, axis=0),
-        jnp.sum(full(d_branch), axis=0),
-        jnp.sum(d_second * own_normed2, axis=0),
-        jnp.sum(d_second, axis=0),
-        jnp.sum(full(own_cot), axis=0),
-        grad_b_qv.reshape(-1),
-        placed(grad_b_in, PLACES * hidden),
-    ]
-    stacked = jnp.concatenate([v.reshape(devices, -1) for v in partials], axis=1)
-    summed = sum_small(stacked)
-    grad_w_out = full(grad_out)
-    grad_w_qkv = from_places(grad_qkv, 3)
+    grad_tokens = norm_back((d_normed[0], up, down), own, gain1, d_residual, "norm1_back", False)[0]
+    grad_w_out = converted(grad_out, "out_back")
+    grad_w_qkv, summed = from_places_and_rows(
+        grad_qkv, 3, own_rows, summed.shape[1], "qkv_back"
+    )
+    near_devices = sp * fs
+    place = my_sp * fs + lax.axis_index("fs")
     g_gain1, g_bias1, g_b_out, g_gain2, g_bias2, g_b_down, g_b_qv, g_b_in = (
-        summed[cuts[i] : cuts[i + 1]] for i in range(len(sizes))
+        lax.dynamic_slice_in_dim(summed, cuts[i] * near_devices + place * sizes[i], sizes[i], 1)[0]
+        for i in range(len(sizes))
     )
     return (
         output[None],

time: 556 us -> 548 us (0.986)
  Pallas kernels: 45.5 us -> 73.6 us
  other arithmetic: 65.9 us -> 44 us
  starting transfers between devices: 122 us -> 114 us
  waiting for transfers between devices: 179 us -> 172 us
  local copies, waits for them, and re-layouts: 68.1 us -> 61.8 us
    pallas_call x2 -> x12, Pallas kernels: 20.9 us -> 43.3 us  [the longest x1 11.8 us: attention(): pl.pallas_call(functools.partial(attend_back_body, heads, rows // BLK, my...]
    reduce_sum x4 -> x1, other arithmetic: 9.2 us -> 1.13 us  [on_device(): g_b_down = jnp.sum(full(own_cot), axis=0)]
    concatenate x9 -> x1, local copies, waits for them, and re-layouts: 6.54 us -> 0.08 us  [on_device(): jnp.concatenate([query_pos, query_seg, key_pos, key_seg, first_head])]
    ppermute x64, waiting for transfers between devices: 155 us -> 149 us  [hop(): return (lax.ppermute(upward, 'tp', up), lax.ppermute(downward, 'tp', down))]
    unnamed x277 -> x301, local copies, waits for them, and re-layouts: 29.9 us -> 35 us
    ppermute x10 -> x7, starting transfers between devices: 15.8 us -> 11.3 us  [swap(): return lax.ppermute(values, name, [(i, i ^ bit) for i in range(size)])]
    dot_general x37 -> x36, matrix products: 52.1 us -> 55 us  [dot(): lax.dot_general(left, right, (((left_dim,), (right_dim,)), ((), ())), pre...]
    ppermute x10 -> x7, waiting for transfers between devices: 24 us -> 22.5 us  [swap(): return lax.ppermute(values, name, [(i, i ^ bit) for i in range(size)])]
  transfers between devices with their start and end apart: 86 -> 83, of which waited for: 42 -> 45; matrix products, arithmetic and copies ran while one was open for 27% -> 22% of each run, Pallas kernels for 8% -> 14%
where the time goes in v3:
time: 548 us; the launch traced here: 537 us
  waiting for transfers between devices  172 us (31%)
  starting transfers between devices  114 us (21%)
  Pallas kernels  73.6 us (13%)
  local copies, waits for them, and re-layouts  61.8 us (11%)
  matrix products  55 us (10%)
  other arithmetic  44 us (8%)
  between operations  16.7 us (3%)
    ppermute x64, waiting for transfers between devices, hop(): return (lax.ppermute(upward, 'tp', up), lax.ppermute(downward, 'tp', down))  149 us
    ppermute x64, starting transfers between devices, hop(): return (lax.ppermute(upward, 'tp', up), lax.ppermute(downward, 'tp', down))  79.9 us
    dot_general x36, matrix products, dot(): lax.dot_general(left, right, (((left_dim,), (right_dim,)), ((), ())), pre...  55 us
    unnamed x301, local copies, waits for them, and re-layouts  35 us
    convert_element_type x21, other arithmetic, half(): return values.astype(jnp.bfloat16)  27.4 us
    pallas_call x4, Pallas kernels, rows_product(): pl.pallas_call(body, grid=(out_rows // tile,), in_specs=[pl.BlockSpec((v....  24.9 us
    all_to_all x4, starting transfers between devices, exchange(): return lax.all_to_all(pieces, 'tp', split_axis=0, concat_axis=0, tiled=True)  22.7 us
    ppermute x7, waiting for transfers between devices, swap(): return lax.ppermute(values, name, [(i, i ^ bit) for i in range(size)])  22.5 us
  transfers between devices with their start and end apart: 83, of which 45 were waited for; matrix products, arithmetic and copies ran while one was open for 22% of the time, Pallas kernels for 14%

profile of v3, /device:TPU:8, one launch (start us, length us, event | category | flops | bytes accessed | tf_op | source)
XLA Modules:
  0.0 537.2 jit_solution(8138410347674460849)
XLA Ops:
  17.7 6.3 %all-to-all-start = ((bf16[8,64,768]{2,1,0:T(8,128)(2,1)}), bf16[8,64,768]{2,1,0:T(8,128)(2,1)}, u32[]{:S(2)}, u32[]{:S(2)}) async-start(bf16[8,64,768]{2,1,0:T(8,128)(2,1)} %reshape.285), calls=%async_computation | async-start | bytes 1572864 | tf_op jit(solution)/shard_map/all_to_all | solution.py:128
  28.3 6.6 %collective-permute-start.7 = (bf16[8,768]{1,0:T(8,128)(2,1)S(1)}, bf16[8,768]{1,0:T(8,128)(2,1)S(1)}, u32[]{:S(2)}, u32[]{:S(2)}) collective-permute-start(bf16[8,768]{1,0:T(8,128)(2,1)S(1)} %pad_maximum_fusion.14), channel_id=1, source_target_pairs={{0,8},{4,12},{8,0},{12,4},{16,24},{20,28},{24,16},{28,20},{1,9},{5... | collective-permute-start | bytes 36872 | tf_op jit(solution)/shard_map/ppermute | solution.py:103
  37.9 5.9 %collective-permute-done.7 = bf16[8,768]{1,0:T(8,128)(2,1)S(1)} collective-permute-done((bf16[8,768]{1,0:T(8,128)(2,1)S(1)}, bf16[8,768]{1,0:T(8,128)(2,1)S(1)}, u32[]{:S(2)}, u32[]{:S(2)}) %collective-permute-start.7) | collective-permute-done | bytes 12320 | tf_op jit(solution)/shard_map/ppermute | solution.py:103
  46.4 11.4 %collective-permute-done.8 = bf16[16,768]{1,0:T(8,128)(2,1)S(1)} collective-permute-done((bf16[16,768]{1,0:T(8,128)(2,1)S(1)}, bf16[16,768]{1,0:T(8,128)(2,1)S(1)}, u32[]{:S(2)}, u32[]{:S(2)}) %collective-permute-start.8) | collective-permute-done | bytes 24608 | tf_op jit(solution)/shard_map/ppermute | solution.py:103
  64.1 6.5 %all-to-all-start.1 = ((bf16[8,64,1024]{2,1,0:T(8,128)(2,1)}), bf16[8,64,1024]{2,1,0:T(8,128)(2,1)}, u32[]{:S(2)}, u32[]{:S(2)}) async-start(bf16[8,64,1024]{2,1,0:T(8,128)(2,1)} %copy.40), calls=%async_computation.1 | async-start | bytes 2097152 | tf_op jit(solution)/shard_map/all_to_all | solution.py:128
  94.1 8.4 %collective-permute-done.12 = bf16[64,2048]{1,0:T(8,128)(2,1)S(1)} collective-permute-done((bf16[64,2048]{1,0:T(8,128)(2,1)}, bf16[64,2048]{1,0:T(8,128)(2,1)S(1)}, u32[]{:S(2)}, u32[]{:S(2)}) %collective-permute-start.12) | collective-permute-done | bytes 262176 | tf_op jit(solution)/shard_map/ppermute | solution.py:61
  119.8 9.7 %attend.1 = (bf16[1024,256]{1,0:T(8,128)(2,1)S(1)}, f32[2,1,1024]{2,1,0:T(1,128)S(1)}) custom-call(s32[33]{0:T(128)S(1)} %concatenate.100.table, bf16[1024,768]{1,0:T(8,128)(2,1)} %fusion.27.query.key.value, bf16[1024,768]{1,0:T(8,128)(2,1)} %fusion.27.query.key.value, bf16[1024,768]{1,0:T(8,128)(2,1)} %fusion.27.query.key.value), custom_call_target="tpu_custom_call" | custom-call | flops 1073741824 | bytes 33554432 | tf_op jit(solution)/shard_map/attend/pallas_call | solution.py:281
  141.2 7.0 %collective-permute-done.19 = bf16[128,2048]{1,0:T(8,128)(2,1)S(1)} collective-permute-done((bf16[128,2048]{1,0:T(8,128)(2,1)}, bf16[128,2048]{1,0:T(8,128)(2,1)S(1)}, u32[]{:S(2)}, u32[]{:S(2)}) %collective-permute-start.19) | collective-permute-done | bytes 524320 | tf_op jit(solution)/shard_map/ppermute | solution.py:61
  158.0 6.7 %copy.42 = bf16[8,256,1024]{2,1,0:T(8,128)(2,1)} copy(bf16[8,256,1024]{2,0,1:T(8,128)(2,1)} %all-gather.11.cloned.1.call-done) | data formatting | bytes 8388608 | tf_op jit(solution)/shard_map/all_gather | solution.py:334
  185.3 9.9 %collective-permute-done.28 = bf16[128,2048]{1,0:T(8,128)(2,1)} collective-permute-done((bf16[128,2048]{1,0:T(8,128)(2,1)}, bf16[128,2048]{1,0:T(8,128)(2,1)}, u32[]{:S(2)}, u32[]{:S(2)}) %collective-permute-start.28) | collective-permute-done | bytes 524320 | tf_op jit(solution)/shard_map/ppermute | solution.py:61
  199.1 11.3 %collective-permute-start.29 = (bf16[128,2048]{1,0:T(8,128)(2,1)S(1)}, bf16[128,2048]{1,0:T(8,128)(2,1)S(1)}, u32[]{:S(2)}, u32[]{:S(2)}) collective-permute-start(bf16[128,2048]{1,0:T(8,128)(2,1)S(1)} %add_convert_fusion.12.refs_0_), channel_id=1, source_target_pairs={{0,8},{8,16},{16,24},{24,28},{28,20},{20,12},{12,4},{4,0},{1,9},{9... | collective-permute-start | bytes 1572872 | tf_op jit(solution)/shard_map/ppermute | solution.py:61
  276.2 7.5 %grad_in.1 = bf16[2048,1024]{1,0:T(8,128)(2,1)} custom-call(bf16[128,2048]{1,0:T(8,128)(2,1)S(1)} %add_convert_fusion.12.refs_0_, bf16[256,2048]{1,0:T(8,128)(2,1)S(1)} %constant_dynamic-update-slice_fusion.12.refs_1_, bf16[256,2048]{1,0:T(8,128)(2,1)S(1)} %constant_dynamic-update-slice_fusion.14.refs_2_, ...), custom_call_target="tpu_custom_call" | custom-call | flops 1048576 | bytes 1048576 | tf_op jit(solution)/shard_map/grad_in/pallas_call | solution.py:158
  298.3 9.8 %collective-permute-done.45 = bf16[128,2048]{1,0:T(8,128)(2,1)S(1)} collective-permute-done((bf16[128,2048]{1,0:T(8,128)(2,1)S(1)}, bf16[128,2048]{1,0:T(8,128)(2,1)S(1)}, u32[]{:S(2)}, u32[]{:S(2)}) %collective-permute-start.45) | collective-permute-done | bytes 524320 | tf_op jit(solution)/shard_map/ppermute | solution.py:61
  308.1 6.2 %collective-permute-done.43 = bf16[128,2048]{1,0:T(8,128)(2,1)S(1)} collective-permute-done((bf16[128,2048]{1,0:T(8,128)(2,1)S(1)}, bf16[128,2048]{1,0:T(8,128)(2,1)S(1)}, u32[]{:S(2)}, u32[]{:S(2)}) %collective-permute-start.43) | collective-permute-done | bytes 524320 | tf_op jit(solution)/shard_map/ppermute | solution.py:61
  322.1 8.5 %grad_down.1 = bf16[1024,2048]{1,0:T(8,128)(2,1)} custom-call(bf16[128,1024]{1,0:T(8,128)(2,1)S(1)} %copy-done.78, bf16[256,1024]{1,0:T(8,128)(2,1)S(1)} %copy-done.83, bf16[256,1024]{1,0:T(8,128)(2,1)S(1)} %copy-done.85, bf16[256,1024]{1,0:T(8,128)(2,1)S(1)} %copy-done.87, bf16[128,1024]{1,0:T(8,128)(2,1)S(1)} %copy-done.80, ...), custom_call_target="tpu_custom_call" | custom-call | flops 1048576 | bytes 1048576 | tf_op jit(solution)/shard_map/grad_down/pallas_call | solution.py:158
  332.2 8.5 %collective-permute-done.48.downward = bf16[128,2048]{1,0:T(8,128)(2,1)} collective-permute-done((bf16[128,2048]{1,0:T(8,128)(2,1)}, bf16[128,2048]{1,0:T(8,128)(2,1)}, u32[]{:S(2)}, u32[]{:S(2)}) %collective-permute-start.48) | collective-permute-done | bytes 524320 | tf_op jit(solution)/shard_map/ppermute | solution.py:61
  355.9 5.9 %collective-permute-done.52 = bf16[128,2048]{1,0:T(8,128)(2,1)S(1)} collective-permute-done((bf16[128,2048]{1,0:T(8,128)(2,1)S(1)}, bf16[128,2048]{1,0:T(8,128)(2,1)S(1)}, u32[]{:S(2)}, u32[]{:S(2)}) %collective-permute-start.52) | collective-permute-done | bytes 524320 | tf_op jit(solution)/shard_map/ppermute | solution.py:61
  376.1 4.9 collective-permute-done.55
  402.8 11.8 %attend_back.1 = bf16[1024,768]{1,0:T(8,128)(2,1)S(1)} custom-call(s32[33]{0:T(128)S(1)} %concatenate.100.table, bf16[1024,768]{1,0:T(8,128)(2,1)} %fusion.27.query.key.value, bf16[1024,768]{1,0:T(8,128)(2,1)} %fusion.27.query.key.value, bf16[1024,768]{1,0:T(8,128)(2,1)} %fusion.27.query.key.value, f32[2,1,1024]{2,1,0:T(1,128)} %copy-done.99, ...), custom_call_target="tpu_custom_call" | custom-call | flops 2684354560 | bytes 33554432 | tf_op jit(solution)/shard_map/attend_back/pallas_call | solution.py:295
  423.1 6.1 %grad_qkv.1 = bf16[2048,768]{1,0:T(8,128)(2,1)} custom-call(bf16[128,2048]{1,0:T(8,128)(2,1)S(1)} %copy-done.28, bf16[256,2048]{1,0:T(8,128)(2,1)S(1)} %copy-done.35, bf16[256,2048]{1,0:T(8,128)(2,1)S(1)} %copy-done.34, bf16[256,2048]{1,0:T(8,128)(2,1)S(1)} %copy-done.40, bf16[128,2048]{1,0:T(8,128)(2,1)S(1)} %copy-done.30, ...), custom_call_target="tpu_custom_call" | custom-call | flops 1048576 | bytes 1048576 | tf_op jit(solution)/shard_map/grad_qkv/pallas_call | solution.py:158
  445.6 5.4 %norm1_sums.1 = (f32[1,2048]{1,0:T(1,128)S(1)}, f32[1,2048]{1,0:T(1,128)S(1)}, f32[1,768]{1,0:T(1,128)S(1)}) custom-call(bf16[128,2048]{1,0:T(8,128)(2,1)S(1)} %get-tuple-element.329.refs_0_.part, bf16[256,2048]{1,0:T(8,128)(2,1)S(1)} %get-tuple-element.307.refs_1_, bf16[256,2048]{1,0:T(8,128)(2,1)S(1)} %get-tuple-element.308.refs_2_, ...), custom_call_target="tpu_custom_call" | custom-call | flops 1048576 | bytes 1048576 | tf_op jit(solution)/shard_map/norm1_sums/pallas_call | solution.py:504
  451.1 7.4 %collective-permute-done.63 = bf16[128,2048]{1,0:T(8,128)(2,1)S(1)} collective-permute-done((bf16[128,2048]{1,0:T(8,128)(2,1)S(1)}, bf16[128,2048]{1,0:T(8,128)(2,1)S(1)}, u32[]{:S(2)}, u32[]{:S(2)}) %collective-permute-start.63) | collective-permute-done | bytes 524320 | tf_op jit(solution)/shard_map/ppermute | solution.py:61
  479.0 5.1 all-to-all-start.3
  494.7 24.3 %collective-permute-done.70.downward = bf16[128,2048]{1,0:T(8,128)(2,1)} collective-permute-done((bf16[128,2048]{1,0:T(8,128)(2,1)}, bf16[128,2048]{1,0:T(8,128)(2,1)}, u32[]{:S(2)}, u32[]{:S(2)}) %collective-permute-start.70) | collective-permute-done | bytes 524320 | tf_op jit(solution)/shard_map/ppermute | solution.py:61
  (654 shorter events, 319.4 us)
Async XLA Ops:
  7.3 51.1 %all-gather.5.cloned.1.call-start = ((), (), s32[]{:S(2)}) async-start(), calls=%async_computation.8 | async-start | bytes 5242880 | tf_op jit(solution)/shard_map/all_gather | solution.py:568
  15.6 19.3 %collective-permute-start.1 = (bf16[128,2048]{1,0:T(8,128)(2,1)S(1)}, bf16[128,2048]{1,0:T(8,128)(2,1)}, u32[]{:S(2)}, u32[]{:S(2)}) collective-permute-start(bf16[128,2048]{1,0:T(8,128)(2,1)S(1)} %bitcast.131), channel_id=1, source_target_pairs={{8,0},{16,8},{24,16},{28,24},{20,28},{12,20},{4,12},{0,4},{9,1},{1... | collective-permute-start | bytes 1572872 | tf_op jit(solution)/shard_map/ppermute | solution.py:61
  17.7 40.7 %all-to-all-start = ((bf16[8,64,768]{2,1,0:T(8,128)(2,1)}), bf16[8,64,768]{2,1,0:T(8,128)(2,1)}, u32[]{:S(2)}, u32[]{:S(2)}) async-start(bf16[8,64,768]{2,1,0:T(8,128)(2,1)} %reshape.285), calls=%async_computation | async-start | bytes 1572864 | tf_op jit(solution)/shard_map/all_to_all | solution.py:128
  23.9 63.9 %all-gather.7.cloned.1.call-start = ((), (), s32[]{:S(2)}) async-start(), calls=%async_computation.9 | async-start | bytes 3932160 | tf_op jit(solution)/shard_map/all_gather | solution.py:334
  34.9 23.4 %collective-permute-start.3 = (bf16[128,2048]{1,0:T(8,128)(2,1)}, bf16[128,2048]{1,0:T(8,128)(2,1)}, u32[]{:S(2)}, u32[]{:S(2)}) collective-permute-start(bf16[128,2048]{1,0:T(8,128)(2,1)} %collective-permute-done.1), channel_id=1, source_target_pairs={{8,0},{16,8},{24,16},{28,24},{20,28},{12,20},{4,12},{0,4},{9,1},{1... | collective-permute-start | bytes 1572872 | tf_op jit(solution)/shard_map/ppermute | solution.py:61
  35.0 23.4 %collective-permute-start.2 = (bf16[128,2048]{1,0:T(8,128)(2,1)}, bf16[128,2048]{1,0:T(8,128)(2,1)}, u32[]{:S(2)}, u32[]{:S(2)}) collective-permute-start(bf16[128,2048]{1,0:T(8,128)(2,1)} %collective-permute-done), channel_id=1, source_target_pairs={{0,8},{8,16},{16,24},{24,28},{28,20},{20,12},{12,4},{4,0},{1,9},{9... | collective-permute-start | bytes 1572872 | tf_op jit(solution)/shard_map/ppermute | solution.py:61
  64.1 47.0 %all-to-all-start.1 = ((bf16[8,64,1024]{2,1,0:T(8,128)(2,1)}), bf16[8,64,1024]{2,1,0:T(8,128)(2,1)}, u32[]{:S(2)}, u32[]{:S(2)}) async-start(bf16[8,64,1024]{2,1,0:T(8,128)(2,1)} %copy.40), calls=%async_computation.1 | async-start | bytes 2097152 | tf_op jit(solution)/shard_map/all_to_all | solution.py:128
  70.6 40.5 %all-gather.9.cloned.1.call-start = ((), (), s32[]{:S(2)}) async-start(), calls=%async_computation.10 | async-start | bytes 1310720 | tf_op jit(solution)/shard_map/all_gather | solution.py:609
  75.5 82.5 %all-gather.11.cloned.1.call-start = ((), (), s32[]{:S(2)}) async-start(), calls=%async_computation.11 | async-start | bytes 5242880 | tf_op jit(solution)/shard_map/all_gather | solution.py:334
  82.5 20.0 %collective-permute-start.12 = (bf16[64,2048]{1,0:T(8,128)(2,1)}, bf16[64,2048]{1,0:T(8,128)(2,1)S(1)}, u32[]{:S(2)}, u32[]{:S(2)}) collective-permute-start(bf16[64,2048]{1,0:T(8,128)(2,1)} %slice.157), channel_id=1, source_target_pairs={{8,0},{16,8},{24,16},{28,24},{20,28},{12,20},{4,12},{0,4},{9,1},{1... | collective-permute-start | bytes 786440 | tf_op jit(solution)/shard_map/ppermute | solution.py:61
  116.7 265.1 %reduce-scatter.5.cloned.1.call-start = ((), (), s32[]{:S(2)}) async-start(), calls=%async_computation.12 | async-start | bytes 5242880 | tf_op jit(solution)/shard_map/reduce_scatter | solution.py:691
  198.4 19.3 %collective-permute-start.30 = (bf16[128,2048]{1,0:T(8,128)(2,1)S(1)}, bf16[128,2048]{1,0:T(8,128)(2,1)S(1)}, u32[]{:S(2)}, u32[]{:S(2)}) collective-permute-start(bf16[128,2048]{1,0:T(8,128)(2,1)S(1)} %add_convert_fusion.12.refs_0_), channel_id=1, source_target_pairs={{8,0},{16,8},{24,16},{28,24},{20,28},{12,20},{4,12},{0,4},{9,1},{1... | collective-permute-start | bytes 1572872 | tf_op jit(solution)/shard_map/ppermute | solution.py:61
  199.1 22.0 %collective-permute-start.29 = (bf16[128,2048]{1,0:T(8,128)(2,1)S(1)}, bf16[128,2048]{1,0:T(8,128)(2,1)S(1)}, u32[]{:S(2)}, u32[]{:S(2)}) collective-permute-start(bf16[128,2048]{1,0:T(8,128)(2,1)S(1)} %add_convert_fusion.12.refs_0_), channel_id=1, source_target_pairs={{0,8},{8,16},{16,24},{24,28},{28,20},{20,12},{12,4},{4,0},{1,9},{9... | collective-permute-start | bytes 1572872 | tf_op jit(solution)/shard_map/ppermute | solution.py:61
  290.5 125.3 %reduce-scatter.7.cloned.1.call-start = ((), (), s32[]{:S(2)}) async-start(), calls=%async_computation.13 | async-start | bytes 5242880 | tf_op jit(solution)/shard_map/reduce_scatter | solution.py:705
  319.0 21.6 %collective-permute-start.48 = (bf16[128,2048]{1,0:T(8,128)(2,1)}, bf16[128,2048]{1,0:T(8,128)(2,1)}, u32[]{:S(2)}, u32[]{:S(2)}) collective-permute-start(bf16[128,2048]{1,0:T(8,128)(2,1)} %get-tuple-element.361), channel_id=1, source_target_pairs={{8,0},{16,8},{24,16},{28,24},{20,28},{12,20},{4,12},{0,4},{9,1},{1... | collective-permute-start | bytes 1572872 | tf_op jit(solution)/shard_map/ppermute | solution.py:61
  320.5 22.1 %collective-permute-start.47 = (bf16[128,2048]{1,0:T(8,128)(2,1)}, bf16[128,2048]{1,0:T(8,128)(2,1)}, u32[]{:S(2)}, u32[]{:S(2)}) collective-permute-start(bf16[128,2048]{1,0:T(8,128)(2,1)} %get-tuple-element.362), channel_id=1, source_target_pairs={{0,8},{8,16},{16,24},{24,28},{28,20},{20,12},{12,4},{4,0},{1,9},{9... | collective-permute-start | bytes 1572872 | tf_op jit(solution)/shard_map/ppermute | solution.py:61
  342.7 133.9 %reduce-scatter.9.cloned.1.call-start = ((), (), s32[]{:S(2)}) async-start(), calls=%async_computation.14 | async-start | bytes 3932160 | tf_op jit(solution)/shard_map/reduce_scatter | solution.py:740
  430.7 28.7 %all-to-all-start.2 = ((bf16[8,64,1024]{2,1,0:T(8,128)(2,1)}), bf16[8,64,1024]{2,1,0:T(8,128)(2,1)}, u32[]{:S(2)}, u32[]{:S(2)}) async-start(bf16[8,64,1024]{2,1,0:T(8,128)(2,1)} %reduce-scatter.5.cloned.1.call-done), calls=%async_computation.4 | async-start | bytes 2097152 | tf_op jit(solution)/shard_map/all_to_all | solution.py:128
  435.5 92.9 %reduce-scatter.11.cloned.1.call-start = ((), (), s32[]{:S(2)}) async-start(), calls=%async_computation.15 | async-start | bytes 1310720 | tf_op jit(solution)/shard_map/reduce_scatter | solution.py:765
  438.3 20.2 %collective-permute-start.63 = (bf16[128,2048]{1,0:T(8,128)(2,1)S(1)}, bf16[128,2048]{1,0:T(8,128)(2,1)S(1)}, u32[]{:S(2)}, u32[]{:S(2)}) collective-permute-start(bf16[128,2048]{1,0:T(8,128)(2,1)S(1)} %pad_maximum_fusion.10), channel_id=1, source_target_pairs={{0,8},{8,16},{16,24},{24,28},{28,20},{20,12},{12,4},{4,0},{1,9},{9... | collective-permute-start | bytes 1572872 | tf_op jit(solution)/shard_map/ppermute | solution.py:61
  439.9 19.5 %collective-permute-start.64 = (bf16[128,2048]{1,0:T(8,128)(2,1)S(1)}, bf16[128,2048]{1,0:T(8,128)(2,1)}, u32[]{:S(2)}, u32[]{:S(2)}) collective-permute-start(bf16[128,2048]{1,0:T(8,128)(2,1)S(1)} %pad_maximum_fusion.11), channel_id=1, source_target_pairs={{8,0},{16,8},{24,16},{28,24},{20,28},{12,20},{4,12},{0,4},{9,1},{1... | collective-permute-start | bytes 1572872 | tf_op jit(solution)/shard_map/ppermute | solution.py:61
  479.0 40.0 %all-to-all-start.3 = ((bf16[8,80,768]{2,1,0:T(8,128)(2,1)}), bf16[8,80,768]{2,1,0:T(8,128)(2,1)}, u32[]{:S(2)}, u32[]{:S(2)}) async-start(bf16[8,80,768]{2,1,0:T(8,128)(2,1)} %copy-done.47), calls=%async_computation.6 | async-start | bytes 1966080 | tf_op jit(solution)/shard_map/all_to_all | solution.py:128
  486.7 32.3 %collective-permute-start.70 = (bf16[128,2048]{1,0:T(8,128)(2,1)}, bf16[128,2048]{1,0:T(8,128)(2,1)}, u32[]{:S(2)}, u32[]{:S(2)}) collective-permute-start(bf16[128,2048]{1,0:T(8,128)(2,1)} %get-tuple-element.349), channel_id=1, source_target_pairs={{8,0},{16,8},{24,16},{28,24},{20,28},{12,20},{4,12},{0,4},{9,1},{1... | collective-permute-start | bytes 1572872 | tf_op jit(solution)/shard_map/ppermute | solution.py:61
  486.7 32.3 %collective-permute-start.69 = (bf16[128,2048]{1,0:T(8,128)(2,1)}, bf16[128,2048]{1,0:T(8,128)(2,1)}, u32[]{:S(2)}, u32[]{:S(2)}) collective-permute-start(bf16[128,2048]{1,0:T(8,128)(2,1)} %get-tuple-element.350), channel_id=1, source_target_pairs={{0,8},{8,16},{16,24},{24,28},{28,20},{20,12},{12,4},{4,0},{1,9},{9... | collective-permute-start | bytes 1572872 | tf_op jit(solution)/shard_map/ppermute | solution.py:61
  (199 other events, 1955.4 us)
Sparse Core Ops, SparseCore 0:
  10.3 35.6 all-gather.4
  58.6 28.7 all-gather.6
  89.5 16.7 all-gather.8
  116.8 34.2 all-gather.10
  290.6 43.7 reduce-scatter.4
  342.8 44.0 reduce-scatter.6
  430.8 36.3 reduce-scatter.8
  479.1 24.0 reduce-scatter.10

commit v4 on v3

--- a/solution.py
+++ b/solution.py
@@ -356,7 +356,7 @@
 
 def norm_back(sums, rows, gain, direct, name, branch):
     n, width = rows.shape
-    step = 32
+    step = 64
 
     def body(part, upward, downward, rows_ref, gain_ref, direct_ref, grad_ref, *rest):
         @pl.when(pl.program_id(0) == 0)
@@ -431,7 +431,7 @@
 def with_rows(pieces, rows, name):
     places, n, width = pieces.shape
     more = -(-rows.shape[1] // width)
-    padded = -(-more // 16) * 16
+    padded = -(-more // 8) * 8
 
     def body(pieces_ref, rows_ref, out_ref):
         out_ref[:, :n, :] = pieces_ref[...]
@@ -708,7 +708,7 @@
         (d_second_parts[0], up, down), residual, gain2, own_cot, "norm2_back", True
     )
     low, high = hop(d_branch, d_branch)
-    out_up, out_down = hop(*next_sum(ffn_parts[1], out_up, out_down))
+    out_up, out_down = next_sum(ffn_parts[1], out_up, out_down)
     low, high, out_up, out_down = fence(low, high, out_up, out_down)
     d_branch_parts, d_attended = [d_branch], [dot(d_branch, out_slice, 1, 1, jnp.bfloat16)]
     for index in range(1, 5):
@@ -719,16 +719,21 @@
             low, high, grad_in, d_attended[index] = fence(low, high, grad_in, d_attended[index])
         elif index == 3:
             low, high = last_hop(low, high)
-            low, high, grad_in, d_attended[index] = fence(low, high, grad_in, d_attended[index])
+            low, high, grad_in, d_attended[index], out_up, out_down = fence(
+                low, high, grad_in, d_attended[index], out_up, out_down
+            )
             grad_in = exchange(grad_in)
 
+    out_up, out_down = hop(out_up, out_down)
     grads = attention(table, heads, my_heads, mixed, keys, first_key, d_attended, level)
     if sp == 1:
         (d_mixed,) = grads
     else:
         d_keys = half(lax.psum_scatter(full(grads[1]), "sp", scatter_dimension=0, tiled=True))
         d_mixed = jnp.concatenate([grads[0], d_keys], axis=1)
-    d_mixed, d_branch_parts[4], grad_down = fence(d_mixed, d_branch_parts[4], grad_down)
+    d_mixed, d_branch_parts[4], grad_down, out_up, out_down = fence(
+        d_mixed, d_branch_parts[4], grad_down, out_up, out_down
+    )
 
     mixed_parts = by_part(d_mixed)
     far = dot(mixed_parts[4], qkv_slice, 1, 1, jnp.bfloat16)

time: 548 us -> 538 us (0.982)
  waiting for transfers between devices: 172 us -> 166 us
    ppermute x64, waiting for transfers between devices: 149 us -> 143 us  [hop(): return (lax.ppermute(upward, 'tp', up), lax.ppermute(downward, 'tp', down))]
    unnamed x301 -> x289, local copies, waits for them, and re-layouts: 35 us -> 33 us
  transfers between devices with their start and end apart: 83 -> 83, of which waited for: 45 -> 43; matrix products, arithmetic and copies ran while one was open for 22% -> 22% of each run, Pallas kernels for 14% -> 14%
where the time goes in v4:
time: 538 us; the launch traced here: 530 us
  waiting for transfers between devices  166 us (31%)
  starting transfers between devices  115 us (21%)
  Pallas kernels  73.7 us (14%)
  local copies, waits for them, and re-layouts  59.8 us (11%)
  matrix products  54.9 us (10%)
  other arithmetic  44.9 us (8%)
  between operations  16.7 us (3%)
    ppermute x64, waiting for transfers between devices, hop(): return (lax.ppermute(upward, 'tp', up), lax.ppermute(downward, 'tp', down))  143 us
    ppermute x64, starting transfers between devices, hop(): return (lax.ppermute(upward, 'tp', up), lax.ppermute(downward, 'tp', down))  79.4 us
    dot_general x36, matrix products, dot(): lax.dot_general(left, right, (((left_dim,), (right_dim,)), ((), ())), pre...  54.9 us
    unnamed x289, local copies, waits for them, and re-layouts  33 us
    convert_element_type x21, other arithmetic, half(): return values.astype(jnp.bfloat16)  28.3 us
    pallas_call x4, Pallas kernels, rows_product(): pl.pallas_call(body, grid=(out_rows // tile,), in_specs=[pl.BlockSpec((v....  25 us
    all_to_all x4, starting transfers between devices, exchange(): return lax.all_to_all(pieces, 'tp', split_axis=0, concat_axis=0, tiled=True)  23.9 us
    ppermute x7, waiting for transfers between devices, swap(): return lax.ppermute(values, name, [(i, i ^ bit) for i in range(size)])  22.5 us
  transfers between devices with their start and end apart: 83, of which 43 were waited for; matrix products, arithmetic and copies ran while one was open for 22% of the time, Pallas kernels for 14%

profile of v4, /device:TPU:8, one launch (start us, length us, event | category | flops | bytes accessed | tf_op | source)
XLA Modules:
  0.0 530.3 jit_solution(1765051822560640030)
XLA Ops:
  17.7 6.3 %all-to-all-start = ((bf16[8,64,768]{2,1,0:T(8,128)(2,1)}), bf16[8,64,768]{2,1,0:T(8,128)(2,1)}, u32[]{:S(2)}, u32[]{:S(2)}) async-start(bf16[8,64,768]{2,1,0:T(8,128)(2,1)} %reshape.285), calls=%async_computation | async-start | bytes 1572864 | tf_op jit(solution)/shard_map/all_to_all | solution.py:128
  28.3 6.6 %collective-permute-start.7 = (bf16[8,768]{1,0:T(8,128)(2,1)S(1)}, bf16[8,768]{1,0:T(8,128)(2,1)S(1)}, u32[]{:S(2)}, u32[]{:S(2)}) collective-permute-start(bf16[8,768]{1,0:T(8,128)(2,1)S(1)} %pad_maximum_fusion.14), channel_id=1, source_target_pairs={{0,8},{4,12},{8,0},{12,4},{16,24},{20,28},{24,16},{28,20},{1,9},{5... | collective-permute-start | bytes 36872 | tf_op jit(solution)/shard_map/ppermute | solution.py:103
  37.9 5.9 %collective-permute-done.7 = bf16[8,768]{1,0:T(8,128)(2,1)S(1)} collective-permute-done((bf16[8,768]{1,0:T(8,128)(2,1)S(1)}, bf16[8,768]{1,0:T(8,128)(2,1)S(1)}, u32[]{:S(2)}, u32[]{:S(2)}) %collective-permute-start.7) | collective-permute-done | bytes 12320 | tf_op jit(solution)/shard_map/ppermute | solution.py:103
  46.4 11.4 %collective-permute-done.8 = bf16[16,768]{1,0:T(8,128)(2,1)S(1)} collective-permute-done((bf16[16,768]{1,0:T(8,128)(2,1)S(1)}, bf16[16,768]{1,0:T(8,128)(2,1)S(1)}, u32[]{:S(2)}, u32[]{:S(2)}) %collective-permute-start.8) | collective-permute-done | bytes 24608 | tf_op jit(solution)/shard_map/ppermute | solution.py:103
  64.1 6.5 %all-to-all-start.1 = ((bf16[8,64,1024]{2,1,0:T(8,128)(2,1)}), bf16[8,64,1024]{2,1,0:T(8,128)(2,1)}, u32[]{:S(2)}, u32[]{:S(2)}) async-start(bf16[8,64,1024]{2,1,0:T(8,128)(2,1)} %copy.40), calls=%async_computation.1 | async-start | bytes 2097152 | tf_op jit(solution)/shard_map/all_to_all | solution.py:128
  94.1 8.4 %collective-permute-done.12 = bf16[64,2048]{1,0:T(8,128)(2,1)S(1)} collective-permute-done((bf16[64,2048]{1,0:T(8,128)(2,1)}, bf16[64,2048]{1,0:T(8,128)(2,1)S(1)}, u32[]{:S(2)}, u32[]{:S(2)}) %collective-permute-start.12) | collective-permute-done | bytes 262176 | tf_op jit(solution)/shard_map/ppermute | solution.py:61
  119.8 9.7 %attend.1 = (bf16[1024,256]{1,0:T(8,128)(2,1)S(1)}, f32[2,1,1024]{2,1,0:T(1,128)S(1)}) custom-call(s32[33]{0:T(128)S(1)} %concatenate.100.table, bf16[1024,768]{1,0:T(8,128)(2,1)} %fusion.27.query.key.value, bf16[1024,768]{1,0:T(8,128)(2,1)} %fusion.27.query.key.value, bf16[1024,768]{1,0:T(8,128)(2,1)} %fusion.27.query.key.value), custom_call_target="tpu_custom_call" | custom-call | flops 1073741824 | bytes 33554432 | tf_op jit(solution)/shard_map/attend/pallas_call | solution.py:281
  141.2 7.0 %collective-permute-done.19 = bf16[128,2048]{1,0:T(8,128)(2,1)S(1)} collective-permute-done((bf16[128,2048]{1,0:T(8,128)(2,1)}, bf16[128,2048]{1,0:T(8,128)(2,1)S(1)}, u32[]{:S(2)}, u32[]{:S(2)}) %collective-permute-start.19) | collective-permute-done | bytes 524320 | tf_op jit(solution)/shard_map/ppermute | solution.py:61
  158.0 6.7 %copy.42 = bf16[8,256,1024]{2,1,0:T(8,128)(2,1)} copy(bf16[8,256,1024]{2,0,1:T(8,128)(2,1)} %all-gather.11.cloned.1.call-done) | data formatting | bytes 8388608 | tf_op jit(solution)/shard_map/all_gather | solution.py:334
  185.0 9.8 %collective-permute-done.28 = bf16[128,2048]{1,0:T(8,128)(2,1)} collective-permute-done((bf16[128,2048]{1,0:T(8,128)(2,1)}, bf16[128,2048]{1,0:T(8,128)(2,1)}, u32[]{:S(2)}, u32[]{:S(2)}) %collective-permute-start.28) | collective-permute-done | bytes 524320 | tf_op jit(solution)/shard_map/ppermute | solution.py:61
  199.2 10.7 %collective-permute-start.29 = (bf16[128,2048]{1,0:T(8,128)(2,1)S(1)}, bf16[128,2048]{1,0:T(8,128)(2,1)S(1)}, u32[]{:S(2)}, u32[]{:S(2)}) collective-permute-start(bf16[128,2048]{1,0:T(8,128)(2,1)S(1)} %add_convert_fusion.12.refs_0_), channel_id=1, source_target_pairs={{0,8},{8,16},{16,24},{24,28},{28,20},{20,12},{12,4},{4,0},{1,9},{9... | collective-permute-start | bytes 1572872 | tf_op jit(solution)/shard_map/ppermute | solution.py:61
  276.7 7.5 %grad_in.1 = bf16[2048,1024]{1,0:T(8,128)(2,1)} custom-call(bf16[128,2048]{1,0:T(8,128)(2,1)S(1)} %add_convert_fusion.12.refs_0_, bf16[256,2048]{1,0:T(8,128)(2,1)S(1)} %constant_dynamic-update-slice_fusion.12.refs_1_, bf16[256,2048]{1,0:T(8,128)(2,1)S(1)} %constant_dynamic-update-slice_fusion.14.refs_2_, ...), custom_call_target="tpu_custom_call" | custom-call | flops 1048576 | bytes 1048576 | tf_op jit(solution)/shard_map/grad_in/pallas_call | solution.py:158
  298.7 9.4 %collective-permute-done.45 = bf16[128,2048]{1,0:T(8,128)(2,1)S(1)} collective-permute-done((bf16[128,2048]{1,0:T(8,128)(2,1)S(1)}, bf16[128,2048]{1,0:T(8,128)(2,1)S(1)}, u32[]{:S(2)}, u32[]{:S(2)}) %collective-permute-start.45) | collective-permute-done | bytes 524320 | tf_op jit(solution)/shard_map/ppermute | solution.py:61
  308.2 5.6 %collective-permute-done.43 = bf16[128,2048]{1,0:T(8,128)(2,1)S(1)} collective-permute-done((bf16[128,2048]{1,0:T(8,128)(2,1)S(1)}, bf16[128,2048]{1,0:T(8,128)(2,1)S(1)}, u32[]{:S(2)}, u32[]{:S(2)}) %collective-permute-start.43) | collective-permute-done | bytes 524320 | tf_op jit(solution)/shard_map/ppermute | solution.py:61
  321.6 8.6 %grad_down.1 = bf16[1024,2048]{1,0:T(8,128)(2,1)} custom-call(bf16[128,1024]{1,0:T(8,128)(2,1)S(1)} %copy-done.77, bf16[256,1024]{1,0:T(8,128)(2,1)S(1)} %copy-done.82, bf16[256,1024]{1,0:T(8,128)(2,1)S(1)} %copy-done.84, bf16[256,1024]{1,0:T(8,128)(2,1)S(1)} %copy-done.86, bf16[128,1024]{1,0:T(8,128)(2,1)S(1)} %copy-done.79, ...), custom_call_target="tpu_custom_call" | custom-call | flops 1048576 | bytes 1048576 | tf_op jit(solution)/shard_map/grad_down/pallas_call | solution.py:158
  351.6 6.1 %collective-permute-done.52 = bf16[128,2048]{1,0:T(8,128)(2,1)S(1)} collective-permute-done((bf16[128,2048]{1,0:T(8,128)(2,1)S(1)}, bf16[128,2048]{1,0:T(8,128)(2,1)S(1)}, u32[]{:S(2)}, u32[]{:S(2)}) %collective-permute-start.52) | collective-permute-done | bytes 524320 | tf_op jit(solution)/shard_map/ppermute | solution.py:61
  361.9 8.3 %collective-permute-done.53 = bf16[128,2048]{1,0:T(8,128)(2,1)} collective-permute-done((bf16[128,2048]{1,0:T(8,128)(2,1)S(1)}, bf16[128,2048]{1,0:T(8,128)(2,1)}, u32[]{:S(2)}, u32[]{:S(2)}) %collective-permute-start.53) | collective-permute-done | bytes 524320 | tf_op jit(solution)/shard_map/ppermute | solution.py:61
  392.6 11.8 %attend_back.1 = bf16[1024,768]{1,0:T(8,128)(2,1)S(1)} custom-call(s32[33]{0:T(128)S(1)} %concatenate.100.table, bf16[1024,768]{1,0:T(8,128)(2,1)} %fusion.27.query.key.value, bf16[1024,768]{1,0:T(8,128)(2,1)} %fusion.27.query.key.value, bf16[1024,768]{1,0:T(8,128)(2,1)} %fusion.27.query.key.value, f32[2,1,1024]{2,1,0:T(1,128)} %copy-done.94, ...), custom_call_target="tpu_custom_call" | custom-call | flops 2684354560 | bytes 33554432 | tf_op jit(solution)/shard_map/attend_back/pallas_call | solution.py:295
  413.0 6.2 %grad_qkv.1 = bf16[2048,768]{1,0:T(8,128)(2,1)} custom-call(bf16[128,2048]{1,0:T(8,128)(2,1)S(1)} %copy-done.28, bf16[256,2048]{1,0:T(8,128)(2,1)S(1)} %copy-done.35, bf16[256,2048]{1,0:T(8,128)(2,1)S(1)} %copy-done.34, bf16[256,2048]{1,0:T(8,128)(2,1)S(1)} %copy-done.40, bf16[128,2048]{1,0:T(8,128)(2,1)S(1)} %copy-done.30, ...), custom_call_target="tpu_custom_call" | custom-call | flops 1048576 | bytes 1048576 | tf_op jit(solution)/shard_map/grad_qkv/pallas_call | solution.py:158
  422.8 5.6 %all-to-all-start.2 = ((bf16[8,64,1024]{2,1,0:T(8,128)(2,1)}), bf16[8,64,1024]{2,1,0:T(8,128)(2,1)}, u32[]{:S(2)}, u32[]{:S(2)}) async-start(bf16[8,64,1024]{2,1,0:T(8,128)(2,1)} %reduce-scatter.5.cloned.1.call-done), calls=%async_computation.4 | async-start | bytes 2097152 | tf_op jit(solution)/shard_map/all_to_all | solution.py:128
  438.5 5.4 %norm1_sums.1 = (f32[1,2048]{1,0:T(1,128)S(1)}, f32[1,2048]{1,0:T(1,128)S(1)}, f32[1,768]{1,0:T(1,128)S(1)}) custom-call(bf16[128,2048]{1,0:T(8,128)(2,1)S(1)} %get-tuple-element.337.refs_0_.part, bf16[256,2048]{1,0:T(8,128)(2,1)S(1)} %get-tuple-element.315.refs_1_, bf16[256,2048]{1,0:T(8,128)(2,1)S(1)} %get-tuple-element.316.refs_2_, ...), custom_call_target="tpu_custom_call" | custom-call | flops 1048576 | bytes 1048576 | tf_op jit(solution)/shard_map/norm1_sums/pallas_call | solution.py:504
  444.0 7.7 %collective-permute-done.63 = bf16[128,2048]{1,0:T(8,128)(2,1)S(1)} collective-permute-done((bf16[128,2048]{1,0:T(8,128)(2,1)S(1)}, bf16[128,2048]{1,0:T(8,128)(2,1)S(1)}, u32[]{:S(2)}, u32[]{:S(2)}) %collective-permute-start.63) | collective-permute-done | bytes 524320 | tf_op jit(solution)/shard_map/ppermute | solution.py:61
  473.3 5.4 %all-to-all-start.3 = ((bf16[8,72,768]{2,1,0:T(8,128)(2,1)}), bf16[8,72,768]{2,1,0:T(8,128)(2,1)}, u32[]{:S(2)}, u32[]{:S(2)}) async-start(bf16[8,72,768]{2,1,0:T(8,128)(2,1)} %qkv_with_sums.1), calls=%async_computation.6 | async-start | bytes 1769472 | tf_op jit(solution)/shard_map/all_to_all | solution.py:128
  488.4 22.6 %collective-permute-done.70.downward = bf16[128,2048]{1,0:T(8,128)(2,1)} collective-permute-done((bf16[128,2048]{1,0:T(8,128)(2,1)}, bf16[128,2048]{1,0:T(8,128)(2,1)}, u32[]{:S(2)}, u32[]{:S(2)}) %collective-permute-start.70) | collective-permute-done | bytes 524320 | tf_op jit(solution)/shard_map/ppermute | solution.py:61
  (642 shorter events, 314.3 us)
Async XLA Ops:
  7.3 51.1 %all-gather.5.cloned.1.call-start = ((), (), s32[]{:S(2)}) async-start(), calls=%async_computation.8 | async-start | bytes 5242880 | tf_op jit(solution)/shard_map/all_gather | solution.py:568
  15.6 19.3 %collective-permute-start.1 = (bf16[128,2048]{1,0:T(8,128)(2,1)S(1)}, bf16[128,2048]{1,0:T(8,128)(2,1)}, u32[]{:S(2)}, u32[]{:S(2)}) collective-permute-start(bf16[128,2048]{1,0:T(8,128)(2,1)S(1)} %bitcast.131), channel_id=1, source_target_pairs={{8,0},{16,8},{24,16},{28,24},{20,28},{12,20},{4,12},{0,4},{9,1},{1... | collective-permute-start | bytes 1572872 | tf_op jit(solution)/shard_map/ppermute | solution.py:61
  16.1 18.9 %collective-permute-start = (bf16[128,2048]{1,0:T(8,128)(2,1)S(1)}, bf16[128,2048]{1,0:T(8,128)(2,1)}, u32[]{:S(2)}, u32[]{:S(2)}) collective-permute-start(bf16[128,2048]{1,0:T(8,128)(2,1)S(1)} %bitcast.132), channel_id=1, source_target_pairs={{0,8},{8,16},{16,24},{24,28},{28,20},{20,12},{12,4},{4,0},{1,9},{9... | collective-permute-start | bytes 1572872 | tf_op jit(solution)/shard_map/ppermute | solution.py:61
  17.7 40.7 %all-to-all-start = ((bf16[8,64,768]{2,1,0:T(8,128)(2,1)}), bf16[8,64,768]{2,1,0:T(8,128)(2,1)}, u32[]{:S(2)}, u32[]{:S(2)}) async-start(bf16[8,64,768]{2,1,0:T(8,128)(2,1)} %reshape.285), calls=%async_computation | async-start | bytes 1572864 | tf_op jit(solution)/shard_map/all_to_all | solution.py:128
  23.9 63.9 %all-gather.7.cloned.1.call-start = ((), (), s32[]{:S(2)}) async-start(), calls=%async_computation.9 | async-start | bytes 3932160 | tf_op jit(solution)/shard_map/all_gather | solution.py:334
  34.9 23.4 %collective-permute-start.3 = (bf16[128,2048]{1,0:T(8,128)(2,1)}, bf16[128,2048]{1,0:T(8,128)(2,1)}, u32[]{:S(2)}, u32[]{:S(2)}) collective-permute-start(bf16[128,2048]{1,0:T(8,128)(2,1)} %collective-permute-done.1), channel_id=1, source_target_pairs={{8,0},{16,8},{24,16},{28,24},{20,28},{12,20},{4,12},{0,4},{9,1},{1... | collective-permute-start | bytes 1572872 | tf_op jit(solution)/shard_map/ppermute | solution.py:61
  35.0 23.4 %collective-permute-start.2 = (bf16[128,2048]{1,0:T(8,128)(2,1)}, bf16[128,2048]{1,0:T(8,128)(2,1)}, u32[]{:S(2)}, u32[]{:S(2)}) collective-permute-start(bf16[128,2048]{1,0:T(8,128)(2,1)} %collective-permute-done), channel_id=1, source_target_pairs={{0,8},{8,16},{16,24},{24,28},{28,20},{20,12},{12,4},{4,0},{1,9},{9... | collective-permute-start | bytes 1572872 | tf_op jit(solution)/shard_map/ppermute | solution.py:61
  64.1 47.0 %all-to-all-start.1 = ((bf16[8,64,1024]{2,1,0:T(8,128)(2,1)}), bf16[8,64,1024]{2,1,0:T(8,128)(2,1)}, u32[]{:S(2)}, u32[]{:S(2)}) async-start(bf16[8,64,1024]{2,1,0:T(8,128)(2,1)} %copy.40), calls=%async_computation.1 | async-start | bytes 2097152 | tf_op jit(solution)/shard_map/all_to_all | solution.py:128
  70.6 40.5 %all-gather.9.cloned.1.call-start = ((), (), s32[]{:S(2)}) async-start(), calls=%async_computation.10 | async-start | bytes 1310720 | tf_op jit(solution)/shard_map/all_gather | solution.py:609
  75.5 82.5 %all-gather.11.cloned.1.call-start = ((), (), s32[]{:S(2)}) async-start(), calls=%async_computation.11 | async-start | bytes 5242880 | tf_op jit(solution)/shard_map/all_gather | solution.py:334
  82.5 20.1 %collective-permute-start.12 = (bf16[64,2048]{1,0:T(8,128)(2,1)}, bf16[64,2048]{1,0:T(8,128)(2,1)S(1)}, u32[]{:S(2)}, u32[]{:S(2)}) collective-permute-start(bf16[64,2048]{1,0:T(8,128)(2,1)} %slice.157), channel_id=1, source_target_pairs={{8,0},{16,8},{24,16},{28,24},{20,28},{12,20},{4,12},{0,4},{9,1},{1... | collective-permute-start | bytes 786440 | tf_op jit(solution)/shard_map/ppermute | solution.py:61
  116.7 253.5 %reduce-scatter.5.cloned.1.call-start = ((), (), s32[]{:S(2)}) async-start(), calls=%async_computation.12 | async-start | bytes 5242880 | tf_op jit(solution)/shard_map/reduce_scatter | solution.py:691
  197.9 19.3 %collective-permute-start.30 = (bf16[128,2048]{1,0:T(8,128)(2,1)S(1)}, bf16[128,2048]{1,0:T(8,128)(2,1)S(1)}, u32[]{:S(2)}, u32[]{:S(2)}) collective-permute-start(bf16[128,2048]{1,0:T(8,128)(2,1)S(1)} %add_convert_fusion.12.refs_0_), channel_id=1, source_target_pairs={{8,0},{16,8},{24,16},{28,24},{20,28},{12,20},{4,12},{0,4},{9,1},{1... | collective-permute-start | bytes 1572872 | tf_op jit(solution)/shard_map/ppermute | solution.py:61
  199.2 22.0 %collective-permute-start.29 = (bf16[128,2048]{1,0:T(8,128)(2,1)S(1)}, bf16[128,2048]{1,0:T(8,128)(2,1)S(1)}, u32[]{:S(2)}, u32[]{:S(2)}) collective-permute-start(bf16[128,2048]{1,0:T(8,128)(2,1)S(1)} %add_convert_fusion.12.refs_0_), channel_id=1, source_target_pairs={{0,8},{8,16},{16,24},{24,28},{28,20},{20,12},{12,4},{4,0},{1,9},{9... | collective-permute-start | bytes 1572872 | tf_op jit(solution)/shard_map/ppermute | solution.py:61
  290.9 114.7 %reduce-scatter.7.cloned.1.call-start = ((), (), s32[]{:S(2)}) async-start(), calls=%async_computation.13 | async-start | bytes 5242880 | tf_op jit(solution)/shard_map/reduce_scatter | solution.py:705
  320.4 20.0 %collective-permute-start.47 = (bf16[128,2048]{1,0:T(8,128)(2,1)}, bf16[128,2048]{1,0:T(8,128)(2,1)}, u32[]{:S(2)}, u32[]{:S(2)}) collective-permute-start(bf16[128,2048]{1,0:T(8,128)(2,1)} %get-tuple-element.370), channel_id=1, source_target_pairs={{0,8},{8,16},{16,24},{24,28},{28,20},{20,12},{12,4},{4,0},{1,9},{9... | collective-permute-start | bytes 1572872 | tf_op jit(solution)/shard_map/ppermute | solution.py:61
  340.4 130.6 %reduce-scatter.9.cloned.1.call-start = ((), (), s32[]{:S(2)}) async-start(), calls=%async_computation.14 | async-start | bytes 3932160 | tf_op jit(solution)/shard_map/reduce_scatter | solution.py:745
  422.8 31.4 %all-to-all-start.2 = ((bf16[8,64,1024]{2,1,0:T(8,128)(2,1)}), bf16[8,64,1024]{2,1,0:T(8,128)(2,1)}, u32[]{:S(2)}, u32[]{:S(2)}) async-start(bf16[8,64,1024]{2,1,0:T(8,128)(2,1)} %reduce-scatter.5.cloned.1.call-done), calls=%async_computation.4 | async-start | bytes 2097152 | tf_op jit(solution)/shard_map/all_to_all | solution.py:128
  428.5 93.0 %reduce-scatter.11.cloned.1.call-start = ((), (), s32[]{:S(2)}) async-start(), calls=%async_computation.15 | async-start | bytes 1310720 | tf_op jit(solution)/shard_map/reduce_scatter | solution.py:770
  431.2 20.5 %collective-permute-start.63 = (bf16[128,2048]{1,0:T(8,128)(2,1)S(1)}, bf16[128,2048]{1,0:T(8,128)(2,1)S(1)}, u32[]{:S(2)}, u32[]{:S(2)}) collective-permute-start(bf16[128,2048]{1,0:T(8,128)(2,1)S(1)} %pad_maximum_fusion.10), channel_id=1, source_target_pairs={{0,8},{8,16},{16,24},{24,28},{28,20},{20,12},{12,4},{4,0},{1,9},{9... | collective-permute-start | bytes 1572872 | tf_op jit(solution)/shard_map/ppermute | solution.py:61
  432.8 21.5 %collective-permute-start.64 = (bf16[128,2048]{1,0:T(8,128)(2,1)S(1)}, bf16[128,2048]{1,0:T(8,128)(2,1)}, u32[]{:S(2)}, u32[]{:S(2)}) collective-permute-start(bf16[128,2048]{1,0:T(8,128)(2,1)S(1)} %pad_maximum_fusion.11), channel_id=1, source_target_pairs={{8,0},{16,8},{24,16},{28,24},{20,28},{12,20},{4,12},{0,4},{9,1},{1... | collective-permute-start | bytes 1572872 | tf_op jit(solution)/shard_map/ppermute | solution.py:61
  473.3 37.8 %all-to-all-start.3 = ((bf16[8,72,768]{2,1,0:T(8,128)(2,1)}), bf16[8,72,768]{2,1,0:T(8,128)(2,1)}, u32[]{:S(2)}, u32[]{:S(2)}) async-start(bf16[8,72,768]{2,1,0:T(8,128)(2,1)} %qkv_with_sums.1), calls=%async_computation.6 | async-start | bytes 1769472 | tf_op jit(solution)/shard_map/all_to_all | solution.py:128
  481.5 29.6 %collective-permute-start.70 = (bf16[128,2048]{1,0:T(8,128)(2,1)}, bf16[128,2048]{1,0:T(8,128)(2,1)}, u32[]{:S(2)}, u32[]{:S(2)}) collective-permute-start(bf16[128,2048]{1,0:T(8,128)(2,1)} %get-tuple-element.357), channel_id=1, source_target_pairs={{8,0},{16,8},{24,16},{28,24},{20,28},{12,20},{4,12},{0,4},{9,1},{1... | collective-permute-start | bytes 1572872 | tf_op jit(solution)/shard_map/ppermute | solution.py:61
  481.5 29.6 %collective-permute-start.69 = (bf16[128,2048]{1,0:T(8,128)(2,1)}, bf16[128,2048]{1,0:T(8,128)(2,1)}, u32[]{:S(2)}, u32[]{:S(2)}) collective-permute-start(bf16[128,2048]{1,0:T(8,128)(2,1)} %get-tuple-element.358), channel_id=1, source_target_pairs={{0,8},{8,16},{16,24},{24,28},{28,20},{20,12},{12,4},{4,0},{1,9},{9... | collective-permute-start | bytes 1572872 | tf_op jit(solution)/shard_map/ppermute | solution.py:61
  (193 other events, 1824.6 us)
Sparse Core Ops, SparseCore 0:
  10.3 35.6 all-gather.4
  58.6 28.7 all-gather.6
  89.5 16.7 all-gather.8
  116.9 34.2 all-gather.10
  291.0 43.2 reduce-scatter.4
  340.5 43.9 reduce-scatter.6
  422.9 38.1 reduce-scatter.8
  473.4 24.1 reduce-scatter.10

commit v5 on v4

--- a/solution.py
+++ b/solution.py
@@ -626,7 +626,8 @@
     mixed, cot_low1, cot_high1, in_pieces, out_slice = fence(
         mixed, cot_low1, cot_high1, in_pieces, out_slice
     )
-    in_slice = gather_rows(in_pieces)
+    in_slice = lax.all_gather(in_pieces, TOKENS, axis=0, tiled=False)
+    in_slice = in_slice.transpose(1, 0, 2, 3).reshape(-1, hidden)
     cot_low2, cot_high2 = hop(cot_low1, cot_high1)
     keys = mixed
     if sp > 1:
@@ -643,13 +644,13 @@
         branch_low, branch_high, cot_low3, cot_high3, *branch_parts
     )
     up, down = hop(*first_sum(branch_parts[3], branch_low, branch_high))
-    cot_low4, cot_high4 = last_hop(cot_low3, cot_high3)
-    up, down, cot_low4, cot_high4, in_slice = fence(up, down, cot_low4, cot_high4, in_slice)
+    up, down, in_slice = fence(up, down, in_slice)
     up, down = hop(*next_sum(branch_parts[2], up, down))
     cot_parts = [own_cot, join((cot_low1, cot_high1)), join((cot_low2, cot_high2))]
-    cot_parts += [join((cot_low3, cot_high3)), join((cot_low4, cot_high4))]
+    cot_parts.append(join((cot_low3, cot_high3)))
     up, down, *cot_parts = fence(up, down, *cot_parts)
-    up, down = fence(*hop(*next_sum(branch_parts[1], up, down)))
+    up, down = hop(*next_sum(branch_parts[1], up, down))
+    up, down, cot_low3, cot_high3 = fence(up, down, cot_low3, cot_high3)
     residual = full(own) + last_sum(branch_parts[0], up, down) + out_bias
 
     own_normed2, scale2 = normalize(residual)
@@ -661,6 +662,7 @@
             new_low, new_high = hop(low, high)
         elif index == 3:
             new_low, new_high = last_hop(low, high)
+            cot_low4, cot_high4 = last_hop(cot_low3, cot_high3)
         if index:
             second_parts.append(join((low, high)))
         pre_act = dot(second_parts[index], in_slice, 1, 0) + in_bias
@@ -677,6 +679,9 @@
             low, high, *held = fence(new_low, new_high, *[parts[index] for parts in made])
             for parts, value in zip(made, held, strict=True):
                 parts[index] = value
+        if index == 3:
+            low, cot_low4, cot_high4 = fence(low, cot_low4, cot_high4)
+            cot_parts.append(join((cot_low4, cot_high4)))
 
     low, high = hop(*jnp.split(d_second_parts[4], 2))
     ffn_parts += [dot(act, down_slice, 1, 0, jnp.bfloat16) for act in act_parts[3:]]
@@ -746,12 +751,11 @@
     up, down = hop(*first_sum(near, low, high))
     d_normed = [*products(mixed_parts[:3], qkv_slice, "d_normed"), near, far]
     g_gain1, g_bias1, mixed_sum = norm_sums(d_normed, token_parts, mixed_parts, "norm1_sums")
-    up, down, grad_in, g_gain1, g_bias1, mixed_sum, *d_normed[:3] = fence(
-        up, down, grad_in, g_gain1, g_bias1, mixed_sum, *d_normed[:3]
+    grad_out = rows_product(attended_parts, d_branch_parts, 128, "grad_out")
+    up, down, grad_in, grad_out, g_gain1, g_bias1, mixed_sum, *d_normed[:3] = fence(
+        up, down, grad_in, grad_out, g_gain1, g_bias1, mixed_sum, *d_normed[:3]
     )
     up, down = hop(*next_sum(d_normed[2], up, down))
-    grad_out = rows_product(attended_parts, d_branch_parts, 128, "grad_out")
-    grad_w_in = from_places(grad_in, 1, "in_back")
     grad_b_qv = jnp.zeros((2, width), jnp.float32)
     for i in range(2):
         piece = mixed_sum[:, 2 * i * head_cols : (2 * i + 1) * head_cols]
@@ -761,12 +765,15 @@
     summed = sum_small(summed, TOKENS)
     own_rows = grad_qkv.shape[1]
     grad_qkv = with_rows(grad_qkv, summed, "qkv_with_sums")
-    up, down, grad_out, grad_w_in, grad_qkv = fence(up, down, grad_out, grad_w_in, grad_qkv)
+    up, down, grad_out, grad_in, grad_qkv = fence(up, down, grad_out, grad_in, grad_qkv)
     up, down = hop(*next_sum(d_normed[1], up, down))
     grad_qkv = exchange(grad_qkv)
+    grad_w_in = from_places(grad_in, 1, "in_back")
     grad_w_down = converted(grad_down, "down_back")
     output = total((ffn_parts[0], out_up, out_down), residual, down_bias, "output")
-    up, down, grad_w_down, output, grad_qkv = fence(up, down, grad_w_down, output, grad_qkv)
+    up, down, grad_w_down, grad_w_in, output, grad_qkv = fence(
+        up, down, grad_w_down, grad_w_in, output, grad_qkv
+    )
     grad_out = lax.psum_scatter(grad_out, TOKENS, scatter_dimension=0, tiled=True)
     grad_tokens = norm_back((d_normed[0], up, down), own, gain1, d_residual, "norm1_back", False)[0]
     grad_w_out = converted(grad_out, "out_back")

time: 538 us -> 526 us (0.978)
  starting transfers between devices: 115 us -> 107 us
    ppermute x64, waiting for transfers between devices: 143 us -> 134 us  [hop(): return (lax.ppermute(upward, 'tp', up), lax.ppermute(downward, 'tp', down))]
    ppermute x64, starting transfers between devices: 79.4 us -> 71.8 us  [hop(): return (lax.ppermute(upward, 'tp', up), lax.ppermute(downward, 'tp', down))]
    all_gather x1 -> x0, local copies, waits for them, and re-layouts: 6.65 us -> none  [gather_rows(): rows = lax.all_gather(rows, TOKENS, axis=1, tiled=True)]
    unnamed x289 -> x292, local copies, waits for them, and re-layouts: 33 us -> 35.9 us
  transfers between devices with their start and end apart: 83 -> 83, of which waited for: 43 -> 42; matrix products, arithmetic and copies ran while one was open for 22% -> 23% of each run, Pallas kernels for 14% -> 14%
where the time goes in v5:
time: 526 us; the launch traced here: 516 us
  waiting for transfers between devices  161 us (31%)
  starting transfers between devices  107 us (20%)
  Pallas kernels  73.8 us (14%)
  local copies, waits for them, and re-layouts  57 us (11%)
  matrix products  54.9 us (10%)
  other arithmetic  45.7 us (9%)
  between operations  16.9 us (3%)
    ppermute x64, waiting for transfers between devices, hop(): return (lax.ppermute(upward, 'tp', up), lax.ppermute(downward, 'tp', down))  134 us
    ppermute x64, starting transfers between devices, hop(): return (lax.ppermute(upward, 'tp', up), lax.ppermute(downward, 'tp', down))  71.8 us
    dot_general x36, matrix products, dot(): lax.dot_general(left, right, (((left_dim,), (right_dim,)), ((), ())), pre...  54.9 us
    unnamed x292, local copies, waits for them, and re-layouts  35.9 us
    convert_element_type x21, other arithmetic, half(): return values.astype(jnp.bfloat16)  29.4 us
    ppermute x7, waiting for transfers between devices, swap(): return lax.ppermute(values, name, [(i, i ^ bit) for i in range(size)])  26.2 us
    pallas_call x4, Pallas kernels, rows_product(): pl.pallas_call(body, grid=(out_rows // tile,), in_specs=[pl.BlockSpec((v....  25 us
    all_to_all x4, starting transfers between devices, exchange(): return lax.all_to_all(pieces, 'tp', split_axis=0, concat_axis=0, tiled=True)  23.8 us
  transfers between devices with their start and end apart: 83, of which 42 were waited for; matrix products, arithmetic and copies ran while one was open for 23% of the time, Pallas kernels for 14%

profile of v5, /device:TPU:8, one launch (start us, length us, event | category | flops | bytes accessed | tf_op | source)
XLA Modules:
  0.0 516.1 jit_solution(3931094162978069330)
XLA Ops:
  17.7 6.3 %all-to-all-start = ((bf16[8,64,768]{2,1,0:T(8,128)(2,1)}), bf16[8,64,768]{2,1,0:T(8,128)(2,1)}, u32[]{:S(2)}, u32[]{:S(2)}) async-start(bf16[8,64,768]{2,1,0:T(8,128)(2,1)} %reshape.285), calls=%async_computation | async-start | bytes 1572864 | tf_op jit(solution)/shard_map/all_to_all | solution.py:128
  28.3 6.6 %collective-permute-start.7 = (bf16[8,768]{1,0:T(8,128)(2,1)S(1)}, bf16[8,768]{1,0:T(8,128)(2,1)S(1)}, u32[]{:S(2)}, u32[]{:S(2)}) collective-permute-start(bf16[8,768]{1,0:T(8,128)(2,1)S(1)} %pad_maximum_fusion.13), channel_id=1, source_target_pairs={{0,8},{4,12},{8,0},{12,4},{16,24},{20,28},{24,16},{28,20},{1,9},{5... | collective-permute-start | bytes 36872 | tf_op jit(solution)/shard_map/ppermute | solution.py:103
  37.9 5.9 %collective-permute-done.7 = bf16[8,768]{1,0:T(8,128)(2,1)S(1)} collective-permute-done((bf16[8,768]{1,0:T(8,128)(2,1)S(1)}, bf16[8,768]{1,0:T(8,128)(2,1)S(1)}, u32[]{:S(2)}, u32[]{:S(2)}) %collective-permute-start.7) | collective-permute-done | bytes 12320 | tf_op jit(solution)/shard_map/ppermute | solution.py:103
  46.4 11.4 %collective-permute-done.8 = bf16[16,768]{1,0:T(8,128)(2,1)S(1)} collective-permute-done((bf16[16,768]{1,0:T(8,128)(2,1)S(1)}, bf16[16,768]{1,0:T(8,128)(2,1)S(1)}, u32[]{:S(2)}, u32[]{:S(2)}) %collective-permute-start.8) | collective-permute-done | bytes 24608 | tf_op jit(solution)/shard_map/ppermute | solution.py:103
  64.1 6.5 %all-to-all-start.1 = ((bf16[8,64,1024]{2,1,0:T(8,128)(2,1)}), bf16[8,64,1024]{2,1,0:T(8,128)(2,1)}, u32[]{:S(2)}, u32[]{:S(2)}) async-start(bf16[8,64,1024]{2,1,0:T(8,128)(2,1)} %copy.45), calls=%async_computation.1 | async-start | bytes 2097152 | tf_op jit(solution)/shard_map/all_to_all | solution.py:128
  94.1 8.4 %collective-permute-done.12 = bf16[64,2048]{1,0:T(8,128)(2,1)S(1)} collective-permute-done((bf16[64,2048]{1,0:T(8,128)(2,1)}, bf16[64,2048]{1,0:T(8,128)(2,1)S(1)}, u32[]{:S(2)}, u32[]{:S(2)}) %collective-permute-start.12) | collective-permute-done | bytes 262176 | tf_op jit(solution)/shard_map/ppermute | solution.py:61
  117.8 9.7 %attend.1 = (bf16[1024,256]{1,0:T(8,128)(2,1)S(1)}, f32[2,1,1024]{2,1,0:T(1,128)S(1)}) custom-call(s32[33]{0:T(128)S(1)} %concatenate.100.table, bf16[1024,768]{1,0:T(8,128)(2,1)} %fusion.27.query.key.value, bf16[1024,768]{1,0:T(8,128)(2,1)} %fusion.27.query.key.value, bf16[1024,768]{1,0:T(8,128)(2,1)} %fusion.27.query.key.value), custom_call_target="tpu_custom_call" | custom-call | flops 1073741824 | bytes 33554432 | tf_op jit(solution)/shard_map/attend/pallas_call | solution.py:281
  138.7 6.4 %collective-permute-done.19 = bf16[128,2048]{1,0:T(8,128)(2,1)S(1)} collective-permute-done((bf16[128,2048]{1,0:T(8,128)(2,1)}, bf16[128,2048]{1,0:T(8,128)(2,1)S(1)}, u32[]{:S(2)}, u32[]{:S(2)}) %collective-permute-start.19) | collective-permute-done | bytes 524320 | tf_op jit(solution)/shard_map/ppermute | solution.py:61
  149.8 5.0 copy.46
  174.7 6.9 %collective-permute-done.26 = bf16[128,2048]{1,0:T(8,128)(2,1)} collective-permute-done((bf16[128,2048]{1,0:T(8,128)(2,1)}, bf16[128,2048]{1,0:T(8,128)(2,1)}, u32[]{:S(2)}, u32[]{:S(2)}) %collective-permute-start.26) | collective-permute-done | bytes 524320 | tf_op jit(solution)/shard_map/ppermute | solution.py:61
  258.8 7.6 %grad_in.1 = bf16[2048,1024]{1,0:T(8,128)(2,1)} custom-call(bf16[128,2048]{1,0:T(8,128)(2,1)S(1)} %add_convert_fusion.12.refs_0_, bf16[256,2048]{1,0:T(8,128)(2,1)S(1)} %constant_dynamic-update-slice_fusion.12.refs_1_, bf16[256,2048]{1,0:T(8,128)(2,1)S(1)} %constant_dynamic-update-slice_fusion.14.refs_2_, ...), custom_call_target="tpu_custom_call" | custom-call | flops 1048576 | bytes 1048576 | tf_op jit(solution)/shard_map/grad_in/pallas_call | solution.py:158
  281.1 5.5 %collective-permute-done.45 = bf16[128,2048]{1,0:T(8,128)(2,1)S(1)} collective-permute-done((bf16[128,2048]{1,0:T(8,128)(2,1)S(1)}, bf16[128,2048]{1,0:T(8,128)(2,1)S(1)}, u32[]{:S(2)}, u32[]{:S(2)}) %collective-permute-start.45) | collective-permute-done | bytes 524320 | tf_op jit(solution)/shard_map/ppermute | solution.py:61
  289.2 8.7 %collective-permute-done.43 = bf16[128,2048]{1,0:T(8,128)(2,1)S(1)} collective-permute-done((bf16[128,2048]{1,0:T(8,128)(2,1)S(1)}, bf16[128,2048]{1,0:T(8,128)(2,1)S(1)}, u32[]{:S(2)}, u32[]{:S(2)}) %collective-permute-start.43) | collective-permute-done | bytes 524320 | tf_op jit(solution)/shard_map/ppermute | solution.py:61
  308.6 8.5 %grad_down.1 = bf16[1024,2048]{1,0:T(8,128)(2,1)} custom-call(bf16[128,1024]{1,0:T(8,128)(2,1)S(1)} %copy-done.79, bf16[256,1024]{1,0:T(8,128)(2,1)S(1)} %copy-done.84, bf16[256,1024]{1,0:T(8,128)(2,1)S(1)} %copy-done.86, bf16[256,1024]{1,0:T(8,128)(2,1)S(1)} %copy-done.88, bf16[128,1024]{1,0:T(8,128)(2,1)S(1)} %copy-done.81, ...), custom_call_target="tpu_custom_call" | custom-call | flops 1048576 | bytes 1048576 | tf_op jit(solution)/shard_map/grad_down/pallas_call | solution.py:158
  317.1 5.5 %collective-permute-done.48.downward = bf16[128,2048]{1,0:T(8,128)(2,1)} collective-permute-done((bf16[128,2048]{1,0:T(8,128)(2,1)}, bf16[128,2048]{1,0:T(8,128)(2,1)}, u32[]{:S(2)}, u32[]{:S(2)}) %collective-permute-start.48) | collective-permute-done | bytes 524320 | tf_op jit(solution)/shard_map/ppermute | solution.py:61
  336.2 7.4 %collective-permute-done.52 = bf16[128,2048]{1,0:T(8,128)(2,1)S(1)} collective-permute-done((bf16[128,2048]{1,0:T(8,128)(2,1)S(1)}, bf16[128,2048]{1,0:T(8,128)(2,1)S(1)}, u32[]{:S(2)}, u32[]{:S(2)}) %collective-permute-start.52) | collective-permute-done | bytes 524320 | tf_op jit(solution)/shard_map/ppermute | solution.py:61
  350.6 7.8 %collective-permute-done.53 = bf16[128,2048]{1,0:T(8,128)(2,1)} collective-permute-done((bf16[128,2048]{1,0:T(8,128)(2,1)S(1)}, bf16[128,2048]{1,0:T(8,128)(2,1)}, u32[]{:S(2)}, u32[]{:S(2)}) %collective-permute-start.53) | collective-permute-done | bytes 524320 | tf_op jit(solution)/shard_map/ppermute | solution.py:61
  365.4 5.0 collective-permute-done.55
  382.7 11.8 %attend_back.1 = bf16[1024,768]{1,0:T(8,128)(2,1)S(1)} custom-call(s32[33]{0:T(128)S(1)} %concatenate.100.table, bf16[1024,768]{1,0:T(8,128)(2,1)} %fusion.27.query.key.value, bf16[1024,768]{1,0:T(8,128)(2,1)} %fusion.27.query.key.value, bf16[1024,768]{1,0:T(8,128)(2,1)} %fusion.27.query.key.value, f32[2,1,1024]{2,1,0:T(1,128)} %copy-done.94, ...), custom_call_target="tpu_custom_call" | custom-call | flops 2684354560 | bytes 33554432 | tf_op jit(solution)/shard_map/attend_back/pallas_call | solution.py:295
  403.2 6.1 %grad_qkv.1 = bf16[2048,768]{1,0:T(8,128)(2,1)} custom-call(bf16[128,2048]{1,0:T(8,128)(2,1)S(1)} %copy-done.30, bf16[256,2048]{1,0:T(8,128)(2,1)S(1)} %copy-done.37, bf16[256,2048]{1,0:T(8,128)(2,1)S(1)} %copy-done.36, bf16[256,2048]{1,0:T(8,128)(2,1)S(1)} %copy-done.42, bf16[128,2048]{1,0:T(8,128)(2,1)S(1)} %copy-done.32, ...), custom_call_target="tpu_custom_call" | custom-call | flops 1048576 | bytes 1048576 | tf_op jit(solution)/shard_map/grad_qkv/pallas_call | solution.py:158
  412.1 4.8 all-to-all-start.2
  440.0 5.4 %norm1_sums.1 = (f32[1,2048]{1,0:T(1,128)S(1)}, f32[1,2048]{1,0:T(1,128)S(1)}, f32[1,768]{1,0:T(1,128)S(1)}) custom-call(bf16[128,2048]{1,0:T(8,128)(2,1)S(1)} %get-tuple-element.345.refs_0_.part, bf16[256,2048]{1,0:T(8,128)(2,1)S(1)} %get-tuple-element.322.refs_1_, bf16[256,2048]{1,0:T(8,128)(2,1)S(1)} %get-tuple-element.323.refs_2_, ...), custom_call_target="tpu_custom_call" | custom-call | flops 1048576 | bytes 1048576 | tf_op jit(solution)/shard_map/norm1_sums/pallas_call | solution.py:504
  460.6 6.2 %all-to-all-start.3 = ((bf16[8,72,768]{2,1,0:T(8,128)(2,1)}), bf16[8,72,768]{2,1,0:T(8,128)(2,1)}, u32[]{:S(2)}, u32[]{:S(2)}) async-start(bf16[8,72,768]{2,1,0:T(8,128)(2,1)} %qkv_with_sums.1), calls=%async_computation.6 | async-start | bytes 1769472 | tf_op jit(solution)/shard_map/all_to_all | solution.py:128
  479.1 19.6 %collective-permute-done.70.downward = bf16[128,2048]{1,0:T(8,128)(2,1)} collective-permute-done((bf16[128,2048]{1,0:T(8,128)(2,1)}, bf16[128,2048]{1,0:T(8,128)(2,1)}, u32[]{:S(2)}, u32[]{:S(2)}) %collective-permute-start.70) | collective-permute-done | bytes 524320 | tf_op jit(solution)/shard_map/ppermute | solution.py:61
  (644 shorter events, 316.1 us)
Async XLA Ops:
  7.3 51.1 %all-gather.6.cloned.1.call-start = ((), (), s32[]{:S(2)}) async-start(), calls=%async_computation.8 | async-start | bytes 5242880 | tf_op jit(solution)/shard_map/all_gather | solution.py:568
  15.6 19.3 %collective-permute-start.1 = (bf16[128,2048]{1,0:T(8,128)(2,1)S(1)}, bf16[128,2048]{1,0:T(8,128)(2,1)}, u32[]{:S(2)}, u32[]{:S(2)}) collective-permute-start(bf16[128,2048]{1,0:T(8,128)(2,1)S(1)} %bitcast.134), channel_id=1, source_target_pairs={{8,0},{16,8},{24,16},{28,24},{20,28},{12,20},{4,12},{0,4},{9,1},{1... | collective-permute-start | bytes 1572872 | tf_op jit(solution)/shard_map/ppermute | solution.py:61
  17.7 40.7 %all-to-all-start = ((bf16[8,64,768]{2,1,0:T(8,128)(2,1)}), bf16[8,64,768]{2,1,0:T(8,128)(2,1)}, u32[]{:S(2)}, u32[]{:S(2)}) async-start(bf16[8,64,768]{2,1,0:T(8,128)(2,1)} %reshape.285), calls=%async_computation | async-start | bytes 1572864 | tf_op jit(solution)/shard_map/all_to_all | solution.py:128
  23.9 63.9 %all-gather.8.cloned.1.call-start = ((), (), s32[]{:S(2)}) async-start(), calls=%async_computation.9 | async-start | bytes 3932160 | tf_op jit(solution)/shard_map/all_gather | solution.py:334
  34.9 23.4 %collective-permute-start.3 = (bf16[128,2048]{1,0:T(8,128)(2,1)}, bf16[128,2048]{1,0:T(8,128)(2,1)}, u32[]{:S(2)}, u32[]{:S(2)}) collective-permute-start(bf16[128,2048]{1,0:T(8,128)(2,1)} %collective-permute-done.1), channel_id=1, source_target_pairs={{8,0},{16,8},{24,16},{28,24},{20,28},{12,20},{4,12},{0,4},{9,1},{1... | collective-permute-start | bytes 1572872 | tf_op jit(solution)/shard_map/ppermute | solution.py:61
  35.0 23.4 %collective-permute-start.2 = (bf16[128,2048]{1,0:T(8,128)(2,1)}, bf16[128,2048]{1,0:T(8,128)(2,1)}, u32[]{:S(2)}, u32[]{:S(2)}) collective-permute-start(bf16[128,2048]{1,0:T(8,128)(2,1)} %collective-permute-done), channel_id=1, source_target_pairs={{0,8},{8,16},{16,24},{24,28},{28,20},{20,12},{12,4},{4,0},{1,9},{9... | collective-permute-start | bytes 1572872 | tf_op jit(solution)/shard_map/ppermute | solution.py:61
  64.1 46.9 %all-to-all-start.1 = ((bf16[8,64,1024]{2,1,0:T(8,128)(2,1)}), bf16[8,64,1024]{2,1,0:T(8,128)(2,1)}, u32[]{:S(2)}, u32[]{:S(2)}) async-start(bf16[8,64,1024]{2,1,0:T(8,128)(2,1)} %copy.45), calls=%async_computation.1 | async-start | bytes 2097152 | tf_op jit(solution)/shard_map/all_to_all | solution.py:128
  70.6 40.4 %all-gather.10.cloned.1.call-start = ((), (), s32[]{:S(2)}) async-start(), calls=%async_computation.10 | async-start | bytes 1310720 | tf_op jit(solution)/shard_map/all_gather | solution.py:609
  75.5 74.3 %all-gather.12.cloned.1.call-start = ((), (), s32[]{:S(2)}) async-start(), calls=%async_computation.15 | async-start | bytes 5242880 | tf_op jit(solution)/shard_map/all_gather | solution.py:629
  82.5 20.0 %collective-permute-start.12 = (bf16[64,2048]{1,0:T(8,128)(2,1)}, bf16[64,2048]{1,0:T(8,128)(2,1)S(1)}, u32[]{:S(2)}, u32[]{:S(2)}) collective-permute-start(bf16[64,2048]{1,0:T(8,128)(2,1)} %slice.157), channel_id=1, source_target_pairs={{8,0},{16,8},{24,16},{28,24},{20,28},{12,20},{4,12},{0,4},{9,1},{1... | collective-permute-start | bytes 786440 | tf_op jit(solution)/shard_map/ppermute | solution.py:61
  114.2 244.2 %reduce-scatter.5.cloned.1.call-start = ((), (), s32[]{:S(2)}) async-start(), calls=%async_computation.11 | async-start | bytes 5242880 | tf_op jit(solution)/shard_map/reduce_scatter | solution.py:696
  189.3 48.1 %collective-permute-start.36 = (bf16[64,2048]{1,0:T(8,128)(2,1)S(1)}, bf16[64,2048]{1,0:T(8,128)(2,1)S(1)}, u32[]{:S(2)}, u32[]{:S(2)}) collective-permute-start(bf16[64,2048]{1,0:T(8,128)(2,1)S(1)} %slice.178), channel_id=1, source_target_pairs={{8,0},{16,8},{24,16},{28,24},{20,28},{12,20},{4,12},{0,4},{9,1},{1... | collective-permute-start | bytes 786440 | tf_op jit(solution)/shard_map/ppermute | solution.py:61
  190.5 46.9 %collective-permute-start.35 = (bf16[64,2048]{1,0:T(8,128)(2,1)S(1)}, bf16[64,2048]{1,0:T(8,128)(2,1)S(1)}, u32[]{:S(2)}, u32[]{:S(2)}) collective-permute-start(bf16[64,2048]{1,0:T(8,128)(2,1)S(1)} %slice.177), channel_id=1, source_target_pairs={{0,8},{8,16},{16,24},{24,28},{28,20},{20,12},{12,4},{4,0},{1,9},{9... | collective-permute-start | bytes 786440 | tf_op jit(solution)/shard_map/ppermute | solution.py:61
  273.2 122.5 %reduce-scatter.7.cloned.1.call-start = ((), (), s32[]{:S(2)}) async-start(), calls=%async_computation.12 | async-start | bytes 5242880 | tf_op jit(solution)/shard_map/reduce_scatter | solution.py:710
  278.5 19.4 %collective-permute-start.43 = (bf16[128,2048]{1,0:T(8,128)(2,1)S(1)}, bf16[128,2048]{1,0:T(8,128)(2,1)S(1)}, u32[]{:S(2)}, u32[]{:S(2)}) collective-permute-start(bf16[128,2048]{1,0:T(8,128)(2,1)S(1)} %get-tuple-element.384), channel_id=1, source_target_pairs={{0,8},{8,16},{16,24},{24,28},{28,20},{20,12},{12,4},{4,0},{1,9},{9... | collective-permute-start | bytes 1572872 | tf_op jit(solution)/shard_map/ppermute | solution.py:61
  278.6 21.9 %collective-permute-start.46 = (bf16[128,2048]{1,0:T(8,128)(2,1)S(1)}, bf16[128,2048]{1,0:T(8,128)(2,1)S(1)}, u32[]{:S(2)}, u32[]{:S(2)}) collective-permute-start(bf16[128,2048]{1,0:T(8,128)(2,1)S(1)} %pad_maximum_fusion.8), channel_id=1, source_target_pairs={{8,0},{16,8},{24,16},{28,24},{20,28},{12,20},{4,12},{0,4},{9,1},{1... | collective-permute-start | bytes 1572872 | tf_op jit(solution)/shard_map/ppermute | solution.py:61
  325.0 133.4 %reduce-scatter.9.cloned.1.call-start = ((), (), s32[]{:S(2)}) async-start(), calls=%async_computation.13 | async-start | bytes 3932160 | tf_op jit(solution)/shard_map/reduce_scatter | solution.py:750
  412.1 33.4 %all-to-all-start.2 = ((bf16[8,64,1024]{2,1,0:T(8,128)(2,1)}), bf16[8,64,1024]{2,1,0:T(8,128)(2,1)}, u32[]{:S(2)}, u32[]{:S(2)}) async-start(bf16[8,64,1024]{2,1,0:T(8,128)(2,1)} %reduce-scatter.5.cloned.1.call-done), calls=%async_computation.4 | async-start | bytes 2097152 | tf_op jit(solution)/shard_map/all_to_all | solution.py:128
  417.0 90.1 %reduce-scatter.11.cloned.1.call-start = ((), (), s32[]{:S(2)}) async-start(), calls=%async_computation.14 | async-start | bytes 1310720 | tf_op jit(solution)/shard_map/reduce_scatter | solution.py:777
  421.6 23.9 %collective-permute-start.63 = (bf16[128,2048]{1,0:T(8,128)(2,1)}, bf16[128,2048]{1,0:T(8,128)(2,1)}, u32[]{:S(2)}, u32[]{:S(2)}) collective-permute-start(bf16[128,2048]{1,0:T(8,128)(2,1)} %pad_maximum_fusion.9), channel_id=1, source_target_pairs={{0,8},{8,16},{16,24},{24,28},{28,20},{20,12},{12,4},{4,0},{1,9},{9... | collective-permute-start | bytes 1572872 | tf_op jit(solution)/shard_map/ppermute | solution.py:61
  423.9 21.5 %collective-permute-start.64 = (bf16[128,2048]{1,0:T(8,128)(2,1)}, bf16[128,2048]{1,0:T(8,128)(2,1)}, u32[]{:S(2)}, u32[]{:S(2)}) collective-permute-start(bf16[128,2048]{1,0:T(8,128)(2,1)} %pad_maximum_fusion.10), channel_id=1, source_target_pairs={{8,0},{16,8},{24,16},{28,24},{20,28},{12,20},{4,12},{0,4},{9,1},{1... | collective-permute-start | bytes 1572872 | tf_op jit(solution)/shard_map/ppermute | solution.py:61
  460.6 38.1 %all-to-all-start.3 = ((bf16[8,72,768]{2,1,0:T(8,128)(2,1)}), bf16[8,72,768]{2,1,0:T(8,128)(2,1)}, u32[]{:S(2)}, u32[]{:S(2)}) async-start(bf16[8,72,768]{2,1,0:T(8,128)(2,1)} %qkv_with_sums.1), calls=%async_computation.6 | async-start | bytes 1769472 | tf_op jit(solution)/shard_map/all_to_all | solution.py:128
  469.4 29.3 %collective-permute-start.70 = (bf16[128,2048]{1,0:T(8,128)(2,1)}, bf16[128,2048]{1,0:T(8,128)(2,1)}, u32[]{:S(2)}, u32[]{:S(2)}) collective-permute-start(bf16[128,2048]{1,0:T(8,128)(2,1)} %get-tuple-element.365), channel_id=1, source_target_pairs={{8,0},{16,8},{24,16},{28,24},{20,28},{12,20},{4,12},{0,4},{9,1},{1... | collective-permute-start | bytes 1572872 | tf_op jit(solution)/shard_map/ppermute | solution.py:61
  469.4 29.3 %collective-permute-start.69 = (bf16[128,2048]{1,0:T(8,128)(2,1)}, bf16[128,2048]{1,0:T(8,128)(2,1)}, u32[]{:S(2)}, u32[]{:S(2)}) collective-permute-start(bf16[128,2048]{1,0:T(8,128)(2,1)} %get-tuple-element.366), channel_id=1, source_target_pairs={{0,8},{8,16},{16,24},{24,28},{28,20},{20,12},{12,4},{4,0},{1,9},{9... | collective-permute-start | bytes 1572872 | tf_op jit(solution)/shard_map/ppermute | solution.py:61
  (194 other events, 1854.9 us)
Sparse Core Ops, SparseCore 0:
  10.3 35.6 all-gather.5
  58.6 28.7 all-gather.7
  89.5 16.7 all-gather.9
  114.3 34.7 all-gather.11
  273.3 44.6 reduce-scatter.4
  325.1 45.7 reduce-scatter.6
  412.2 35.8 reduce-scatter.8
  460.7 25.4 reduce-scatter.10
